TPU v7x, 32 devices: a whole 2x2x4 slice. The times are simulated.
32 devices in a mesh: grp: 2 (over x), seq: 16 (over z, y, core).
Axes of the slice: x: 2, y: 2, z: 4, core: 2. Of those that a mesh axis runs over, the one named last changes fastest.
Arguments:
- activations: bfloat16 [16384, 1536], P(('grp', 'seq')), parts along dimension 0, may hold values from -60 to 60, as said below
- dilated_tap_weight: bfloat16 [3, 1536, 768], replicated, may hold values from -0.09375 to 0.09375
- conv_mix: bfloat16 [768, 1536], replicated, may hold values from -0.21875 to 0.21875
- w_query: bfloat16 [1536, 128], replicated, may hold values from -0.15625 to 0.15625
- w_keyval: bfloat16 [1536, 256], replicated, may hold values from -0.15625 to 0.15625
- contact_tiles: bfloat16 [16, 128, 128], replicated, may hold values from -8 to 250, as said below
- tile_codes: int32 [128, 65], P(('grp', 'seq')), parts along dimension 0, may hold values from 0 to 15
- bin_valid: int32 [16384], P('grp'), parts along dimension 0, may hold values 0 or 1
Outputs:
- attended: bfloat16 [16384, 128], P(('grp', 'seq')), parts along dimension 0
There are 2 independent parts, one for each index of `grp`. A program takes and returns all parts, laid end to end along the dimension named above; an argument that names none is the same for every part. Nothing has to cross between parts.
Inputs may be any that keep to these rules, and one draw needn't show every extreme that they name: `activations`: finite values. `contact_tiles`: finite values.
All inputs are finite; a program needn't handle non-finite values.
Results may differ from a plain program's by a relative error of at most 0.005.
Values may be sent and summed in bfloat16 or wider, within the bound.
No kernel may reach another device: no remote copies, remote signals or barrier semaphores. Data moves between devices by JAX's collectives and lax.ppermute only.
A program may use at most 64 MiB of HBM per device.

v0:
```python
import math

import jax
import jax.numpy as jnp
from jax import lax
from jax.sharding import PartitionSpec as P

HDIM = 128
CONV_DILATION = 8
HALF = 4096


masked_score = -1e30
norm_eps = 1e-06


def padded(x, sides, width):
    for axis, dim in sides:
        size, length = (lax.axis_size(axis), x.shape[dim])
        up = [(i, (i + 1) % size) for i in range(size - 1)]
        down = [(j, i) for i, j in up]
        last = lax.slice_in_dim(x, length - width, length, axis=dim)
        initial = lax.slice_in_dim(x, 0, width, axis=dim)
        before = lax.ppermute(last, axis, up)
        after = lax.ppermute(initial, axis, down)
        x = jnp.concatenate([before, x, after], axis=dim)
    return x


def tile_bias(codes_local, contact_tiles, query_first, key_first, key_count):
    tile_size = contact_tiles.shape[1]
    code_count = contact_tiles.shape[0]
    offset_count = codes_local.shape[1]
    query_tiles_n = codes_local.shape[0]
    key_tiles_n = key_count // tile_size
    query_tiles = query_first + jnp.arange(query_tiles_n, dtype=jnp.int32)
    key_tiles = key_first + jnp.arange(key_tiles_n, dtype=jnp.int32)
    offset = jnp.clip(
        key_tiles[None, :] - query_tiles[:, None] + offset_count // 2, 0, offset_count - 1
    )
    slots = jnp.arange(offset_count, dtype=jnp.int32)
    picked = jnp.sum(
        jnp.where(offset[:, :, None] == slots[None, None, :], codes_local[:, None, :], 0), axis=2
    )
    picked_full = jnp.broadcast_to(
        picked[:, None, :, None], (query_tiles_n, tile_size, key_tiles_n, tile_size)
    ).reshape(query_tiles_n * tile_size, key_count)
    bias_block = jnp.zeros((query_tiles_n * tile_size, key_count), jnp.float32)
    for code in range(code_count):
        spread_tile = jnp.broadcast_to(
            contact_tiles[code][None, :, None, :],
            (query_tiles_n, tile_size, key_tiles_n, tile_size),
        ).reshape(query_tiles_n * tile_size, key_count)
        bias_block = jnp.where(picked_full == code, spread_tile.astype(jnp.float32), bias_block)
    return bias_block


def block_scores(
    query_heads, keyval, bin_valid, codes_local, contact_tiles, query_start, key_start, total_bins
):
    key_count = keyval.shape[0]
    query_rows, head_count, head_dim = query_heads.shape
    width_heads = head_count * head_dim
    tile_size = contact_tiles.shape[1]
    key_heads = keyval[:, :width_heads].reshape(key_count, head_count, head_dim)
    value_heads = keyval[:, width_heads:].reshape(key_count, head_count, head_dim)
    raw_scores = jnp.einsum(
        "qhd,khd->qhk", query_heads, key_heads, preferred_element_type=jnp.float32
    ) * (1.0 / math.sqrt(head_dim))
    bias_block = tile_bias(
        codes_local,
        contact_tiles,
        query_start // tile_size,
        jnp.floor_divide(key_start, tile_size),
        key_count,
    )
    key_pos = key_start + jnp.arange(key_count, dtype=jnp.int32)
    query_pos = query_start + jnp.arange(query_rows, dtype=jnp.int32)
    inside = (key_pos >= 0) & (key_pos < total_bins)
    valid_keys = lax.dynamic_slice_in_dim(
        bin_valid, jnp.clip(key_start, 0, total_bins - key_count), key_count
    )
    in_band = jnp.abs(key_pos[None, :] - query_pos[:, None]) <= HALF
    kept_pairs = (
        inside[None, :]
        & in_band
        & ((valid_keys[None, :] == 1) | (key_pos[None, :] == query_pos[:, None]))
    )
    scores = jnp.where(kept_pairs[:, None, :], raw_scores + bias_block[:, None, :], masked_score)
    return (scores, value_heads)


def absorb(softmax_state, pairs):
    row_peak, row_total, weighted = softmax_state
    new_peak = row_peak
    for scores, value_heads in pairs:
        new_peak = jnp.maximum(new_peak, jnp.max(scores, axis=-1))
    rescale = jnp.exp(row_peak - new_peak)
    row_total = row_total * rescale
    weighted = weighted * rescale[..., None]
    for scores, value_heads in pairs:
        probs = jnp.exp(scores - new_peak[..., None])
        row_total = row_total + jnp.sum(probs, axis=-1)
        weighted = weighted + jnp.einsum(
            "qhk,khd->qhd",
            probs.astype(jnp.bfloat16),
            value_heads,
            preferred_element_type=jnp.float32,
        )
    return (new_peak, row_total, weighted)


def per_device(
    activations,
    dilated_tap_weight,
    conv_mix,
    w_query,
    w_keyval,
    contact_tiles,
    tile_codes,
    bin_valid,
):
    genomic_bin_rows = activations.shape[0]
    seq_size = lax.axis_size("seq")
    position = lax.axis_index("seq")
    total_bins = seq_size * genomic_bin_rows
    query_start = position * genomic_bin_rows
    border_padded = padded(activations, (("seq", 0),), CONV_DILATION)
    raised_features = jax.nn.gelu(border_padded.astype(jnp.float32), approximate=False).astype(
        jnp.bfloat16
    )
    tap_low = jnp.dot(raised_features, dilated_tap_weight[0], preferred_element_type=jnp.float32)
    tap_mid = jnp.dot(raised_features, dilated_tap_weight[1], preferred_element_type=jnp.float32)
    tap_high = jnp.dot(raised_features, dilated_tap_weight[2], preferred_element_type=jnp.float32)
    conv_sum = (
        tap_low[0:genomic_bin_rows] + tap_mid[CONV_DILATION : CONV_DILATION + genomic_bin_rows]
    )
    conv_sum = conv_sum + tap_high[2 * CONV_DILATION : 2 * CONV_DILATION + genomic_bin_rows]
    squeezed = jax.nn.gelu(conv_sum, approximate=False).astype(jnp.bfloat16)
    mixed_rows = activations.astype(jnp.float32) + jnp.dot(
        squeezed, conv_mix, preferred_element_type=jnp.float32
    )
    normed = (
        mixed_rows * lax.rsqrt(jnp.mean(mixed_rows * mixed_rows, axis=-1, keepdims=True) + norm_eps)
    ).astype(jnp.bfloat16)
    queries = jnp.dot(normed, w_query, preferred_element_type=jnp.float32).astype(jnp.bfloat16)
    keyval = jnp.dot(normed, w_keyval, preferred_element_type=jnp.float32).astype(jnp.bfloat16)
    width_heads = queries.shape[1]
    head_count = w_keyval.shape[1] // (2 * HDIM)
    query_heads = queries.reshape(genomic_bin_rows, head_count, HDIM)
    reach = HALF // genomic_bin_rows

    def absorb_pair(softmax_state, from_below, from_above, distance):
        low_pair = block_scores(
            query_heads,
            from_below,
            bin_valid,
            tile_codes,
            contact_tiles,
            query_start,
            query_start - distance * genomic_bin_rows,
            total_bins,
        )
        high_pair = block_scores(
            query_heads,
            from_above,
            bin_valid,
            tile_codes,
            contact_tiles,
            query_start,
            query_start + distance * genomic_bin_rows,
            total_bins,
        )
        return absorb(softmax_state, (low_pair, high_pair))

    initial = (
        jnp.full((genomic_bin_rows, head_count), masked_score, jnp.float32),
        jnp.zeros((genomic_bin_rows, head_count), jnp.float32),
        jnp.zeros((genomic_bin_rows, head_count, HDIM), jnp.float32),
    )
    own_pair = block_scores(
        query_heads,
        keyval,
        bin_valid,
        tile_codes,
        contact_tiles,
        query_start,
        query_start,
        total_bins,
    )
    softmax_state = absorb(initial, (own_pair,))
    everything = lax.all_gather(keyval, "seq", axis=0, tiled=True)

    def collect_turn(distance, state_now):
        low_start = jnp.clip(
            query_start - distance * genomic_bin_rows, 0, total_bins - genomic_bin_rows
        )
        high_start = jnp.clip(
            query_start + distance * genomic_bin_rows, 0, total_bins - genomic_bin_rows
        )
        from_below = lax.dynamic_slice_in_dim(everything, low_start, genomic_bin_rows, 0)
        from_above = lax.dynamic_slice_in_dim(everything, high_start, genomic_bin_rows, 0)
        return absorb_pair(state_now, from_below, from_above, distance)

    softmax_state = lax.fori_loop(1, reach + 1, collect_turn, softmax_state)
    row_peak, row_total, weighted = softmax_state
    attended = (weighted / row_total[..., None]).reshape(genomic_bin_rows, width_heads)
    return attended.astype(jnp.bfloat16)


def solution(mesh):
    in_specs = (P(("grp", "seq"), None), P(), P(), P(), P(), P(), P(("grp", "seq"), None), P("grp"))
    out_specs = P(("grp", "seq"), None)
    return jax.shard_map(
        per_device, mesh=mesh, in_specs=in_specs, out_specs=out_specs, check_vma=False
    )
```

profile of v0, /device:TPU:13, one launch (start us, length us, event | category | flops | bytes accessed | tf_op | source)
XLA Modules:
  0.0 542.6 jit_solution(11341009575677297269)
XLA Ops:
  7.4 3.7 collective-permute-start
  11.2 1.9 collective-permute-start.1
  13.1 4.1 collective-permute-done.1
  17.2 8.1 %fusion.31 = bf16[528,1536]{1,0:T(8,128)(2,1)S(1)} fusion(bf16[8,1536]{1,0:T(8,128)(2,1)S(1)} %collective-permute-done.1, bf16[512,1536]{1,0:T(8,128)(2,1)} %param.10, bf16[8,1536]{1,0:T(8,128)(2,1)S(1)} %collective-permute-done), kind=kLoop, calls=%fused_computation.109 | loop fusion | flops 57581568 | bytes 3244032 | tf_op jit(solution)/shard_map/convert_element_type | solution.py:129
  25.4 4.8 fusion.61
  30.1 4.3 fusion.63
  34.4 11.6 %multiply_reduce_fusion = (f32[512]{0:T(512)S(1)}, f32[512,1536]{1,0:T(8,128)}) fusion(bf16[768,1536]{1,0:T(8,128)(2,1)S(1)} %copy-done, f32[512,768]{1,0:T(8,128)} %fusion.61, f32[512,768]{1,0:T(8,128)} %fusion.63, bf16[3,1536,768]{2,1,0:T(8,128)(2,1)} %param.11, bf16[528,1536]{1,0:T(8,128)(2,1)} %copy-done.18, bf16[512,1536]{1,0:T(8,128)(2,1)} %param.10), kind=kOutput, calls=%fused_computation.141 | convolution fusion | flops 2445409792 | bytes 14157824 | tf_op jit(solution)/shard_map/dot_general | solution.py:140
  46.0 3.5 convolution_convert_fusion
  76.7 4.5 select_select_fusion.2
  87.6 3.2 convolution_convert_fusion.1
  93.7 5.4 %all-gather.2.cloned.1.call-done = bf16[8192,256]{1,0:T(8,128)(2,1)} async-done(((bf16[512,256]{1,0:T(8,128)(2,1)}), bf16[8192,256]{1,0:T(8,128)(2,1)}) %all-gather.2.cloned.1.call-update) | async-done | bytes 4194320 | tf_op jit(solution)/shard_map/all_gather | solution.py:192
  99.2 434.8 %while.20 = (s32[]{:T(128)}, f32[512,1]{0,1:T(1,128)S(1)}, f32[512,1]{0,1:T(1,128)S(1)}, f32[512,1,128]{0,2,1:T(8,128)}, s32[]{:T(128)}, /*index=5*/s32[8192]{0:...) while((s32[]{:T(128)}, f32[512,1]{0,1:T(1,128)S(1)}, ...), condition=%wide.region_11.12_spmd, body=%wide.region_4.11_spmd.sunk | while | flops 285161664 | bytes 33061628 | solution.py:205
  109.7 1.7 bitcast_convert_fusion.33
  112.4 3.9 select_select_fusion.5
  123.7 4.1 fusion.191
  137.6 4.3 select_select_fusion.6
  145.7 2.5 fusion.192
  164.1 1.7 bitcast_convert_fusion.33
  166.7 3.9 select_select_fusion.5
  178.1 4.1 fusion.191
  192.0 4.3 select_select_fusion.6
  200.0 2.5 fusion.192
  221.1 3.9 select_select_fusion.5
  232.4 4.1 fusion.191
  246.3 4.3 select_select_fusion.6
  254.4 2.5 fusion.192
  275.4 3.9 select_select_fusion.5
  286.7 4.1 fusion.191
  300.7 4.3 select_select_fusion.6
  308.7 2.5 fusion.192
  327.1 1.7 bitcast_convert_fusion.33
  329.8 3.9 select_select_fusion.5
  341.1 4.1 fusion.191
  355.0 4.3 select_select_fusion.6
  363.0 2.5 fusion.192
  384.1 3.9 select_select_fusion.5
  395.4 4.1 fusion.191
  409.4 4.3 select_select_fusion.6
  417.4 2.5 fusion.192
  438.5 3.9 select_select_fusion.5
  449.8 4.1 fusion.191
  463.7 4.3 select_select_fusion.6
  471.7 2.5 fusion.192
  490.2 1.7 bitcast_convert_fusion.33
  492.8 3.9 select_select_fusion.5
  504.1 4.1 fusion.191
  518.0 4.3 select_select_fusion.6
  526.0 2.5 fusion.192
  (829 shorter events, 346.2 us)
Async XLA Ops:
  6.5 27.9 %copy-start = (bf16[768,1536]{1,0:T(8,128)(2,1)S(1)}, bf16[768,1536]{1,0:T(8,128)(2,1)}, u32[]{:S(2)}) copy-start(bf16[768,1536]{1,0:T(8,128)(2,1)} %param.12) | copy-start | bytes 7077892
  6.5 92.6 %all-gather.2.cloned.1.call-start = ((), (), s32[]{:S(2)}) async-start(), calls=%async_computation | async-start | bytes 4456448 | tf_op jit(solution)/shard_map/all_gather | solution.py:192
  7.4 5.6 %collective-permute-start = (bf16[8,1536]{1,0:T(8,128)(2,1)S(1)}, bf16[8,1536]{1,0:T(8,128)(2,1)S(1)}, u32[]{:S(2)}, u32[]{:S(2)}) collective-permute-start(bf16[8,1536]{1,0:T(8,128)(2,1)S(1)} %get-tuple-element.461), channel_id=1, source_target_pairs={{0,1},{1,2},{2,3},{3,4},{4,5},{5,6},{6,7},{7,8},{8,9},{9,10},{10,1... | collective-permute-start | bytes 73736 | tf_op jit(solution)/shard_map/ppermute | solution.py:24
  11.2 6.0 %collective-permute-start.1 = (bf16[8,1536]{1,0:T(8,128)(2,1)S(1)}, bf16[8,1536]{1,0:T(8,128)(2,1)S(1)}, u32[]{:S(2)}, u32[]{:S(2)}) collective-permute-start(bf16[8,1536]{1,0:T(8,128)(2,1)S(1)} %get-tuple-element.462), channel_id=1, source_target_pairs={{1,0},{2,1},{3,2},{4,3},{5,4},{6,5},{7,6},{8,7},{9,8},{10,9},{11,1... | collective-permute-start | bytes 73736 | tf_op jit(solution)/shard_map/ppermute | solution.py:25
  25.3 4.8 copy-start.18
  46.0 3.6 copy-start.22
  46.0 12.7 %copy-start.16 = (bf16[16,128,128]{2,1,0:T(8,128)(2,1)S(1)}, bf16[16,128,128]{2,1,0:T(8,128)(2,1)}, u32[]{:S(2)}) copy-start(bf16[16,128,128]{2,1,0:T(8,128)(2,1)} %param.15) | copy-start | bytes 1572868
  86.6 4.2 copy-start.17
  86.6 4.2 copy-start.21
  86.6 4.2 copy-start.19
  86.6 4.2 copy-start.20
  123.7 4.7 copy-start.23
  142.0 3.7 copy-start.24
  142.0 3.7 copy-start.26
  143.4 4.8 copy-start.25
  148.2 3.3 copy-start.14
  178.1 4.7 copy-start.23
  196.3 3.7 copy-start.24
  196.3 3.7 copy-start.26
  197.8 4.8 copy-start.25
  202.6 3.3 copy-start.14
  232.4 4.7 copy-start.23
  250.7 3.7 copy-start.24
  250.7 3.7 copy-start.26
  252.1 4.8 copy-start.25
  256.9 3.3 copy-start.14
  286.7 4.7 copy-start.23
  305.0 3.7 copy-start.24
  305.0 3.7 copy-start.26
  306.4 4.8 copy-start.25
  311.3 3.3 copy-start.14
  341.1 4.7 copy-start.23
  359.4 3.7 copy-start.24
  359.4 3.7 copy-start.26
  360.8 4.8 copy-start.25
  395.4 4.7 copy-start.23
  413.7 3.7 copy-start.24
  413.7 3.7 copy-start.26
  415.1 4.8 copy-start.25
  419.9 3.3 copy-start.14
  449.8 4.7 copy-start.23
  468.0 3.7 copy-start.24
  468.0 3.7 copy-start.26
  469.4 4.8 copy-start.25
  504.1 4.7 copy-start.23
  522.4 3.7 copy-start.24
  522.4 3.7 copy-start.26
  523.8 4.8 copy-start.25
  (115 other events, 90.4 us)
Sparse Core Ops, SparseCore 0:
  49.6 49.5 all-gather.1
where the time goes:
time: 549 us; the launch traced here: 543 us
  local copies, waits for them, and re-layouts  273 us (50%)
  other arithmetic  131 us (24%)
  matrix products  107 us (19%)
  between operations  13.6 us (2%)
  waiting for transfers between devices  9.56 us (2%)
  starting transfers between devices  5.62 us (1%)
    eq x289, local copies, waits for them, and re-layouts, tile_bias(): picked_full == code  194 us
    select_n x17, other arithmetic, tile_bias(): jnp.where(picked_full == code, spread_tile.astype(jnp.float32), bias_block)  70.4 us
    dot_general x17, matrix products, block_scores(): jnp.einsum('qhd,khd->qhk', query_heads, key_heads, preferred_element_type...  54.6 us
    convert_element_type x25, local copies, waits for them, and re-layouts, tile_bias(): spread_tile.astype(jnp.float32)  29 us
    dot_general x17, matrix products, absorb(): jnp.einsum('qhk,khd->qhd', probs.astype(jnp.bfloat16), value_heads, prefe...  25.4 us
    select_n x17, local copies, waits for them, and re-layouts, tile_bias(): jnp.where(picked_full == code, spread_tile.astype(jnp.float32), bias_block)  24 us
    convert_element_type x9, other arithmetic, tile_bias(): spread_tile.astype(jnp.float32)  14.6 us
    reduce_sum x9, other arithmetic, absorb(): row_total = row_total + jnp.sum(probs, axis=-1)  12.4 us
  transfers between devices with their start and end apart: 3, of which 2 were waited for; matrix products, arithmetic and copies ran while one was open for 8% of the time, Pallas kernels for 0%

commit v1 on v0

v1 whole, which is shorter than its diff:
```python
import functools
import math

import jax
import jax.numpy as jnp
from jax import lax
from jax.experimental import pallas as pl
from jax.experimental.pallas import tpu as pltpu
from jax.sharding import PartitionSpec as P

HDIM = 128
CONV_DILATION = 8
HALF = 4096


masked_score = -1e30
norm_eps = 1e-06


def padded(x, sides, width):
    for axis, dim in sides:
        size, length = (lax.axis_size(axis), x.shape[dim])
        up = [(i, (i + 1) % size) for i in range(size - 1)]
        down = [(j, i) for i, j in up]
        last = lax.slice_in_dim(x, length - width, length, axis=dim)
        initial = lax.slice_in_dim(x, 0, width, axis=dim)
        before = lax.ppermute(last, axis, up)
        after = lax.ppermute(initial, axis, down)
        x = jnp.concatenate([before, x, after], axis=dim)
    return x


LOG2E = 1.4426950408889634


def attend_kernel(
    reach,
    codes_ref,
    place_ref,
    q_ref,
    kv_ref,
    tiles_ref,
    valid_ref,
    out_ref,
    kv_buf,
    bias_buf,
    scores,
    peak,
    total,
    acc,
    sems,
):
    rows, head_dim = q_ref.shape
    code_count, tile, _ = tiles_ref.shape
    tiles_per_block = rows // tile
    position = place_ref[0]
    first = place_ref[1]
    count = place_ref[2]
    factor = LOG2E / math.sqrt(head_dim)

    def fetch(i):
        return pltpu.make_async_copy(
            kv_ref.at[pl.ds((first + i) * rows, rows), :], kv_buf.at[i], sems.at[i]
        )

    @pl.loop(0, count)
    def _(i):
        fetch(i).start()

    bias_buf[...] = tiles_ref[...].astype(jnp.float32) * LOG2E
    peak[...] = jnp.full_like(peak, masked_score)

    @pl.loop(0, count)
    def _(i):
        fetch(i).wait()
        block = first + i
        keys = kv_buf[i, :, :head_dim]
        raw = lax.dot_general(
            q_ref[...], keys, (((1,), (1,)), ((), ())), preferred_element_type=jnp.float32
        )
        invalid = jnp.where(valid_ref[block] == 1, 0.0, masked_score)
        shift = block - position

        def tile_scores(qt, kt):
            offset = jnp.clip(shift * tiles_per_block + kt - qt + HALF // tile, 0, 2 * (HALF // tile))
            part = raw[qt * tile : (qt + 1) * tile, kt * tile : (kt + 1) * tile]
            return part * factor + bias_buf[codes_ref[qt, offset]]

        def keep(qt, columns):
            peak_now = peak[qt * tile : (qt + 1) * tile, :]
            for kt, column in enumerate(columns):
                scores[i, qt * tile : (qt + 1) * tile, kt * tile : (kt + 1) * tile] = column
                peak_now = jnp.maximum(peak_now, column)
            peak[qt * tile : (qt + 1) * tile, :] = peak_now

        plain = (shift != 0) & (jnp.abs(shift) < reach)

        @pl.when(plain)
        def _():
            for qt in range(tiles_per_block):
                keep(
                    qt,
                    [
                        tile_scores(qt, kt) + invalid[:, kt * tile : (kt + 1) * tile]
                        for kt in range(tiles_per_block)
                    ],
                )

        @pl.when(jnp.logical_not(plain))
        def _():
            lag = lax.broadcasted_iota(jnp.int32, (tile, tile), 1) - lax.broadcasted_iota(
                jnp.int32, (tile, tile), 0
            )
            for qt in range(tiles_per_block):
                columns = []
                for kt in range(tiles_per_block):
                    apart = lag + (shift * rows + (kt - qt) * tile)
                    dropped = jnp.where(
                        apart == 0, 0.0, invalid[:, kt * tile : (kt + 1) * tile]
                    )
                    dropped = jnp.where(jnp.abs(apart) <= HALF, dropped, masked_score)
                    columns.append(tile_scores(qt, kt) + dropped)
                keep(qt, columns)

    peak[...] = jnp.broadcast_to(jnp.max(peak[...], axis=1, keepdims=True), peak.shape)
    total[...] = jnp.zeros_like(total)
    acc[...] = jnp.zeros_like(acc)

    @pl.loop(0, count)
    def _(i):
        parts = []
        sums = total[...]
        for kt in range(tiles_per_block):
            probs = jnp.exp2(scores[i, :, kt * tile : (kt + 1) * tile] - peak[...])
            sums = sums + probs
            parts.append(probs.astype(jnp.bfloat16))
        total[...] = sums
        acc[...] += jnp.dot(
            jnp.concatenate(parts, axis=1),
            kv_buf[i, :, head_dim:],
            preferred_element_type=jnp.float32,
        )

    out_ref[...] = (acc[...] / jnp.sum(total[...], axis=1, keepdims=True)).astype(out_ref.dtype)


def attend(queries, everything, contact_tiles, tile_codes, bin_valid, position, seq_size):
    rows, head_dim = queries.shape
    reach = HALF // rows
    tile = contact_tiles.shape[1]
    slots = min(seq_size, 2 * reach + 1)
    first = jnp.maximum(position - reach, 0)
    last = jnp.minimum(position + reach, seq_size - 1)
    place = jnp.stack([position, first, last - first + 1]).astype(jnp.int32)
    valid_rows = bin_valid.reshape(seq_size, 1, rows)
    vmem = pl.BlockSpec(memory_space=pltpu.VMEM)
    smem = pl.BlockSpec(memory_space=pltpu.SMEM)
    return pl.pallas_call(
        functools.partial(attend_kernel, reach),
        out_shape=jax.ShapeDtypeStruct((rows, head_dim), jnp.bfloat16),
        in_specs=[smem, smem, vmem, pl.BlockSpec(memory_space=pl.ANY), vmem, vmem],
        out_specs=vmem,
        scratch_shapes=[
            pltpu.VMEM((slots, rows, 2 * head_dim), jnp.bfloat16),
            pltpu.VMEM(contact_tiles.shape, jnp.float32),
            pltpu.VMEM((slots, rows, rows), jnp.float32),
            pltpu.VMEM((rows, tile), jnp.float32),
            pltpu.VMEM((rows, tile), jnp.float32),
            pltpu.VMEM((rows, head_dim), jnp.float32),
            pltpu.SemaphoreType.DMA((slots,)),
        ],
        compiler_params=pltpu.CompilerParams(vmem_limit_bytes=60 << 20),
        name="attend",
    )(tile_codes, place, queries, everything, contact_tiles, valid_rows)


def per_device(
    activations,
    dilated_tap_weight,
    conv_mix,
    w_query,
    w_keyval,
    contact_tiles,
    tile_codes,
    bin_valid,
):
    genomic_bin_rows = activations.shape[0]
    seq_size = lax.axis_size("seq")
    position = lax.axis_index("seq")
    border_padded = padded(activations, (("seq", 0),), CONV_DILATION)
    raised_features = jax.nn.gelu(border_padded.astype(jnp.float32), approximate=False).astype(
        jnp.bfloat16
    )
    tap_low = jnp.dot(raised_features, dilated_tap_weight[0], preferred_element_type=jnp.float32)
    tap_mid = jnp.dot(raised_features, dilated_tap_weight[1], preferred_element_type=jnp.float32)
    tap_high = jnp.dot(raised_features, dilated_tap_weight[2], preferred_element_type=jnp.float32)
    conv_sum = (
        tap_low[0:genomic_bin_rows] + tap_mid[CONV_DILATION : CONV_DILATION + genomic_bin_rows]
    )
    conv_sum = conv_sum + tap_high[2 * CONV_DILATION : 2 * CONV_DILATION + genomic_bin_rows]
    squeezed = jax.nn.gelu(conv_sum, approximate=False).astype(jnp.bfloat16)
    mixed_rows = activations.astype(jnp.float32) + jnp.dot(
        squeezed, conv_mix, preferred_element_type=jnp.float32
    )
    normed = (
        mixed_rows * lax.rsqrt(jnp.mean(mixed_rows * mixed_rows, axis=-1, keepdims=True) + norm_eps)
    ).astype(jnp.bfloat16)
    queries = jnp.dot(normed, w_query, preferred_element_type=jnp.float32).astype(jnp.bfloat16)
    keyval = jnp.dot(normed, w_keyval, preferred_element_type=jnp.float32).astype(jnp.bfloat16)
    everything = lax.all_gather(keyval, "seq", axis=0, tiled=True)
    return attend(queries, everything, contact_tiles, tile_codes, bin_valid, position, seq_size)


def solution(mesh):
    in_specs = (P(("grp", "seq"), None), P(), P(), P(), P(), P(), P(("grp", "seq"), None), P("grp"))
    out_specs = P(("grp", "seq"), None)
    return jax.shard_map(
        per_device, mesh=mesh, in_specs=in_specs, out_specs=out_specs, check_vma=False
    )
```

time: 549 us -> 122 us (0.22); the launches traced: 543 us -> 122 us
  local copies, waits for them, and re-layouts: 273 us -> 0.92 us
  other arithmetic: 131 us -> 8.76 us
  matrix products: 107 us -> 27 us
  waiting for transfers between devices: 9.56 us -> 50 us
  Pallas kernels: 0 us -> 16.3 us
    eq x289 -> x0, local copies, waits for them, and re-layouts: 194 us -> none  [tile_bias(): picked_full == code]
    dot_general x34 -> x0, matrix products: 80 us -> none  [the longest x17 54.6 us: block_scores(): jnp.einsum('qhd,khd->qhk', query_heads, key_heads, preferred_element_type...]
    select_n x17 -> x0, other arithmetic: 70.4 us -> none  [tile_bias(): jnp.where(picked_full == code, spread_tile.astype(jnp.float32), bias_block)]
    all_gather x1, waiting for transfers between devices: 5.43 us -> 45.9 us  [per_device(): everything = lax.all_gather(keyval, 'seq', axis=0, tiled=True)]
    convert_element_type x25 -> x0, local copies, waits for them, and re-layouts: 29 us -> none  [tile_bias(): spread_tile.astype(jnp.float32)]
    select_n x17 -> x0, local copies, waits for them, and re-layouts: 24 us -> none  [tile_bias(): jnp.where(picked_full == code, spread_tile.astype(jnp.float32), bias_block)]
    eq x26 -> x0, other arithmetic: 21.6 us -> none  [the longest x9 11.8 us: block_scores(): valid_keys[None, :] == 1]
    pallas_call x0 -> x1, Pallas kernels: none -> 16.3 us  [attend(): pl.pallas_call(functools.partial(attend_kernel, reach), out_shape=jax.Sha...]
  transfers between devices with their start and end apart: 3 -> 3, of which waited for: 2 -> 2; matrix products, arithmetic and copies ran while one was open for 8% -> 3% of each run, Pallas kernels for 0% -> 0%
where the time goes in v1:
time: 122 us
  waiting for transfers between devices  50 us (41%)
  matrix products  27 us (22%)
  Pallas kernels  16.3 us (13%)
  between operations  13.5 us (11%)
  other arithmetic  8.76 us (7%)
  starting transfers between devices  5.62 us (5%)
    all_gather x1, waiting for transfers between devices, per_device(): everything = lax.all_gather(keyval, 'seq', axis=0, tiled=True)  45.9 us
    pallas_call x1, Pallas kernels, attend(): pl.pallas_call(functools.partial(attend_kernel, reach), out_shape=jax.Sha...  16.3 us
    dot_general x1, matrix products, per_device(): jnp.dot(squeezed, conv_mix, preferred_element_type=jnp.float32)  11.6 us
    convert_element_type x1, other arithmetic, per_device(): jax.nn.gelu(border_padded.astype(jnp.float32), approximate=False)  8.14 us
    dot_general x1, matrix products, per_device(): jnp.dot(raised_features, dilated_tap_weight[2], preferred_element_type=jn...  4.81 us
    dot_general x1, matrix products, per_device(): jnp.dot(raised_features, dilated_tap_weight[1], preferred_element_type=jn...  4.21 us
    ppermute x1, waiting for transfers between devices, padded(): after = lax.ppermute(initial, axis, down)  4.11 us
    ppermute x1, starting transfers between devices, padded(): before = lax.ppermute(last, axis, up)  3.7 us
  transfers between devices with their start and end apart: 3, of which 2 were waited for; matrix products, arithmetic and copies ran while one was open for 3% of the time, Pallas kernels for 0%

profile of v1, /device:TPU:13, one launch (start us, length us, event | category | flops | bytes accessed | tf_op | source)
XLA Modules:
  0.0 122.1 jit_solution(10562224065845240316)
XLA Ops:
  6.5 0.0 copy-start
  6.5 0.0 all-gather.2.cloned.1.call-start
  6.5 0.9 fusion.122
  7.4 3.7 %collective-permute-start = (bf16[8,1536]{1,0:T(8,128)(2,1)S(1)}, bf16[8,1536]{1,0:T(8,128)(2,1)S(1)}, u32[]{:S(2)}, u32[]{:S(2)}) collective-permute-start(bf16[8,1536]{1,0:T(8,128)(2,1)S(1)} %get-tuple-element.5), channel_id=1, source_target_pairs={{0,1},{1,2},{2,3},{3,4},{4,5},{5,6},{6,7},{7,8},{8,9},{9,10},{10,1... | collective-permute-start | bytes 73736 | tf_op jit(solution)/shard_map/ppermute | solution.py:27
  11.2 1.9 %collective-permute-start.1 = (bf16[8,1536]{1,0:T(8,128)(2,1)S(1)}, bf16[8,1536]{1,0:T(8,128)(2,1)S(1)}, u32[]{:S(2)}, u32[]{:S(2)}) collective-permute-start(bf16[8,1536]{1,0:T(8,128)(2,1)S(1)} %get-tuple-element.6), channel_id=1, source_target_pairs={{1,0},{2,1},{3,2},{4,3},{5,4},{6,5},{7,6},{8,7},{9,8},{10,9},{11,1... | collective-permute-start | bytes 73736 | tf_op jit(solution)/shard_map/ppermute | solution.py:28
  13.1 0.0 collective-permute-done
  13.1 4.1 %collective-permute-done.1 = bf16[8,1536]{1,0:T(8,128)(2,1)S(1)} collective-permute-done((bf16[8,1536]{1,0:T(8,128)(2,1)S(1)}, bf16[8,1536]{1,0:T(8,128)(2,1)S(1)}, u32[]{:S(2)}, u32[]{:S(2)}) %collective-permute-start.1) | collective-permute-done | bytes 24608 | tf_op jit(solution)/shard_map/ppermute | solution.py:28
  17.2 8.1 %fusion.1 = bf16[528,1536]{1,0:T(8,128)(2,1)S(1)} fusion(bf16[8,1536]{1,0:T(8,128)(2,1)S(1)} %collective-permute-done.1, bf16[512,1536]{1,0:T(8,128)(2,1)} %param.8, bf16[8,1536]{1,0:T(8,128)(2,1)S(1)} %collective-permute-done), kind=kLoop, calls=%fused_computation.4 | loop fusion | flops 57581568 | bytes 3244032 | tf_op jit(solution)/shard_map/convert_element_type | solution.py:191
  25.3 0.0 copy-start.1
  25.4 4.8 %fusion.31 = f32[512,768]{1,0:T(8,128)} fusion(bf16[3,1536,768]{2,1,0:T(8,128)(2,1)} %param.9, bf16[528,1536]{1,0:T(8,128)(2,1)S(1)} %fusion.1), kind=kOutput, calls=%fused_computation.38 | convolution fusion | flops 1207959552 | bytes 5505024 | tf_op jit(solution)/shard_map/dot_general | solution.py:196
  30.2 0.0 copy-done.1
  30.2 4.2 %fusion.33 = f32[512,768]{1,0:T(8,128)} fusion(bf16[3,1536,768]{2,1,0:T(8,128)(2,1)} %param.9, bf16[528,1536]{1,0:T(8,128)(2,1)S(1)} %fusion.1), kind=kOutput, calls=%fused_computation.40 | convolution fusion | flops 1207959552 | bytes 5505024 | tf_op jit(solution)/shard_map/dot_general | solution.py:195
  34.4 0.0 copy-done
  34.4 0.0 copy-start.2
  34.4 11.6 %multiply_reduce_fusion = (f32[512]{0:T(512)S(1)}, f32[512,1536]{1,0:T(8,128)}) fusion(bf16[768,1536]{1,0:T(8,128)(2,1)S(1)} %copy-done, f32[512,768]{1,0:T(8,128)} %fusion.31, f32[512,768]{1,0:T(8,128)} %fusion.33, bf16[3,1536,768]{2,1,0:T(8,128)(2,1)} %param.9, bf16[528,1536]{1,0:T(8,128)(2,1)} %copy-done.1, bf16[512,1536]{1,0:T(8,128)(2,1)} %param.8), kind=kOutput, calls=%fused_computation.36 | convolution fusion | flops 2445409792 | bytes 14157824 | tf_op jit(solution)/shard_map/dot_general | solution.py:202
  46.0 0.0 copy-start.3
  46.0 0.0 copy-done.2
  46.0 3.2 %convolution_convert_fusion = bf16[512,256]{1,0:T(8,128)(2,1)} fusion(bf16[1536,256]{1,0:T(8,128)(2,1)S(1)} %copy-done.2, f32[512,1536]{1,0:T(8,128)} %get-tuple-element.8, f32[512]{0:T(512)S(1)} %add_rsqrt_fusion), kind=kOutput, calls=%fused_computation.69 | convolution fusion | flops 404357120 | bytes 4196352 | tf_op jit(solution)/shard_map/dot_general | solution.py:209
  49.2 0.0 all-gather.2.cloned.1.call-update
  49.3 0.6 pad_add_fusion.place_ref
  49.9 0.0 copy-done.3
  49.9 3.1 %convolution_convert_fusion.1.q_ref = bf16[512,128]{1,0:T(8,128)(2,1)} fusion(bf16[1536,128]{1,0:T(8,128)(2,1)S(1)} %copy-done.3, f32[512,1536]{1,0:T(8,128)} %get-tuple-element.8, f32[512]{0:T(512)S(1)} %add_rsqrt_fusion), kind=kOutput, calls=%fused_computation.70 | convolution fusion | flops 202964992 | bytes 3672064 | tf_op jit(solution)/shard_map/dot_general | solution.py:208
  53.0 45.9 %all-gather.2.cloned.1.call-done.kv_ref = bf16[8192,256]{1,0:T(8,128)(2,1)} async-done(((bf16[512,256]{1,0:T(8,128)(2,1)}), bf16[8192,256]{1,0:T(8,128)(2,1)}) %all-gather.2.cloned.1.call-update) | async-done | bytes 4194320 | tf_op jit(solution)/shard_map/all_gather | solution.py:210
  98.9 16.3 %attend.1 = bf16[512,128]{1,0:T(8,128)(2,1)} custom-call(s32[4,65]{1,0:T(4,128)} %codes_ref.1, s32[3]{0:T(128)} %pad_add_fusion.place_ref, bf16[512,128]{1,0:T(8,128)(2,1)} %convolution_convert_fusion.1.q_ref, bf16[8192,256]{1,0:T(8,128)(2,1)} %all-gather.2.cloned.1.call-done.kv_ref, bf16[16,128,128]{2,1,0:T(8,128)(2,1)} %tiles_ref.1, s32[16,1,512]{2,1,0:T(1,128)} %bitcast.22), custom_call_target="tpu_custom_call" | custom-call | tf_op jit(solution)/shard_map/attend/pallas_call | solution.py:158
  (1 shorter events, 0.0 us)
Async XLA Ops:
  6.5 27.8 %copy-start = (bf16[768,1536]{1,0:T(8,128)(2,1)S(1)}, bf16[768,1536]{1,0:T(8,128)(2,1)}, u32[]{:S(2)}) copy-start(bf16[768,1536]{1,0:T(8,128)(2,1)} %param.10) | copy-start | bytes 7077892
  6.5 92.4 %all-gather.2.cloned.1.call-start = ((), (), s32[]{:S(2)}) async-start(), calls=%async_computation | async-start | bytes 4456448 | tf_op jit(solution)/shard_map/all_gather | solution.py:210
  7.4 5.6 %collective-permute-start = (bf16[8,1536]{1,0:T(8,128)(2,1)S(1)}, bf16[8,1536]{1,0:T(8,128)(2,1)S(1)}, u32[]{:S(2)}, u32[]{:S(2)}) collective-permute-start(bf16[8,1536]{1,0:T(8,128)(2,1)S(1)} %get-tuple-element.5), channel_id=1, source_target_pairs={{0,1},{1,2},{2,3},{3,4},{4,5},{5,6},{6,7},{7,8},{8,9},{9,10},{10,1... | collective-permute-start | bytes 73736 | tf_op jit(solution)/shard_map/ppermute | solution.py:27
  11.2 6.0 %collective-permute-start.1 = (bf16[8,1536]{1,0:T(8,128)(2,1)S(1)}, bf16[8,1536]{1,0:T(8,128)(2,1)S(1)}, u32[]{:S(2)}, u32[]{:S(2)}) collective-permute-start(bf16[8,1536]{1,0:T(8,128)(2,1)S(1)} %get-tuple-element.6), channel_id=1, source_target_pairs={{1,0},{2,1},{3,2},{4,3},{5,4},{6,5},{7,6},{8,7},{9,8},{10,9},{11,1... | collective-permute-start | bytes 73736 | tf_op jit(solution)/shard_map/ppermute | solution.py:28
  25.3 4.8 %copy-start.1 = (bf16[528,1536]{1,0:T(8,128)(2,1)}, bf16[528,1536]{1,0:T(8,128)(2,1)S(1)}, u32[]{:S(2)}) copy-start(bf16[528,1536]{1,0:T(8,128)(2,1)S(1)} %fusion.1) | copy-start | bytes 4866052
  34.4 11.6 %copy-start.2 = (bf16[1536,256]{1,0:T(8,128)(2,1)S(1)}, bf16[1536,256]{1,0:T(8,128)(2,1)}, u32[]{:S(2)}) copy-start(bf16[1536,256]{1,0:T(8,128)(2,1)} %param.12) | copy-start | bytes 2359300
  46.0 3.9 %copy-start.3 = (bf16[1536,128]{1,0:T(8,128)(2,1)S(1)}, bf16[1536,128]{1,0:T(8,128)(2,1)}, u32[]{:S(2)}) copy-start(bf16[1536,128]{1,0:T(8,128)(2,1)} %param.11) | copy-start | bytes 1179652
Sparse Core Ops, SparseCore 0:
  49.4 49.4 all-gather.1

commit v2 on v1

--- a/solution.py
+++ b/solution.py
@@ -17,17 +17,132 @@
 norm_eps = 1e-06
 
 
-def padded(x, sides, width):
-    for axis, dim in sides:
-        size, length = (lax.axis_size(axis), x.shape[dim])
-        up = [(i, (i + 1) % size) for i in range(size - 1)]
-        down = [(j, i) for i, j in up]
-        last = lax.slice_in_dim(x, length - width, length, axis=dim)
-        initial = lax.slice_in_dim(x, 0, width, axis=dim)
-        before = lax.ppermute(last, axis, up)
-        after = lax.ppermute(initial, axis, down)
-        x = jnp.concatenate([before, x, after], axis=dim)
-    return x
+def halo_rows(activations):
+    size = lax.axis_size("seq")
+    odd = lax.axis_index("seq") % 2 == 1
+    rows = activations.shape[0]
+    initial = lax.slice_in_dim(activations, 0, CONV_DILATION, axis=0)
+    last = lax.slice_in_dim(activations, rows - CONV_DILATION, rows, axis=0)
+    inner = [(i, i ^ 1) for i in range(size)]
+    outer = [(i, i + 1) for i in range(1, size - 1, 2)] + [(i + 1, i) for i in range(1, size - 1, 2)]
+    from_outer = lax.ppermute(jnp.where(odd, last, initial), "seq", outer)
+    from_inner = lax.ppermute(jnp.where(odd, initial, last), "seq", inner)
+    before = jnp.where(odd, from_inner, from_outer)
+    after = jnp.where(odd, from_outer, from_inner)
+    return jnp.concatenate([before, after], axis=0)
+
+
+def gelu(v):
+    return 0.5 * v * (1.0 + lax.erf(v * math.sqrt(0.5)))
+
+
+def front_kernel(
+    x_hbm,
+    halo_ref,
+    taps_hbm,
+    mix_hbm,
+    wq_hbm,
+    wkv_hbm,
+    q_ref,
+    kv_ref,
+    x_ref,
+    taps,
+    mix,
+    wq,
+    wkv,
+    outer,
+    inner,
+    squeezed,
+    mixed,
+    sems,
+):
+    rows, channels = x_ref.shape
+    hidden = squeezed.shape[1]
+    copies = [
+        pltpu.make_async_copy(x_hbm, x_ref, sems.at[0]),
+        pltpu.make_async_copy(taps_hbm, taps, sems.at[1]),
+        pltpu.make_async_copy(mix_hbm, mix, sems.at[2]),
+        pltpu.make_async_copy(wq_hbm, wq, sems.at[3]),
+        pltpu.make_async_copy(wkv_hbm, wkv, sems.at[4]),
+    ]
+    for copy in copies:
+        copy.start()
+    edge = gelu(halo_ref[...].astype(jnp.float32))
+    step = 32
+    d = CONV_DILATION
+    copies[0].wait()
+
+    def lift(i, tail):
+        r = pl.multiple_of(i * step, step)
+        g = gelu(x_ref[pl.ds(r, step), :].astype(jnp.float32))
+        inner[pl.ds(r, step), :] = g.astype(jnp.bfloat16)
+        outer[pl.ds(r, step), :] = jnp.concatenate([tail, g[: step - d]], axis=0).astype(
+            jnp.bfloat16
+        )
+        return g[step - d :]
+
+    tail = lax.fori_loop(0, rows // step, lift, edge[:d])
+    outer[rows : rows + 2 * d, :] = jnp.concatenate([tail, edge[d:]], axis=0).astype(jnp.bfloat16)
+
+    copies[1].wait()
+    wide = 256
+    for n in range(hidden // wide):
+        cols = slice(n * wide, (n + 1) * wide)
+        conv = jnp.dot(outer[0:rows, :], taps[0, :, cols], preferred_element_type=jnp.float32)
+        conv += jnp.dot(inner[...], taps[1, :, cols], preferred_element_type=jnp.float32)
+        conv += jnp.dot(
+            outer[2 * d : rows + 2 * d, :], taps[2, :, cols], preferred_element_type=jnp.float32
+        )
+        squeezed[:, cols] = gelu(conv).astype(jnp.bfloat16)
+
+    copies[2].wait()
+    square = jnp.zeros((rows, 128), jnp.float32)
+    for n in range(channels // wide):
+        cols = slice(n * wide, (n + 1) * wide)
+        part = x_ref[:, cols].astype(jnp.float32) + jnp.dot(
+            squeezed[...], mix[:, cols], preferred_element_type=jnp.float32
+        )
+        mixed[:, cols] = part
+        for k in range(wide // 128):
+            piece = part[:, k * 128 : (k + 1) * 128]
+            square += piece * piece
+    gain = lax.rsqrt(jnp.sum(square, axis=1, keepdims=True) / channels + norm_eps)
+    copies[3].wait()
+    copies[4].wait()
+    normed = (mixed[...] * gain).astype(jnp.bfloat16)
+    q_ref[...] = jnp.dot(normed, wq[...], preferred_element_type=jnp.float32).astype(jnp.bfloat16)
+    kv_ref[...] = jnp.dot(normed, wkv[...], preferred_element_type=jnp.float32).astype(jnp.bfloat16)
+
+
+def front(activations, halo, dilated_tap_weight, conv_mix, w_query, w_keyval):
+    rows, channels = activations.shape
+    hidden = conv_mix.shape[0]
+    anywhere = pl.BlockSpec(memory_space=pl.ANY)
+    vmem = pl.BlockSpec(memory_space=pltpu.VMEM)
+    bf16 = jnp.bfloat16
+    return pl.pallas_call(
+        front_kernel,
+        out_shape=[
+            jax.ShapeDtypeStruct((rows, w_query.shape[1]), bf16),
+            jax.ShapeDtypeStruct((rows, w_keyval.shape[1]), bf16),
+        ],
+        in_specs=[anywhere, vmem, anywhere, anywhere, anywhere, anywhere],
+        out_specs=[vmem, vmem],
+        scratch_shapes=[
+            pltpu.VMEM(activations.shape, bf16),
+            pltpu.VMEM(dilated_tap_weight.shape, bf16),
+            pltpu.VMEM(conv_mix.shape, bf16),
+            pltpu.VMEM(w_query.shape, bf16),
+            pltpu.VMEM(w_keyval.shape, bf16),
+            pltpu.VMEM((rows + 2 * CONV_DILATION, channels), bf16),
+            pltpu.VMEM((rows, channels), bf16),
+            pltpu.VMEM((rows, hidden), bf16),
+            pltpu.VMEM((rows, channels), jnp.float32),
+            pltpu.SemaphoreType.DMA((5,)),
+        ],
+        compiler_params=pltpu.CompilerParams(vmem_limit_bytes=60 << 20),
+        name="front",
+    )(activations, halo, dilated_tap_weight, conv_mix, w_query, w_keyval)
 
 
 LOG2E = 1.4426950408889634
@@ -184,29 +299,11 @@
     tile_codes,
     bin_valid,
 ):
-    genomic_bin_rows = activations.shape[0]
     seq_size = lax.axis_size("seq")
     position = lax.axis_index("seq")
-    border_padded = padded(activations, (("seq", 0),), CONV_DILATION)
-    raised_features = jax.nn.gelu(border_padded.astype(jnp.float32), approximate=False).astype(
-        jnp.bfloat16
+    queries, keyval = front(
+        activations, halo_rows(activations), dilated_tap_weight, conv_mix, w_query, w_keyval
     )
-    tap_low = jnp.dot(raised_features, dilated_tap_weight[0], preferred_element_type=jnp.float32)
-    tap_mid = jnp.dot(raised_features, dilated_tap_weight[1], preferred_element_type=jnp.float32)
-    tap_high = jnp.dot(raised_features, dilated_tap_weight[2], preferred_element_type=jnp.float32)
-    conv_sum = (
-        tap_low[0:genomic_bin_rows] + tap_mid[CONV_DILATION : CONV_DILATION + genomic_bin_rows]
-    )
-    conv_sum = conv_sum + tap_high[2 * CONV_DILATION : 2 * CONV_DILATION + genomic_bin_rows]
-    squeezed = jax.nn.gelu(conv_sum, approximate=False).astype(jnp.bfloat16)
-    mixed_rows = activations.astype(jnp.float32) + jnp.dot(
-        squeezed, conv_mix, preferred_element_type=jnp.float32
-    )
-    normed = (
-        mixed_rows * lax.rsqrt(jnp.mean(mixed_rows * mixed_rows, axis=-1, keepdims=True) + norm_eps)
-    ).astype(jnp.bfloat16)
-    queries = jnp.dot(normed, w_query, preferred_element_type=jnp.float32).astype(jnp.bfloat16)
-    keyval = jnp.dot(normed, w_keyval, preferred_element_type=jnp.float32).astype(jnp.bfloat16)
     everything = lax.all_gather(keyval, "seq", axis=0, tiled=True)
     return attend(queries, everything, contact_tiles, tile_codes, bin_valid, position, seq_size)
 

time: 122 us -> 102 us (0.84)
  matrix products: 27 us -> 0 us
  Pallas kernels: 16.3 us -> 30.1 us
  other arithmetic: 8.76 us -> 2.05 us
  waiting for transfers between devices: 50 us -> 52 us
  starting transfers between devices: 5.62 us -> 3.72 us
    dot_general x5 -> x0, matrix products: 27 us -> none  [the longest x1 11.6 us: per_device(): jnp.dot(squeezed, conv_mix, preferred_element_type=jnp.float32)]
    pallas_call x0 -> x1, Pallas kernels: none -> 13.8 us  [front(): pl.pallas_call(front_kernel, out_shape=[jax.ShapeDtypeStruct((rows, w_que...]
    convert_element_type x1 -> x0, other arithmetic: 8.14 us -> none  [per_device(): jax.nn.gelu(border_padded.astype(jnp.float32), approximate=False)]
    all_gather x1, waiting for transfers between devices: 45.9 us -> 49 us  [per_device(): everything = lax.all_gather(keyval, 'seq', axis=0, tiled=True)]
    ppermute x2, starting transfers between devices: 5.62 us -> 3.72 us  [the longest x1 3.04 us: halo_rows(): from_outer = lax.ppermute(jnp.where(odd, last, initial), 'seq', outer)]
  transfers between devices with their start and end apart: 3 -> 3, of which waited for: 2 -> 2; matrix products, arithmetic and copies ran while one was open for 3% -> 1% of each run, Pallas kernels for 0% -> 0%
where the time goes in v2:
time: 102 us; the launch traced here: 101 us
  waiting for transfers between devices  52 us (51%)
  Pallas kernels  30.1 us (30%)
  between operations  13.4 us (13%)
  starting transfers between devices  3.72 us (4%)
  other arithmetic  2.05 us (2%)
    all_gather x1, waiting for transfers between devices, per_device(): everything = lax.all_gather(keyval, 'seq', axis=0, tiled=True)  49 us
    pallas_call x1, Pallas kernels, attend(): pl.pallas_call(functools.partial(attend_kernel, reach), out_shape=jax.Sha...  16.3 us
    pallas_call x1, Pallas kernels, front(): pl.pallas_call(front_kernel, out_shape=[jax.ShapeDtypeStruct((rows, w_que...  13.8 us
    ppermute x1, starting transfers between devices, halo_rows(): from_outer = lax.ppermute(jnp.where(odd, last, initial), 'seq', outer)  3.04 us
    ppermute x1, waiting for transfers between devices, halo_rows(): from_outer = lax.ppermute(jnp.where(odd, last, initial), 'seq', outer)  2.97 us
  transfers between devices with their start and end apart: 3, of which 2 were waited for; matrix products, arithmetic and copies ran while one was open for 1% of the time, Pallas kernels for 0%

profile of v2, /device:TPU:13, one launch (start us, length us, event | category | flops | bytes accessed | tf_op | source)
XLA Modules:
  0.0 101.3 jit_solution(5616557820865036010)
XLA Ops:
  6.5 0.0 all-gather.2.cloned.1.call-start
  6.5 0.8 broadcast_select_fusion.3
  7.3 0.7 collective-permute-start
  8.0 3.0 %collective-permute-start.1 = (bf16[8,1536]{1,0:T(8,128)(2,1)S(1)}, bf16[8,1536]{1,0:T(8,128)(2,1)S(1)}, u32[]{:S(2)}, u32[]{:S(2)}) collective-permute-start(bf16[8,1536]{1,0:T(8,128)(2,1)S(1)} %get-tuple-element.10), channel_id=1, source_target_pairs={{1,2},{3,4},{5,6},{7,8},{9,10},{11,12},{13,14},{2,1},{4,3},{6,5},{... | collective-permute-start | bytes 73736 | tf_op jit(solution)/shard_map/ppermute | solution.py:28
  11.0 0.0 collective-permute-done
  11.0 3.0 %collective-permute-done.1 = bf16[8,1536]{1,0:T(8,128)(2,1)S(1)} collective-permute-done((bf16[8,1536]{1,0:T(8,128)(2,1)S(1)}, bf16[8,1536]{1,0:T(8,128)(2,1)S(1)}, u32[]{:S(2)}, u32[]{:S(2)}) %collective-permute-start.1) | collective-permute-done | bytes 24608 | tf_op jit(solution)/shard_map/ppermute | solution.py:28
  14.0 0.6 pad_maximum_fusion.halo_ref
  14.6 13.8 %front.1 = (bf16[512,128]{1,0:T(8,128)(2,1)}, bf16[512,256]{1,0:T(8,128)(2,1)}) custom-call(bf16[512,1536]{1,0:T(8,128)(2,1)} %x_hbm.1, bf16[16,1536]{1,0:T(8,128)(2,1)} %pad_maximum_fusion.halo_ref, bf16[3,1536,768]{2,1,0:T(8,128)(2,1)} %taps_hbm.1, bf16[768,1536]{1,0:T(8,128)(2,1)} %mix_hbm.1, bf16[1536,128]{1,0:T(8,128)(2,1)} %wq_hbm.1, ...), custom_call_target="tpu_custom_call" | custom-call | tf_op jit(solution)/shard_map/front/pallas_call | solution.py:123
  28.4 0.0 all-gather.2.cloned.1.call-update
  28.5 0.7 pad_add_fusion.place_ref
  29.1 49.0 %all-gather.2.cloned.1.call-done.kv_ref = bf16[8192,256]{1,0:T(8,128)(2,1)} async-done(((bf16[512,256]{1,0:T(8,128)(2,1)}), bf16[8192,256]{1,0:T(8,128)(2,1)}) %all-gather.2.cloned.1.call-update) | async-done | bytes 4194320 | tf_op jit(solution)/shard_map/all_gather | solution.py:307
  78.1 16.3 %attend.1 = bf16[512,128]{1,0:T(8,128)(2,1)} custom-call(s32[4,65]{1,0:T(4,128)} %codes_ref.1, s32[3]{0:T(128)} %pad_add_fusion.place_ref, bf16[512,128]{1,0:T(8,128)(2,1)} %get-tuple-element.7.q_ref, bf16[8192,256]{1,0:T(8,128)(2,1)} %all-gather.2.cloned.1.call-done.kv_ref, bf16[16,128,128]{2,1,0:T(8,128)(2,1)} %tiles_ref.1, s32[16,1,512]{2,1,0:T(1,128)} %bitcast.4), custom_call_target="tpu_custom_call" | custom-call | tf_op jit(solution)/shard_map/attend/pallas_call | solution.py:273
  (1 shorter events, 0.0 us)
Async XLA Ops:
  6.5 71.6 %all-gather.2.cloned.1.call-start = ((), (), s32[]{:S(2)}) async-start(), calls=%async_computation | async-start | bytes 4456448 | tf_op jit(solution)/shard_map/all_gather | solution.py:307
  7.3 3.7 %collective-permute-start = (bf16[8,1536]{1,0:T(8,128)(2,1)S(1)}, bf16[8,1536]{1,0:T(8,128)(2,1)S(1)}, u32[]{:S(2)}, u32[]{:S(2)}) collective-permute-start(bf16[8,1536]{1,0:T(8,128)(2,1)S(1)} %get-tuple-element.9), channel_id=1, source_target_pairs={{0,1},{1,0},{2,3},{3,2},{4,5},{5,4},{6,7},{7,6},{8,9},{9,8},{10,11... | collective-permute-start | bytes 73736 | tf_op jit(solution)/shard_map/ppermute | solution.py:29
  8.0 6.0 %collective-permute-start.1 = (bf16[8,1536]{1,0:T(8,128)(2,1)S(1)}, bf16[8,1536]{1,0:T(8,128)(2,1)S(1)}, u32[]{:S(2)}, u32[]{:S(2)}) collective-permute-start(bf16[8,1536]{1,0:T(8,128)(2,1)S(1)} %get-tuple-element.10), channel_id=1, source_target_pairs={{1,2},{3,4},{5,6},{7,8},{9,10},{11,12},{13,14},{2,1},{4,3},{6,5},{... | collective-permute-start | bytes 73736 | tf_op jit(solution)/shard_map/ppermute | solution.py:28
Sparse Core Ops, SparseCore 0:
  28.6 49.4 all-gather.1

commit v3 on v2

--- a/solution.py
+++ b/solution.py
@@ -39,6 +39,7 @@
 def front_kernel(
     x_hbm,
     halo_ref,
+    codes_ref,
     taps_hbm,
     mix_hbm,
     wq_hbm,
@@ -110,23 +111,33 @@
     copies[3].wait()
     copies[4].wait()
     normed = (mixed[...] * gain).astype(jnp.bfloat16)
-    q_ref[...] = jnp.dot(normed, wq[...], preferred_element_type=jnp.float32).astype(jnp.bfloat16)
+    q_ref[0:rows, :] = jnp.dot(normed, wq[...], preferred_element_type=jnp.float32).astype(
+        jnp.bfloat16
+    )
+    q_ref[rows:, :] = codes_ref[...].astype(jnp.float32).astype(jnp.bfloat16)
     kv_ref[...] = jnp.dot(normed, wkv[...], preferred_element_type=jnp.float32).astype(jnp.bfloat16)
 
 
-def front(activations, halo, dilated_tap_weight, conv_mix, w_query, w_keyval):
+CODE_ROWS = 16
+
+
+def front(activations, halo, tile_codes, dilated_tap_weight, conv_mix, w_query, w_keyval):
     rows, channels = activations.shape
     hidden = conv_mix.shape[0]
+    codes = jnp.pad(
+        tile_codes,
+        ((0, CODE_ROWS - tile_codes.shape[0]), (0, w_query.shape[1] - tile_codes.shape[1])),
+    )
     anywhere = pl.BlockSpec(memory_space=pl.ANY)
     vmem = pl.BlockSpec(memory_space=pltpu.VMEM)
     bf16 = jnp.bfloat16
     return pl.pallas_call(
         front_kernel,
         out_shape=[
-            jax.ShapeDtypeStruct((rows, w_query.shape[1]), bf16),
+            jax.ShapeDtypeStruct((rows + CODE_ROWS, w_query.shape[1]), bf16),
             jax.ShapeDtypeStruct((rows, w_keyval.shape[1]), bf16),
         ],
-        in_specs=[anywhere, vmem, anywhere, anywhere, anywhere, anywhere],
+        in_specs=[anywhere, vmem, vmem, anywhere, anywhere, anywhere, anywhere],
         out_specs=[vmem, vmem],
         scratch_shapes=[
             pltpu.VMEM(activations.shape, bf16),
@@ -142,7 +153,7 @@
         ],
         compiler_params=pltpu.CompilerParams(vmem_limit_bytes=60 << 20),
         name="front",
-    )(activations, halo, dilated_tap_weight, conv_mix, w_query, w_keyval)
+    )(activations, halo, codes, dilated_tap_weight, conv_mix, w_query, w_keyval)
 
 
 LOG2E = 1.4426950408889634
@@ -257,6 +268,294 @@
         )
 
     out_ref[...] = (acc[...] / jnp.sum(total[...], axis=1, keepdims=True)).astype(out_ref.dtype)
+
+
+def score_block(
+    reach, shift, raw, invalid, table, code_at, tile, tiles_per_block, keep
+):
+    factor = LOG2E / math.sqrt(HDIM)
+    rows = tile * tiles_per_block
+
+    def tile_scores(qt, kt):
+        offset = jnp.clip(shift * tiles_per_block + kt - qt + HALF // tile, 0, 2 * (HALF // tile))
+        part = raw[qt * tile : (qt + 1) * tile, kt * tile : (kt + 1) * tile]
+        return part * factor + table[code_at(qt, offset)]
+
+    plain = (shift != 0) & (jnp.abs(shift) < reach)
+
+    @pl.when(plain)
+    def _():
+        for qt in range(tiles_per_block):
+            keep(
+                qt,
+                [
+                    tile_scores(qt, kt) + invalid[:, kt * tile : (kt + 1) * tile]
+                    for kt in range(tiles_per_block)
+                ],
+            )
+
+    @pl.when(jnp.logical_not(plain))
+    def _():
+        lag = lax.broadcasted_iota(jnp.int32, (tile, tile), 1) - lax.broadcasted_iota(
+            jnp.int32, (tile, tile), 0
+        )
+        for qt in range(tiles_per_block):
+            columns = []
+            for kt in range(tiles_per_block):
+                apart = lag + (shift * rows + (kt - qt) * tile)
+                dropped = jnp.where(apart == 0, 0.0, invalid[:, kt * tile : (kt + 1) * tile])
+                dropped = jnp.where(jnp.abs(apart) <= HALF, dropped, masked_score)
+                columns.append(tile_scores(qt, kt) + dropped)
+            keep(qt, columns)
+
+
+def absorb_kernel(reach, flips, blocks, begin, pack, codes_ref, *refs):
+    sets, n = len(flips), len(blocks)
+    q_refs, refs = refs[:sets], refs[sets:]
+    kv_refs, refs = refs[:n], refs[n:]
+    tiles_ref, valid_ref = refs[:2]
+    refs = refs[2:]
+    if not begin:
+        state_refs, refs = refs[: 3 * sets], refs[3 * sets :]
+    outs = 1 if pack else 3 * sets
+    out_refs, refs = refs[:outs], refs[outs:]
+    kv_buf, table, scores, peak, total, acc, sems = refs
+    rows, head_dim = acc.shape
+    tile = tiles_ref.shape[1]
+    tiles_per_block = rows // tile
+    position = lax.axis_index("seq")
+    copies = [
+        pltpu.make_async_copy(kv_refs[j], kv_buf.at[j], sems.at[j]) for j in range(n)
+    ]
+    for copy in copies:
+        copy.start()
+    table[...] = tiles_ref[...].astype(jnp.float32) * LOG2E
+    for copy in copies:
+        copy.wait()
+
+    def pick(values, j):
+        chosen = jnp.int32(values[0])
+        for k in range(1, n):
+            chosen = jnp.where(j == k, values[k], chosen)
+        return chosen
+
+    for s, flip in enumerate(flips):
+        owner = position ^ flip
+        q_ref = q_refs[s]
+        half = 0 if flip == 0 else tiles_per_block
+        if begin:
+            peak[...] = jnp.full_like(peak, masked_score)
+        else:
+            peak[...] = state_refs[3 * s][...]
+
+        def shift_of(j):
+            return (position ^ pick(blocks, j)) - owner
+
+        @pl.loop(0, n)
+        def _(j):
+            shift = shift_of(j)
+
+            @pl.when(jnp.abs(shift) <= reach)
+            def _():
+                raw = lax.dot_general(
+                    q_ref[0:rows, :],
+                    kv_buf[j, :, :head_dim],
+                    (((1,), (1,)), ((), ())),
+                    preferred_element_type=jnp.float32,
+                )
+                invalid = jnp.where(valid_ref[owner + shift] == 1, 0.0, masked_score)
+
+                def keep(qt, columns):
+                    span = slice(qt * tile, (qt + 1) * tile)
+                    peak_now = peak[span, :]
+                    for kt, column in enumerate(columns):
+                        scores[j, span, kt * tile : (kt + 1) * tile] = column
+                        peak_now = jnp.maximum(peak_now, column)
+                    peak[span, :] = peak_now
+
+                score_block(
+                    reach,
+                    shift,
+                    raw,
+                    invalid,
+                    table,
+                    lambda qt, offset: codes_ref[half + qt, offset],
+                    tile,
+                    tiles_per_block,
+                    keep,
+                )
+
+        peak[...] = jnp.broadcast_to(jnp.max(peak[...], axis=1, keepdims=True), peak.shape)
+        if begin:
+            total[...] = jnp.zeros_like(total)
+            acc[...] = jnp.zeros_like(acc)
+        else:
+            rescale = jnp.exp2(state_refs[3 * s][...] - peak[...])
+            total[...] = state_refs[3 * s + 1][...] * rescale
+            acc[...] = state_refs[3 * s + 2][...] * rescale
+
+        @pl.loop(0, n)
+        def _(j):
+            @pl.when(jnp.abs(shift_of(j)) <= reach)
+            def _():
+                parts = []
+                sums = total[...]
+                for kt in range(tiles_per_block):
+                    probs = jnp.exp2(scores[j, :, kt * tile : (kt + 1) * tile] - peak[...])
+                    sums = sums + probs
+                    parts.append(probs.astype(jnp.bfloat16))
+                total[...] = sums
+                acc[...] += jnp.dot(
+                    jnp.concatenate(parts, axis=1),
+                    kv_buf[j, :, head_dim:],
+                    preferred_element_type=jnp.float32,
+                )
+
+        if pack:
+            out_refs[0][0:rows, :] = acc[...]
+            sums = jnp.broadcast_to(jnp.sum(total[...], axis=1, keepdims=True), total.shape)
+            eye = on_diagonal(tile)
+            lines = []
+            for column in (peak[...], sums):
+                for qt in range(tiles_per_block):
+                    part = column[qt * tile : (qt + 1) * tile, :]
+                    lines.append(jnp.sum(jnp.where(eye, part, 0.0), axis=0, keepdims=True))
+            out_refs[0][rows:, :] = jnp.concatenate(lines, axis=0)
+        else:
+            out_refs[3 * s][...] = peak[...]
+            out_refs[3 * s + 1][...] = total[...]
+            out_refs[3 * s + 2][...] = acc[...]
+
+
+def on_diagonal(tile):
+    return lax.broadcasted_iota(jnp.int32, (tile, tile), 0) == lax.broadcasted_iota(
+        jnp.int32, (tile, tile), 1
+    )
+
+
+def absorb(name, reach, codes, queries, keyvals, contact_tiles, valid_rows, flips, blocks, state, pack):
+    rows = keyvals[0].shape[0]
+    head_dim = queries[0].shape[1]
+    tile = contact_tiles.shape[1]
+    n = len(blocks)
+    vmem = pl.BlockSpec(memory_space=pltpu.VMEM)
+    smem = pl.BlockSpec(memory_space=pltpu.SMEM)
+    anywhere = pl.BlockSpec(memory_space=pl.ANY)
+    column = jax.ShapeDtypeStruct((rows, tile), jnp.float32)
+    if pack:
+        out_shape = [jax.ShapeDtypeStruct((rows + 2 * (rows // tile), head_dim), jnp.float32)]
+    else:
+        out_shape = [column, column, column] * len(flips)
+    units = len(flips) * n
+    return pl.pallas_call(
+        functools.partial(absorb_kernel, reach, flips, blocks, not state, pack),
+        out_shape=out_shape,
+        in_specs=[smem]
+        + [vmem] * len(flips)
+        + [anywhere] * n
+        + [vmem, vmem]
+        + [vmem] * len(state),
+        out_specs=[vmem] * len(out_shape),
+        scratch_shapes=[
+            pltpu.VMEM((n, rows, 2 * head_dim), jnp.bfloat16),
+            pltpu.VMEM(contact_tiles.shape, jnp.float32),
+            pltpu.VMEM((n, rows, rows), jnp.float32),
+            pltpu.VMEM((rows, tile), jnp.float32),
+            pltpu.VMEM((rows, tile), jnp.float32),
+            pltpu.VMEM((rows, head_dim), jnp.float32),
+            pltpu.SemaphoreType.DMA((n,)),
+        ],
+        compiler_params=pltpu.CompilerParams(vmem_limit_bytes=40 << 20),
+        cost_estimate=pl.CostEstimate(
+            flops=units * 4 * rows * rows * head_dim,
+            bytes_accessed=units * 4 * rows * rows,
+            transcendentals=units * rows * rows,
+        ),
+        name=name,
+    )(codes, *queries, *keyvals, contact_tiles, valid_rows, *state)
+
+
+def merge_kernel(peak_ref, total_ref, acc_ref, pack_ref, out_ref):
+    rows, head_dim = acc_ref.shape
+    tile = peak_ref.shape[1]
+    eye = on_diagonal(tile)
+    count = rows // tile
+    for qt in range(count):
+        span = slice(qt * tile, (qt + 1) * tile)
+
+        def column(line):
+            row = pack_ref[rows + line : rows + line + 1, :]
+            return jnp.sum(jnp.where(eye, row, 0.0), axis=1, keepdims=True)
+
+        peak_a = peak_ref[span, :]
+        peak_b = column(qt)
+        total_a = jnp.sum(total_ref[span, :], axis=1, keepdims=True)
+        total_b = column(count + qt)
+        top = jnp.maximum(peak_a, peak_b)
+        scale_a = jnp.exp2(peak_a - top)
+        scale_b = jnp.exp2(peak_b - top)
+        whole = total_a * scale_a + total_b * scale_b
+        out_ref[span, :] = (
+            (acc_ref[span, :] * scale_a + pack_ref[span, :] * scale_b) / whole
+        ).astype(out_ref.dtype)
+
+
+def attend_split(queries, keyval, contact_tiles, tile_codes, bin_valid, seq_size):
+    rows = keyval.shape[0]
+    reach = HALF // rows
+    z = seq_size // 4
+    half = z // 2
+    valid_rows = bin_valid.reshape(seq_size, 1, rows)
+
+    def trade(x, flip, some=None):
+        pairs = [(i, i ^ flip) for i in range(seq_size) if some is None or some(i // z)]
+        return lax.ppermute(x, "seq", pairs)
+
+    twin = trade(keyval, 1)
+    peer_queries = trade(queries, half)
+    near = trade(keyval, z)
+    middle = trade(keyval, 3 * z, lambda level: level in (1, 2))
+    far = trade(keyval, 2 * z)
+    peer_codes = peer_queries[rows : rows + tile_codes.shape[0], : tile_codes.shape[1]]
+    codes = jnp.concatenate([tile_codes, peer_codes.astype(jnp.int32)], axis=0)
+    common = (contact_tiles, valid_rows)
+    both = [queries, peer_queries]
+    state = absorb(
+        "own", reach, codes, both, [keyval, twin], *common, (0, half), (0, 1), [], False
+    )
+    near, middle, state = lax.optimization_barrier((near, middle, state))
+    near_twin, middle_twin = trade(near, 1), trade(middle, 1)
+    state = absorb(
+        "near",
+        reach,
+        codes,
+        both,
+        [near, near_twin, middle, middle_twin],
+        *common,
+        (0, half),
+        (z, z + 1, 3 * z, 3 * z + 1),
+        state,
+        False,
+    )
+    far, state = lax.optimization_barrier((far, state))
+    last = [far, trade(far, 1)]
+    steps = (2 * z, 2 * z + 1)
+    (pack,) = absorb(
+        "far_peer", reach, codes, [peer_queries], last, *common, (half,), steps, state[3:], True
+    )
+    other = trade(pack, half)
+    peak, total, acc = absorb(
+        "far_own", reach, codes, [queries], last, *common, (0,), steps, state[:3], False
+    )
+    vmem = pl.BlockSpec(memory_space=pltpu.VMEM)
+    return pl.pallas_call(
+        merge_kernel,
+        out_shape=jax.ShapeDtypeStruct((rows, queries.shape[1]), jnp.bfloat16),
+        in_specs=[vmem] * 4,
+        out_specs=vmem,
+        compiler_params=pltpu.CompilerParams(vmem_limit_bytes=8 << 20),
+        name="merge",
+    )(peak, total, acc, other)
 
 
 def attend(queries, everything, contact_tiles, tile_codes, bin_valid, position, seq_size):
@@ -302,8 +601,17 @@
     seq_size = lax.axis_size("seq")
     position = lax.axis_index("seq")
     queries, keyval = front(
-        activations, halo_rows(activations), dilated_tap_weight, conv_mix, w_query, w_keyval
-    )
+        activations,
+        halo_rows(activations),
+        tile_codes,
+        dilated_tap_weight,
+        conv_mix,
+        w_query,
+        w_keyval,
+    )
+    if seq_size == 16 and seq_size * activations.shape[0] == 2 * HALF:
+        return attend_split(queries, keyval, contact_tiles, tile_codes, bin_valid, seq_size)
+    queries = queries[: activations.shape[0]]
     everything = lax.all_gather(keyval, "seq", axis=0, tiled=True)
     return attend(queries, everything, contact_tiles, tile_codes, bin_valid, position, seq_size)
 

time: 102 us -> 65.8 us (0.65)
  the two profiles are of different devices: /device:TPU:13 before, /device:TPU:0 now
where the time goes in v3:
time: 65.8 us; the launch traced here: 65.5 us
  Pallas kernels  29.4 us (45%)
  waiting for transfers between devices  16.9 us (26%)
  starting transfers between devices  15.5 us (24%)
  local copies, waits for them, and re-layouts  2.2 us (3%)
  other arithmetic  1.41 us (2%)
    ppermute x9, waiting for transfers between devices, trade(): return lax.ppermute(x, 'seq', pairs)  16.9 us
    pallas_call x4, Pallas kernels, absorb(): pl.pallas_call(functools.partial(absorb_kernel, reach, flips, blocks, not...  14.6 us
    ppermute x9, starting transfers between devices, trade(): return lax.ppermute(x, 'seq', pairs)  14.4 us
    pallas_call x1, Pallas kernels, front(): pl.pallas_call(front_kernel, out_shape=[jax.ShapeDtypeStruct((rows + CODE...  13.8 us
  transfers between devices with their start and end apart: 11, of which 4 were waited for; matrix products, arithmetic and copies ran while one was open for 2% of the time, Pallas kernels for 18%

profile of v3, /device:TPU:0, one launch (start us, length us, event | category | flops | bytes accessed | tf_op | source)
XLA Modules:
  0.0 65.5 jit_solution(17840125415258901920)
XLA Ops:
  0.0 0.8 %broadcast_select_fusion.3 = (bf16[8,1536]{1,0:T(8,128)(2,1)S(1)}, bf16[8,1536]{1,0:T(8,128)(2,1)S(1)}) fusion(pred[]{:T(512)S(6)} %eq.5, bf16[512,1536]{1,0:T(8,128)(2,1)} %x_hbm.1), kind=kLoop, calls=%fused_computation.4 | loop fusion | flops 24576 | bytes 98305 | tf_op jit(solution)/shard_map/jit(_where)/select_n | solution.py:29
  0.8 0.5 collective-permute-start
  1.3 0.7 collective-permute-start.1
  1.9 1.3 %pad.4.codes_ref = s32[16,128]{1,0:T(8,128)} pad(s32[4,65]{1,0:T(4,128)} %param.14, s32[]{:T(128)} %constant.16.clone.1), padding=0_12x0_63 | pad | bytes 9236 | tf_op jit(solution)/shard_map/jit(_pad)/pad | solution.py:127
  3.2 0.0 collective-permute-done
  3.2 0.0 collective-permute-done.1
  3.2 0.6 pad_maximum_fusion.halo_ref
  3.8 0.0 copy-start.4
  3.8 0.0 copy-start
  3.8 0.0 copy-start.3
  3.9 13.8 %front.1 = (bf16[528,128]{1,0:T(8,128)(2,1)}, bf16[512,256]{1,0:T(8,128)(2,1)}) custom-call(bf16[512,1536]{1,0:T(8,128)(2,1)} %x_hbm.1, bf16[16,1536]{1,0:T(8,128)(2,1)} %pad_maximum_fusion.halo_ref, s32[16,128]{1,0:T(8,128)} %pad.4.codes_ref, bf16[3,1536,768]{2,1,0:T(8,128)(2,1)} %taps_hbm.1, bf16[768,1536]{1,0:T(8,128)(2,1)} %mix_hbm.1, ...), custom_call_target="tpu_custom_call" | custom-call | tf_op jit(solution)/shard_map/front/pallas_call | solution.py:134
  17.7 5.8 %collective-permute-start.2 = (bf16[528,128]{1,0:T(8,128)(2,1)}, bf16[528,128]{1,0:T(8,128)(2,1)S(1)}, u32[]{:S(2)}, u32[]{:S(2)}) collective-permute-start(bf16[528,128]{1,0:T(8,128)(2,1)} %get-tuple-element.37.refs_0_), channel_id=1, source_target_pairs={{0,2},{1,3},{2,0},{3,1},{4,6},{5,7},{6,4},{7,5},{8,10},{9,11},{10,... | collective-permute-start | bytes 405512 | tf_op jit(solution)/shard_map/ppermute | solution.py:512
  23.5 1.1 %collective-permute-start.6 = (bf16[512,256]{1,0:T(8,128)(2,1)}, bf16[512,256]{1,0:T(8,128)(2,1)S(1)}, u32[]{:S(2)}, u32[]{:S(2)}) collective-permute-start(bf16[512,256]{1,0:T(8,128)(2,1)} %get-tuple-element.38.refs_2_), channel_id=1, source_target_pairs={{0,1},{1,0},{2,3},{3,2},{4,5},{5,4},{6,7},{7,6},{8,9},{9,8},{10,11... | collective-permute-start | bytes 786440 | tf_op jit(solution)/shard_map/ppermute | solution.py:512
  24.6 0.8 %collective-permute-start.5 = (bf16[512,256]{1,0:T(8,128)(2,1)}, bf16[512,256]{1,0:T(8,128)(2,1)S(1)}, u32[]{:S(2)}, u32[]{:S(2)}) collective-permute-start(bf16[512,256]{1,0:T(8,128)(2,1)} %get-tuple-element.38.refs_2_), channel_id=1, source_target_pairs={{4,8},{5,9},{6,10},{7,11},{8,4},{9,5},{10,6},{11,7},{20,24},{21,25... | collective-permute-start | bytes 786440 | tf_op jit(solution)/shard_map/ppermute | solution.py:512
  25.4 4.4 %collective-permute-start.4 = (bf16[512,256]{1,0:T(8,128)(2,1)}, bf16[512,256]{1,0:T(8,128)(2,1)S(1)}, u32[]{:S(2)}, u32[]{:S(2)}) collective-permute-start(bf16[512,256]{1,0:T(8,128)(2,1)} %get-tuple-element.38.refs_2_), channel_id=1, source_target_pairs={{0,4},{1,5},{2,6},{3,7},{4,0},{5,1},{6,2},{7,3},{8,12},{9,13},{10,... | collective-permute-start | bytes 786440 | tf_op jit(solution)/shard_map/ppermute | solution.py:512
  29.9 0.0 collective-permute-done.2.refs_1_.refs_0_
  29.9 0.0 copy-done.4
  29.9 0.0 collective-permute-done.6.refs_3_
  29.9 0.0 copy-done
  29.9 0.0 copy-done.3
  29.9 0.0 copy-start.1
  29.9 0.9 %copy-done.1 = bf16[528,128]{1,0:T(8,128)(2,1)S(1)} copy-done((bf16[528,128]{1,0:T(8,128)(2,1)S(1)}, bf16[528,128]{1,0:T(8,128)(2,1)}, u32[]{:S(2)}) %copy-start.1) | copy-done | bytes 135192
  30.8 5.4 %own.1 = (f32[512,128]{1,0:T(8,128)S(1)}, f32[512,128]{1,0:T(8,128)S(1)}, f32[512,128]{1,0:T(8,128)S(1)}, f32[512,128]{1,0:T(8,128)S(1)}, f32[512,128]{1,0:T(8,128)S(1)}, /*index=5*/f32[512,128]{1,0:T(8,128)S(1)}) custom-call(s32[8,65]{1,0:T(8,128)S(1)} %pad_add_fusion.codes_ref, bf16[528,128]{1,0:T(8,128)(2,1)S(1)} %copy-done.1, ...), custom_call_target="tpu_custom_call" | custom-call | flops 536870912 | bytes 4194304 | tf_op jit(solution)/shard_map/own/pallas_call | solution.py:450
  36.2 0.0 collective-permute-done.5.refs_4_
  36.2 0.1 collective-permute-done.4.refs_2_
  36.3 0.0 copy-start.2
  36.3 0.0 collective-permute-start.7
  36.3 0.5 collective-permute-start.8
  36.8 1.6 %collective-permute-start.3 = (bf16[512,256]{1,0:T(8,128)(2,1)}, bf16[512,256]{1,0:T(8,128)(2,1)S(1)}, u32[]{:S(2)}, u32[]{:S(2)}) collective-permute-start(bf16[512,256]{1,0:T(8,128)(2,1)} %get-tuple-element.38.refs_2_), channel_id=1, source_target_pairs={{0,8},{1,9},{2,10},{3,11},{4,12},{5,13},{6,14},{7,15},{8,0},{9,1},... | collective-permute-start | bytes 786440 | tf_op jit(solution)/shard_map/ppermute | solution.py:512
  38.4 0.0 collective-permute-done.7.refs_3_
  38.4 0.0 collective-permute-done.8.refs_5_
  38.4 4.6 %near.1 = (f32[512,128]{1,0:T(8,128)S(1)}, f32[512,128]{1,0:T(8,128)S(1)}, f32[512,128]{1,0:T(8,128)S(1)}, f32[512,128]{1,0:T(8,128)S(1)}, f32[512,128]{1,0:T(8,128)S(1)}, /*index=5*/f32[512,128]{1,0:T(8,128)S(1)}) custom-call(s32[8,65]{1,0:T(8,128)S(1)} %pad_add_fusion.codes_ref, bf16[528,128]{1,0:T(8,128)(2,1)S(1)} %copy-done.1, ...), custom_call_target="tpu_custom_call" | custom-call | flops 1073741824 | bytes 8388608 | tf_op jit(solution)/shard_map/near/pallas_call | solution.py:450
  43.0 8.8 %collective-permute-done.3.refs_1_ = bf16[512,256]{1,0:T(8,128)(2,1)S(1)} collective-permute-done((bf16[512,256]{1,0:T(8,128)(2,1)}, bf16[512,256]{1,0:T(8,128)(2,1)S(1)}, u32[]{:S(2)}, u32[]{:S(2)}) %collective-permute-start.3) | collective-permute-done | bytes 262176 | tf_op jit(solution)/shard_map/ppermute | solution.py:512
  51.8 0.0 collective-permute-start.9
  51.8 1.5 %collective-permute-done.9.refs_2_ = bf16[512,256]{1,0:T(8,128)(2,1)S(1)} collective-permute-done((bf16[512,256]{1,0:T(8,128)(2,1)S(1)}, bf16[512,256]{1,0:T(8,128)(2,1)S(1)}, u32[]{:S(2)}, u32[]{:S(2)}) %collective-permute-start.9) | collective-permute-done | bytes 262176 | tf_op jit(solution)/shard_map/ppermute | solution.py:512
  53.4 2.7 %far_peer.1 = f32[520,128]{1,0:T(8,128)S(1)} custom-call(s32[8,65]{1,0:T(8,128)S(1)} %pad_add_fusion.codes_ref, bf16[528,128]{1,0:T(8,128)(2,1)S(1)} %collective-permute-done.2.refs_1_.refs_0_, bf16[512,256]{1,0:T(8,128)(2,1)S(1)} %collective-permute-done.3.refs_1_, bf16[512,256]{1,0:T(8,128)(2,1)S(1)} %collective-permute-done.9.refs_2_, ...), custom_call_target="tpu_custom_call" | custom-call | flops 268435456 | bytes 2097152 | tf_op jit(solution)/shard_map/far_peer/pallas_call | solution.py:450
  56.0 0.1 collective-permute-start.10
  56.1 0.0 copy-done.2
  56.1 1.9 %far_own.1 = (f32[512,128]{1,0:T(8,128)S(1)}, f32[512,128]{1,0:T(8,128)S(1)}, f32[512,128]{1,0:T(8,128)S(1)}) custom-call(s32[8,65]{1,0:T(8,128)S(1)} %pad_add_fusion.codes_ref, bf16[528,128]{1,0:T(8,128)(2,1)S(1)} %copy-done.2, bf16[512,256]{1,0:T(8,128)(2,1)S(1)} %collective-permute-done.3.refs_1_, bf16[512,256]{1,0:T(8,128)(2,1)S(1)} %collective-permute-done.9.refs_2_, ...), custom_call_target="tpu_custom_call" | custom-call | flops 268435456 | bytes 2097152 | tf_op jit(solution)/shard_map/far_own/pallas_call | solution.py:450
  58.1 6.5 %collective-permute-done.10.pack_ref = f32[520,128]{1,0:T(8,128)S(1)} collective-permute-done((f32[520,128]{1,0:T(8,128)S(1)}, f32[520,128]{1,0:T(8,128)S(1)}, u32[]{:S(2)}, u32[]{:S(2)}) %collective-permute-start.10) | collective-permute-done | bytes 266272 | tf_op jit(solution)/shard_map/ppermute | solution.py:512
  64.5 0.9 %merge.1 = bf16[512,128]{1,0:T(8,128)(2,1)} custom-call(f32[512,128]{1,0:T(8,128)S(1)} %get-tuple-element.63.peak_ref, f32[512,128]{1,0:T(8,128)S(1)} %get-tuple-element.64.total_ref, f32[512,128]{1,0:T(8,128)S(1)} %get-tuple-element.65.acc_ref, f32[520,128]{1,0:T(8,128)S(1)} %collective-permute-done.10.pack_ref), custom_call_target="tpu_custom_call" | custom-call | tf_op jit(solution)/shard_map/merge/pallas_call | solution.py:551
  (3 shorter events, 0.0 us)
Async XLA Ops:
  0.8 2.4 %collective-permute-start = (bf16[8,1536]{1,0:T(8,128)(2,1)S(1)}, bf16[8,1536]{1,0:T(8,128)(2,1)S(1)}, u32[]{:S(2)}, u32[]{:S(2)}) collective-permute-start(bf16[8,1536]{1,0:T(8,128)(2,1)S(1)} %get-tuple-element.69), channel_id=1, source_target_pairs={{0,1},{1,0},{2,3},{3,2},{4,5},{5,4},{6,7},{7,6},{8,9},{9,8},{10,11... | collective-permute-start | bytes 73736 | tf_op jit(solution)/shard_map/ppermute | solution.py:29
  1.3 1.9 %collective-permute-start.1 = (bf16[8,1536]{1,0:T(8,128)(2,1)S(1)}, bf16[8,1536]{1,0:T(8,128)(2,1)S(1)}, u32[]{:S(2)}, u32[]{:S(2)}) collective-permute-start(bf16[8,1536]{1,0:T(8,128)(2,1)S(1)} %get-tuple-element.70), channel_id=1, source_target_pairs={{1,2},{3,4},{5,6},{7,8},{9,10},{11,12},{13,14},{2,1},{4,3},{6,5},{... | collective-permute-start | bytes 73736 | tf_op jit(solution)/shard_map/ppermute | solution.py:28
  3.8 26.0 %copy-start.4 = (s32[4,65]{1,0:T(4,128)S(1)}, s32[4,65]{1,0:T(4,128)}, u32[]{:S(2)}) copy-start(s32[4,65]{1,0:T(4,128)} %param.14) | copy-start | bytes 3124
  3.8 26.1 %copy-start = (bf16[16,128,128]{2,1,0:T(8,128)(2,1)S(1)}, bf16[16,128,128]{2,1,0:T(8,128)(2,1)}, u32[]{:S(2)}) copy-start(bf16[16,128,128]{2,1,0:T(8,128)(2,1)} %refs_3_.3) | copy-start | bytes 1572868
  3.8 26.1 %copy-start.3 = (s32[8192]{0:T(1024)S(1)}, s32[8192]{0:T(1024)}, u32[]{:S(2)}) copy-start(s32[8192]{0:T(1024)} %param.15) | copy-start | bytes 98308
  17.7 12.2 %collective-permute-start.2 = (bf16[528,128]{1,0:T(8,128)(2,1)}, bf16[528,128]{1,0:T(8,128)(2,1)S(1)}, u32[]{:S(2)}, u32[]{:S(2)}) collective-permute-start(bf16[528,128]{1,0:T(8,128)(2,1)} %get-tuple-element.37.refs_0_), channel_id=1, source_target_pairs={{0,2},{1,3},{2,0},{3,1},{4,6},{5,7},{6,4},{7,5},{8,10},{9,11},{10,... | collective-permute-start | bytes 405512 | tf_op jit(solution)/shard_map/ppermute | solution.py:512
  23.5 6.4 %collective-permute-start.6 = (bf16[512,256]{1,0:T(8,128)(2,1)}, bf16[512,256]{1,0:T(8,128)(2,1)S(1)}, u32[]{:S(2)}, u32[]{:S(2)}) collective-permute-start(bf16[512,256]{1,0:T(8,128)(2,1)} %get-tuple-element.38.refs_2_), channel_id=1, source_target_pairs={{0,1},{1,0},{2,3},{3,2},{4,5},{5,4},{6,7},{7,6},{8,9},{9,8},{10,11... | collective-permute-start | bytes 786440 | tf_op jit(solution)/shard_map/ppermute | solution.py:512
  24.6 11.6 %collective-permute-start.5 = (bf16[512,256]{1,0:T(8,128)(2,1)}, bf16[512,256]{1,0:T(8,128)(2,1)S(1)}, u32[]{:S(2)}, u32[]{:S(2)}) collective-permute-start(bf16[512,256]{1,0:T(8,128)(2,1)} %get-tuple-element.38.refs_2_), channel_id=1, source_target_pairs={{4,8},{5,9},{6,10},{7,11},{8,4},{9,5},{10,6},{11,7},{20,24},{21,25... | collective-permute-start | bytes 786440 | tf_op jit(solution)/shard_map/ppermute | solution.py:512
  25.4 10.9 %collective-permute-start.4 = (bf16[512,256]{1,0:T(8,128)(2,1)}, bf16[512,256]{1,0:T(8,128)(2,1)S(1)}, u32[]{:S(2)}, u32[]{:S(2)}) collective-permute-start(bf16[512,256]{1,0:T(8,128)(2,1)} %get-tuple-element.38.refs_2_), channel_id=1, source_target_pairs={{0,4},{1,5},{2,6},{3,7},{4,0},{5,1},{6,2},{7,3},{8,12},{9,13},{10,... | collective-permute-start | bytes 786440 | tf_op jit(solution)/shard_map/ppermute | solution.py:512
  29.9 0.9 %copy-start.1 = (bf16[528,128]{1,0:T(8,128)(2,1)S(1)}, bf16[528,128]{1,0:T(8,128)(2,1)}, u32[]{:S(2)}) copy-start(bf16[528,128]{1,0:T(8,128)(2,1)} %get-tuple-element.37.refs_0_) | copy-start | bytes 405508
  36.3 19.9 %copy-start.2 = (bf16[528,128]{1,0:T(8,128)(2,1)S(1)}, bf16[528,128]{1,0:T(8,128)(2,1)}, u32[]{:S(2)}) copy-start(bf16[528,128]{1,0:T(8,128)(2,1)} %get-tuple-element.37.refs_0_) | copy-start | bytes 405508
  36.3 2.1 %collective-permute-start.7 = (bf16[512,256]{1,0:T(8,128)(2,1)S(1)}, bf16[512,256]{1,0:T(8,128)(2,1)S(1)}, u32[]{:S(2)}, u32[]{:S(2)}) collective-permute-start(bf16[512,256]{1,0:T(8,128)(2,1)S(1)} %collective-permute-done.4.refs_2_), channel_id=1, source_target_pairs={{0,1},{1,0},{2,3},{3,2},{4,5},{5,4},{6,7},{7,6},{8,9},{9,8},{10,11... | collective-permute-start | bytes 786440 | tf_op jit(solution)/shard_map/ppermute | solution.py:512
  36.3 2.1 %collective-permute-start.8 = (bf16[512,256]{1,0:T(8,128)(2,1)S(1)}, bf16[512,256]{1,0:T(8,128)(2,1)S(1)}, u32[]{:S(2)}, u32[]{:S(2)}) collective-permute-start(bf16[512,256]{1,0:T(8,128)(2,1)S(1)} %collective-permute-done.5.refs_4_), channel_id=1, source_target_pairs={{0,1},{1,0},{2,3},{3,2},{4,5},{5,4},{6,7},{7,6},{8,9},{9,8},{10,11... | collective-permute-start | bytes 786440 | tf_op jit(solution)/shard_map/ppermute | solution.py:512
  36.8 15.0 %collective-permute-start.3 = (bf16[512,256]{1,0:T(8,128)(2,1)}, bf16[512,256]{1,0:T(8,128)(2,1)S(1)}, u32[]{:S(2)}, u32[]{:S(2)}) collective-permute-start(bf16[512,256]{1,0:T(8,128)(2,1)} %get-tuple-element.38.refs_2_), channel_id=1, source_target_pairs={{0,8},{1,9},{2,10},{3,11},{4,12},{5,13},{6,14},{7,15},{8,0},{9,1},... | collective-permute-start | bytes 786440 | tf_op jit(solution)/shard_map/ppermute | solution.py:512
  51.8 1.5 %collective-permute-start.9 = (bf16[512,256]{1,0:T(8,128)(2,1)S(1)}, bf16[512,256]{1,0:T(8,128)(2,1)S(1)}, u32[]{:S(2)}, u32[]{:S(2)}) collective-permute-start(bf16[512,256]{1,0:T(8,128)(2,1)S(1)} %collective-permute-done.3.refs_1_), channel_id=1, source_target_pairs={{0,1},{1,0},{2,3},{3,2},{4,5},{5,4},{6,7},{7,6},{8,9},{9,8},{10,11... | collective-permute-start | bytes 786440 | tf_op jit(solution)/shard_map/ppermute | solution.py:512
  56.0 8.5 %collective-permute-start.10 = (f32[520,128]{1,0:T(8,128)S(1)}, f32[520,128]{1,0:T(8,128)S(1)}, u32[]{:S(2)}, u32[]{:S(2)}) collective-permute-start(f32[520,128]{1,0:T(8,128)S(1)} %far_peer.1), channel_id=1, source_target_pairs={{0,2},{1,3},{2,0},{3,1},{4,6},{5,7},{6,4},{7,5},{8,10},{9,11},{10,... | collective-permute-start | bytes 798728 | tf_op jit(solution)/shard_map/ppermute | solution.py:512

commit v4 on v2

--- a/solution.py
+++ b/solution.py
@@ -8,6 +8,7 @@
 from jax.experimental.pallas import tpu as pltpu
 from jax.sharding import PartitionSpec as P
 
+
 HDIM = 128
 CONV_DILATION = 8
 HALF = 4096
@@ -15,6 +16,7 @@
 
 masked_score = -1e30
 norm_eps = 1e-06
+LOG2E = 1.4426950408889634
 
 
 def halo_rows(activations):
@@ -25,49 +27,33 @@
     last = lax.slice_in_dim(activations, rows - CONV_DILATION, rows, axis=0)
     inner = [(i, i ^ 1) for i in range(size)]
     outer = [(i, i + 1) for i in range(1, size - 1, 2)] + [(i + 1, i) for i in range(1, size - 1, 2)]
+    from_inner = lax.ppermute(jnp.where(odd, initial, last), "seq", inner)
     from_outer = lax.ppermute(jnp.where(odd, last, initial), "seq", outer)
-    from_inner = lax.ppermute(jnp.where(odd, initial, last), "seq", inner)
-    before = jnp.where(odd, from_inner, from_outer)
-    after = jnp.where(odd, from_outer, from_inner)
-    return jnp.concatenate([before, after], axis=0)
+    return from_inner, from_outer
 
 
 def gelu(v):
     return 0.5 * v * (1.0 + lax.erf(v * math.sqrt(0.5)))
 
 
-def front_kernel(
-    x_hbm,
-    halo_ref,
-    taps_hbm,
-    mix_hbm,
-    wq_hbm,
-    wkv_hbm,
-    q_ref,
-    kv_ref,
-    x_ref,
-    taps,
-    mix,
-    wq,
-    wkv,
-    outer,
-    inner,
-    squeezed,
-    mixed,
-    sems,
-):
-    rows, channels = x_ref.shape
-    hidden = squeezed.shape[1]
+def lift_kernel(x_hbm, taps_hbm, mix_hbm, wq_hbm, wkv_hbm, tiles_hbm, *refs):
+    x_ref, taps, mix, wq, wkv, inner, outer, table, tiles, sems = refs
     copies = [
-        pltpu.make_async_copy(x_hbm, x_ref, sems.at[0]),
-        pltpu.make_async_copy(taps_hbm, taps, sems.at[1]),
-        pltpu.make_async_copy(mix_hbm, mix, sems.at[2]),
-        pltpu.make_async_copy(wq_hbm, wq, sems.at[3]),
-        pltpu.make_async_copy(wkv_hbm, wkv, sems.at[4]),
+        pltpu.make_async_copy(source, target, sems.at[i])
+        for i, (source, target) in enumerate(
+            [
+                (x_hbm, x_ref),
+                (tiles_hbm, tiles),
+                (taps_hbm, taps),
+                (mix_hbm, mix),
+                (wq_hbm, wq),
+                (wkv_hbm, wkv),
+            ]
+        )
     ]
     for copy in copies:
         copy.start()
-    edge = gelu(halo_ref[...].astype(jnp.float32))
+    rows, channels = x_ref.shape
     step = 32
     d = CONV_DILATION
     copies[0].wait()
@@ -81,10 +67,73 @@
         )
         return g[step - d :]
 
-    tail = lax.fori_loop(0, rows // step, lift, edge[:d])
-    outer[rows : rows + 2 * d, :] = jnp.concatenate([tail, edge[d:]], axis=0).astype(jnp.bfloat16)
-
+    edge = jnp.zeros((d, channels), jnp.float32)
+    tail = lax.fori_loop(0, rows // step, lift, edge)
+    outer[rows : rows + 2 * d, :] = jnp.concatenate([tail, edge], axis=0).astype(jnp.bfloat16)
     copies[1].wait()
+    table[...] = tiles[...].astype(jnp.float32) * LOG2E
+    for copy in copies[2:]:
+        copy.wait()
+
+
+def lift(activations, dilated_tap_weight, conv_mix, w_query, w_keyval, contact_tiles):
+    rows, channels = activations.shape
+    moved = [
+        pltpu.with_memory_space_constraint(a, pltpu.HBM)
+        for a in (activations, dilated_tap_weight, conv_mix, w_query, w_keyval)
+    ]
+    contact_tiles = pltpu.with_memory_space_constraint(contact_tiles, pltpu.HBM)
+    vmem = pl.BlockSpec(memory_space=pltpu.VMEM)
+    return pl.pallas_call(
+        lift_kernel,
+        out_shape=[jax.ShapeDtypeStruct(a.shape, a.dtype) for a in moved]
+        + [
+            jax.ShapeDtypeStruct((rows, channels), jnp.bfloat16),
+            jax.ShapeDtypeStruct((rows + 2 * CONV_DILATION, channels), jnp.bfloat16),
+            jax.ShapeDtypeStruct(contact_tiles.shape, jnp.float32),
+        ],
+        in_specs=[pl.BlockSpec(memory_space=pltpu.HBM)] * 6,
+        out_specs=[vmem] * 8,
+        scratch_shapes=[
+            pltpu.VMEM(contact_tiles.shape, contact_tiles.dtype),
+            pltpu.SemaphoreType.DMA((6,)),
+        ],
+        compiler_params=pltpu.CompilerParams(vmem_limit_bytes=24 << 20),
+        name="lift",
+    )(*moved, contact_tiles)
+
+
+def front_kernel(
+    x_ref,
+    taps,
+    mix,
+    wq,
+    wkv,
+    inner,
+    outer_ref,
+    twin_ref,
+    outside_ref,
+    codes_ref,
+    q_ref,
+    kv_ref,
+    outer,
+    squeezed,
+    mixed,
+):
+    rows, channels = x_ref.shape
+    hidden = squeezed.shape[1]
+    d = CONV_DILATION
+    odd = lax.axis_index("seq") % 2 == 1
+    beside = gelu(twin_ref[...].astype(jnp.float32))
+    beyond = gelu(outside_ref[...].astype(jnp.float32))
+    before = jnp.where(odd, beside, beyond)
+    after = jnp.where(odd, beyond, beside)
+    outer[...] = outer_ref[...]
+    initial = outer_ref[0 : 2 * d, :].astype(jnp.float32)[d:]
+    last = outer_ref[rows : rows + 2 * d, :].astype(jnp.float32)[:d]
+    outer[0 : 2 * d, :] = jnp.concatenate([before, initial], axis=0).astype(jnp.bfloat16)
+    outer[rows : rows + 2 * d, :] = jnp.concatenate([last, after], axis=0).astype(jnp.bfloat16)
+
     wide = 256
     for n in range(hidden // wide):
         cols = slice(n * wide, (n + 1) * wide)
@@ -95,7 +144,6 @@
         )
         squeezed[:, cols] = gelu(conv).astype(jnp.bfloat16)
 
-    copies[2].wait()
     square = jnp.zeros((rows, 128), jnp.float32)
     for n in range(channels // wide):
         cols = slice(n * wide, (n + 1) * wide)
@@ -107,45 +155,41 @@
             piece = part[:, k * 128 : (k + 1) * 128]
             square += piece * piece
     gain = lax.rsqrt(jnp.sum(square, axis=1, keepdims=True) / channels + norm_eps)
-    copies[3].wait()
-    copies[4].wait()
     normed = (mixed[...] * gain).astype(jnp.bfloat16)
-    q_ref[...] = jnp.dot(normed, wq[...], preferred_element_type=jnp.float32).astype(jnp.bfloat16)
+    q_ref[0:rows, :] = jnp.dot(normed, wq[...], preferred_element_type=jnp.float32).astype(
+        jnp.bfloat16
+    )
+    q_ref[rows:, :] = jnp.zeros((q_ref.shape[0] - rows, q_ref.shape[1]), jnp.bfloat16)
+    q_ref[rows : rows + codes_ref.shape[0], 0 : codes_ref.shape[1]] = (
+        codes_ref[...].astype(jnp.float32).astype(jnp.bfloat16)
+    )
     kv_ref[...] = jnp.dot(normed, wkv[...], preferred_element_type=jnp.float32).astype(jnp.bfloat16)
 
 
-def front(activations, halo, dilated_tap_weight, conv_mix, w_query, w_keyval):
+CODE_ROWS = 16
+
+
+def front(lifted, halo, tile_codes):
+    activations, _, conv_mix, w_query, w_keyval, _, outer = lifted
     rows, channels = activations.shape
-    hidden = conv_mix.shape[0]
-    anywhere = pl.BlockSpec(memory_space=pl.ANY)
     vmem = pl.BlockSpec(memory_space=pltpu.VMEM)
     bf16 = jnp.bfloat16
     return pl.pallas_call(
         front_kernel,
         out_shape=[
-            jax.ShapeDtypeStruct((rows, w_query.shape[1]), bf16),
+            jax.ShapeDtypeStruct((rows + CODE_ROWS, w_query.shape[1]), bf16),
             jax.ShapeDtypeStruct((rows, w_keyval.shape[1]), bf16),
         ],
-        in_specs=[anywhere, vmem, anywhere, anywhere, anywhere, anywhere],
+        in_specs=[vmem] * 10,
         out_specs=[vmem, vmem],
         scratch_shapes=[
-            pltpu.VMEM(activations.shape, bf16),
-            pltpu.VMEM(dilated_tap_weight.shape, bf16),
-            pltpu.VMEM(conv_mix.shape, bf16),
-            pltpu.VMEM(w_query.shape, bf16),
-            pltpu.VMEM(w_keyval.shape, bf16),
-            pltpu.VMEM((rows + 2 * CONV_DILATION, channels), bf16),
-            pltpu.VMEM((rows, channels), bf16),
-            pltpu.VMEM((rows, hidden), bf16),
+            pltpu.VMEM(outer.shape, bf16),
+            pltpu.VMEM((rows, conv_mix.shape[0]), bf16),
             pltpu.VMEM((rows, channels), jnp.float32),
-            pltpu.SemaphoreType.DMA((5,)),
         ],
-        compiler_params=pltpu.CompilerParams(vmem_limit_bytes=60 << 20),
+        compiler_params=pltpu.CompilerParams(vmem_limit_bytes=24 << 20),
         name="front",
-    )(activations, halo, dilated_tap_weight, conv_mix, w_query, w_keyval)
-
-
-LOG2E = 1.4426950408889634
+    )(*lifted, *halo, tile_codes)
 
 
 def attend_kernel(
@@ -166,7 +210,7 @@
     sems,
 ):
     rows, head_dim = q_ref.shape
-    code_count, tile, _ = tiles_ref.shape
+    _, tile, _ = tiles_ref.shape
     tiles_per_block = rows // tile
     position = place_ref[0]
     first = place_ref[1]
@@ -257,6 +301,239 @@
         )
 
     out_ref[...] = (acc[...] / jnp.sum(total[...], axis=1, keepdims=True)).astype(out_ref.dtype)
+
+
+def block_scores(shift, edge, raw, invalid, table, codes_ref, half, qt, tile):
+    factor = LOG2E / math.sqrt(HDIM)
+    count = raw.shape[1] // tile
+    columns = []
+    if edge:
+        lag = lax.broadcasted_iota(jnp.int32, (tile, tile), 1) - lax.broadcasted_iota(
+            jnp.int32, (tile, tile), 0
+        )
+    for kt in range(count):
+        span = slice(kt * tile, (kt + 1) * tile)
+        offset = jnp.clip(shift * count + kt - qt + HALF // tile, 0, 2 * (HALF // tile))
+        dropped = invalid[:, span]
+        if edge:
+            apart = lag + (shift * (tile * count) + (kt - qt) * tile)
+            dropped = jnp.where(apart == 0, 0.0, dropped)
+            dropped = jnp.where(jnp.abs(apart) <= HALF, dropped, masked_score)
+        part = raw[qt * tile : (qt + 1) * tile, span]
+        columns.append((part * factor + table[codes_ref[half + qt, offset]]) + dropped)
+    return columns
+
+
+def absorb_kernel(reach, flips, blocks, begin, pack, codes_ref, *refs):
+    sets, n = len(flips), len(blocks)
+    q_refs, refs = refs[:sets], refs[sets:]
+    kv_refs, refs = refs[:n], refs[n:]
+    table, valid_ref = refs[:2]
+    refs = refs[2:]
+    if not begin:
+        state_refs, refs = refs[: 3 * sets], refs[3 * sets :]
+    outs = 1 if pack else 3 * sets
+    out_refs, refs = refs[:outs], refs[outs:]
+    scores, peak, total, acc = refs
+    rows, head_dim = acc.shape
+    tile = table.shape[1]
+    tiles_per_block = rows // tile
+    position = lax.axis_index("seq")
+
+    for s, flip in enumerate(flips):
+        owner = position ^ flip
+        q_ref = q_refs[s]
+        half = 0 if flip == 0 else tiles_per_block
+        if begin:
+            peak[...] = jnp.full_like(peak, masked_score)
+        else:
+            peak[...] = state_refs[3 * s][...]
+
+        def each(step):
+            for j, block in enumerate(blocks):
+                shift = (position ^ block) - owner
+                run = functools.partial(step, j, shift, (block ^ flip) in (0, reach))
+                if block ^ flip < reach:
+                    run()
+                else:
+                    pl.when(jnp.abs(shift) <= reach)(run)
+
+        def score(j, shift, edge):
+            raw = lax.dot_general(
+                q_ref[0:rows, :],
+                kv_refs[j][:, :head_dim],
+                (((1,), (1,)), ((), ())),
+                preferred_element_type=jnp.float32,
+            )
+            invalid = jnp.where(valid_ref[owner + shift] == 1, 0.0, masked_score)
+            for qt in range(tiles_per_block):
+                span = slice(qt * tile, (qt + 1) * tile)
+                peak_now = peak[span, :]
+                columns = block_scores(
+                    shift, edge, raw, invalid, table, codes_ref, half, qt, tile
+                )
+                for kt, column in enumerate(columns):
+                    scores[j, span, kt * tile : (kt + 1) * tile] = column
+                    peak_now = jnp.maximum(peak_now, column)
+                peak[span, :] = peak_now
+
+        def weigh(j, shift, edge):
+            parts = []
+            sums = total[...]
+            for kt in range(tiles_per_block):
+                probs = jnp.exp2(scores[j, :, kt * tile : (kt + 1) * tile] - peak[...])
+                sums = sums + probs
+                parts.append(probs.astype(jnp.bfloat16))
+            total[...] = sums
+            acc[...] += jnp.dot(
+                jnp.concatenate(parts, axis=1),
+                kv_refs[j][:, head_dim:],
+                preferred_element_type=jnp.float32,
+            )
+
+        each(score)
+        peak[...] = jnp.broadcast_to(jnp.max(peak[...], axis=1, keepdims=True), peak.shape)
+        if begin:
+            total[...] = jnp.zeros_like(total)
+            acc[...] = jnp.zeros_like(acc)
+        else:
+            rescale = jnp.exp2(state_refs[3 * s][...] - peak[...])
+            total[...] = state_refs[3 * s + 1][...] * rescale
+            acc[...] = state_refs[3 * s + 2][...] * rescale
+        each(weigh)
+
+        if pack:
+            out_refs[0][0:rows, :] = acc[...]
+            sums = jnp.broadcast_to(jnp.sum(total[...], axis=1, keepdims=True), total.shape)
+            eye = on_diagonal(tile)
+            lines = []
+            for column in (peak[...], sums):
+                for qt in range(tiles_per_block):
+                    part = column[qt * tile : (qt + 1) * tile, :]
+                    lines.append(jnp.sum(jnp.where(eye, part, 0.0), axis=0, keepdims=True))
+            out_refs[0][rows:, :] = jnp.concatenate(lines, axis=0)
+        else:
+            out_refs[3 * s][...] = peak[...]
+            out_refs[3 * s + 1][...] = total[...]
+            out_refs[3 * s + 2][...] = acc[...]
+
+
+def on_diagonal(tile):
+    return lax.broadcasted_iota(jnp.int32, (tile, tile), 0) == lax.broadcasted_iota(
+        jnp.int32, (tile, tile), 1
+    )
+
+
+def absorb(reach, codes, queries, keyvals, table, valid_rows, flips, blocks, state, pack):
+    rows = keyvals[0].shape[0]
+    head_dim = queries[0].shape[1]
+    tile = table.shape[1]
+    n = len(blocks)
+    vmem = pl.BlockSpec(memory_space=pltpu.VMEM)
+    smem = pl.BlockSpec(memory_space=pltpu.SMEM)
+    column = jax.ShapeDtypeStruct((rows, tile), jnp.float32)
+    if pack:
+        out_shape = [jax.ShapeDtypeStruct((rows + 2 * (rows // tile), head_dim), jnp.float32)]
+    else:
+        out_shape = [column, column, column] * len(flips)
+    units = len(flips) * n
+    return pl.pallas_call(
+        functools.partial(absorb_kernel, reach, flips, blocks, not state, pack),
+        out_shape=out_shape,
+        in_specs=[smem] + [vmem] * (len(flips) + n + 2 + len(state)),
+        out_specs=[vmem] * len(out_shape),
+        scratch_shapes=[
+            pltpu.VMEM((n, rows, rows), jnp.float32),
+            pltpu.VMEM((rows, tile), jnp.float32),
+            pltpu.VMEM((rows, tile), jnp.float32),
+            pltpu.VMEM((rows, head_dim), jnp.float32),
+        ],
+        compiler_params=pltpu.CompilerParams(vmem_limit_bytes=24 << 20),
+        cost_estimate=pl.CostEstimate(
+            flops=units * 4 * rows * rows * head_dim,
+            bytes_accessed=units * 4 * rows * rows,
+            transcendentals=units * rows * rows,
+        ),
+    )(codes, *queries, *keyvals, table, valid_rows, *state)
+
+
+def merge_kernel(peak_ref, total_ref, acc_ref, pack_ref, out_ref):
+    rows, _ = acc_ref.shape
+    tile = peak_ref.shape[1]
+    eye = on_diagonal(tile)
+    count = rows // tile
+    for qt in range(count):
+        span = slice(qt * tile, (qt + 1) * tile)
+
+        def column(line):
+            row = pack_ref[rows + line : rows + line + 1, :]
+            return jnp.sum(jnp.where(eye, row, 0.0), axis=1, keepdims=True)
+
+        peak_a = peak_ref[span, :]
+        peak_b = column(qt)
+        total_a = jnp.sum(total_ref[span, :], axis=1, keepdims=True)
+        total_b = column(count + qt)
+        top = jnp.maximum(peak_a, peak_b)
+        scale_a = jnp.exp2(peak_a - top)
+        scale_b = jnp.exp2(peak_b - top)
+        whole = total_a * scale_a + total_b * scale_b
+        out_ref[span, :] = (
+            (acc_ref[span, :] * scale_a + pack_ref[span, :] * scale_b) / whole
+        ).astype(out_ref.dtype)
+
+
+def attend_split(queries, keyval, table, tile_codes, bin_valid, seq_size):
+    rows = keyval.shape[0]
+    reach = HALF // rows
+    z = seq_size // 4
+    half = z // 2
+    valid_rows = bin_valid.reshape(seq_size, 1, rows)
+
+    def trade(x, flip, some=None):
+        pairs = [(i, i ^ flip) for i in range(seq_size) if some is None or some(i // z)]
+        return lax.ppermute(x, "seq", pairs)
+
+    peer_queries = trade(queries, half)
+    far = trade(keyval, 2 * z)
+    middle = trade(keyval, 3 * z, lambda level: level in (1, 2))
+    near = trade(keyval, z)
+    twin = trade(keyval, 1)
+    peer_codes = peer_queries[rows : rows + tile_codes.shape[0], : tile_codes.shape[1]]
+    codes = jnp.concatenate([tile_codes, peer_codes.astype(jnp.int32)], axis=0)
+    common = (table, valid_rows)
+    state = absorb(
+        reach, codes, [queries, peer_queries], [keyval, twin], *common, (0, half), (0, 1), [], False
+    )
+    near, state = lax.optimization_barrier((near, state))
+    near_twin = trade(near, 1)
+    state = absorb(
+        reach,
+        codes,
+        [queries, peer_queries],
+        [near, near_twin],
+        *common,
+        (0, half),
+        (z, z + 1),
+        state,
+        False,
+    )
+    middle, far, state = lax.optimization_barrier((middle, far, state))
+    middle_twin = trade(middle, 1)
+    far_twin = trade(far, 1)
+    away = [middle, middle_twin, far, far_twin]
+    leaps = (3 * z, 3 * z + 1, 2 * z, 2 * z + 1)
+    (pack,) = absorb(reach, codes, [peer_queries], away, *common, (half,), leaps, state[3:], True)
+    other = trade(pack, half)
+    peak, total, acc = absorb(reach, codes, [queries], away, *common, (0,), leaps, state[:3], False)
+    vmem = pl.BlockSpec(memory_space=pltpu.VMEM)
+    return pl.pallas_call(
+        merge_kernel,
+        out_shape=jax.ShapeDtypeStruct((rows, queries.shape[1]), jnp.bfloat16),
+        in_specs=[vmem] * 4,
+        out_specs=vmem,
+        compiler_params=pltpu.CompilerParams(vmem_limit_bytes=8 << 20),
+        name="merge",
+    )(peak, total, acc, other)
 
 
 def attend(queries, everything, contact_tiles, tile_codes, bin_valid, position, seq_size):
@@ -301,9 +578,14 @@
 ):
     seq_size = lax.axis_size("seq")
     position = lax.axis_index("seq")
-    queries, keyval = front(
-        activations, halo_rows(activations), dilated_tap_weight, conv_mix, w_query, w_keyval
-    )
+    halo = halo_rows(activations)
+    *lifted, table = lift(
+        activations, dilated_tap_weight, conv_mix, w_query, w_keyval, contact_tiles
+    )
+    queries, keyval = front(lifted, halo, tile_codes)
+    if seq_size == 16 and seq_size * activations.shape[0] == 2 * HALF:
+        return attend_split(queries, keyval, table, tile_codes, bin_valid, seq_size)
+    queries = queries[: activations.shape[0]]
     everything = lax.all_gather(keyval, "seq", axis=0, tiled=True)
     return attend(queries, everything, contact_tiles, tile_codes, bin_valid, position, seq_size)
 

time: 102 us -> 62.5 us (0.61)
  the two profiles are of different devices: /device:TPU:13 before, /device:TPU:20 now
where the time goes in v4:
time: 62.5 us; the launch traced here: 62.3 us
  Pallas kernels  26.6 us (43%)
  waiting for transfers between devices  23.5 us (38%)
  starting transfers between devices  11.3 us (18%)
  other arithmetic  0.78 us (1%)
    ppermute x9, waiting for transfers between devices, trade(): return lax.ppermute(x, 'seq', pairs)  23.5 us
    pallas_call x4, Pallas kernels, absorb(): pl.pallas_call(functools.partial(absorb_kernel, reach, flips, blocks, not...  12.9 us
    pallas_call x1, Pallas kernels, front(): pl.pallas_call(front_kernel, out_shape=[jax.ShapeDtypeStruct((rows + CODE...  8.15 us
    ppermute x9, starting transfers between devices, trade(): return lax.ppermute(x, 'seq', pairs)  7.66 us
    pallas_call x1, Pallas kernels, lift(): pl.pallas_call(lift_kernel, out_shape=[jax.ShapeDtypeStruct(a.shape, a.dt...  4.61 us
    ppermute x1, starting transfers between devices, halo_rows(): from_outer = lax.ppermute(jnp.where(odd, last, initial), 'seq', outer)  1.91 us
    ppermute x1, starting transfers between devices, halo_rows(): from_inner = lax.ppermute(jnp.where(odd, initial, last), 'seq', inner)  1.69 us
  transfers between devices with their start and end apart: 11, of which 7 were waited for; matrix products, arithmetic and copies ran while one was open for 0% of the time, Pallas kernels for 22%

profile of v4, /device:TPU:20, one launch (start us, length us, event | category | flops | bytes accessed | tf_op | source)
XLA Modules:
  0.0 62.3 jit_solution(5204163261389969824)
XLA Ops:
  0.0 0.8 %broadcast_select_fusion = (bf16[8,1536]{1,0:T(8,128)(2,1)S(1)}, bf16[8,1536]{1,0:T(8,128)(2,1)S(1)}) fusion(pred[]{:T(512)S(6)} %eq.5, bf16[512,1536]{1,0:T(8,128)(2,1)} %x_hbm.1), kind=kLoop, calls=%fused_computation | loop fusion | flops 24576 | bytes 98305 | tf_op jit(solution)/shard_map/jit(_where)/select_n | solution.py:31
  0.8 1.9 %collective-permute-start.1 = (bf16[8,1536]{1,0:T(8,128)(2,1)S(1)}, bf16[8,1536]{1,0:T(8,128)(2,1)S(1)}, u32[]{:S(2)}, u32[]{:S(2)}) collective-permute-start(bf16[8,1536]{1,0:T(8,128)(2,1)S(1)} %get-tuple-element.85), channel_id=1, source_target_pairs={{1,2},{3,4},{5,6},{7,8},{9,10},{11,12},{13,14},{2,1},{4,3},{6,5},{... | collective-permute-start | bytes 73736 | tf_op jit(solution)/shard_map/ppermute | solution.py:31
  2.7 0.0 copy-start.1
  2.7 1.7 %collective-permute-start = (bf16[8,1536]{1,0:T(8,128)(2,1)S(1)}, bf16[8,1536]{1,0:T(8,128)(2,1)S(1)}, u32[]{:S(2)}, u32[]{:S(2)}) collective-permute-start(bf16[8,1536]{1,0:T(8,128)(2,1)S(1)} %get-tuple-element.86), channel_id=1, source_target_pairs={{0,1},{1,0},{2,3},{3,2},{4,5},{5,4},{6,7},{7,6},{8,9},{9,8},{10,11... | collective-permute-start | bytes 73736 | tf_op jit(solution)/shard_map/ppermute | solution.py:30
  4.4 4.6 %lift.1 = (bf16[512,1536]{1,0:T(8,128)(2,1)S(1)}, bf16[3,1536,768]{2,1,0:T(8,128)(2,1)S(1)}, bf16[768,1536]{1,0:T(8,128)(2,1)S(1)}, bf16[1536,128]{1,0:T(8,128)(...) custom-call(bf16[512,1536]{1,0:T(8,128)(2,1)} %x_hbm.1, ...), custom_call_target="tpu_custom_call" | custom-call | tf_op jit(solution)/shard_map/lift/pallas_call | solution.py:87
  9.0 0.0 collective-permute-done.1.outside_ref
  9.0 0.0 collective-permute-done.twin_ref
  9.0 0.0 copy-done.1
  9.0 0.0 copy-start
  9.0 8.2 %front.1 = (bf16[528,128]{1,0:T(8,128)(2,1)S(1)}, bf16[512,256]{1,0:T(8,128)(2,1)S(1)}) custom-call(bf16[512,1536]{1,0:T(8,128)(2,1)S(1)} %get-tuple-element.45.x_ref, bf16[3,1536,768]{2,1,0:T(8,128)(2,1)S(1)} %get-tuple-element.46.taps, bf16[768,1536]{1,0:T(8,128)(2,1)S(1)} %get-tuple-element.47.mix, bf16[1536,128]{1,0:T(8,128)(2,1)S(1)} %get-tuple-element.48.wq, ...), custom_call_target="tpu_custom_call" | custom-call | tf_op jit(solution)/shard_map/front/pallas_call | solution.py:177
  17.2 0.6 collective-permute-start.2
  17.8 0.0 collective-permute-start.6
  17.8 1.6 %collective-permute-start.5 = (bf16[512,256]{1,0:T(8,128)(2,1)S(1)}, bf16[512,256]{1,0:T(8,128)(2,1)S(1)}, u32[]{:S(2)}, u32[]{:S(2)}) collective-permute-start(bf16[512,256]{1,0:T(8,128)(2,1)S(1)} %get-tuple-element.53.refs_2_), channel_id=1, source_target_pairs={{0,4},{1,5},{2,6},{3,7},{4,0},{5,1},{6,2},{7,3},{8,12},{9,13},{10,... | collective-permute-start | bytes 786440 | tf_op jit(solution)/shard_map/ppermute | solution.py:494
  19.4 3.4 %collective-permute-done.2.refs_1_.refs_0_ = bf16[528,128]{1,0:T(8,128)(2,1)S(1)} collective-permute-done((bf16[528,128]{1,0:T(8,128)(2,1)S(1)}, bf16[528,128]{1,0:T(8,128)(2,1)S(1)}, u32[]{:S(2)}, u32[]{:S(2)}) %collective-permute-start.2) | collective-permute-done | bytes 135200 | tf_op jit(solution)/shard_map/ppermute | solution.py:494
  22.8 0.0 collective-permute-done.6.refs_3_
  22.8 0.0 copy-done
  22.8 2.9 %shard_map.82 = (f32[512,128]{1,0:T(8,128)S(1)}, f32[512,128]{1,0:T(8,128)S(1)}, f32[512,128]{1,0:T(8,128)S(1)}, f32[512,128]{1,0:T(8,128)S(1)}, f32[512,128]{1,0:T(8,128)S(1)}, /*index=5*/f32[512,128]{1,0:T(8,128)S(1)}) custom-call(s32[8,65]{1,0:T(8,128)S(1)} %pad_add_fusion.codes_ref, bf16[528,128]{1,0:T(8,128)(2,1)S(1)} %get-tuple-element.52.refs_0_, ...), custom_call_target="tpu_custom_call" | custom-call | flops 536870912 | bytes 4194304 | tf_op jit(solution)/shard_map/pallas_call | solution.py:440
  25.7 0.8 %collective-permute-done.5.refs_2_ = bf16[512,256]{1,0:T(8,128)(2,1)S(1)} collective-permute-done((bf16[512,256]{1,0:T(8,128)(2,1)S(1)}, bf16[512,256]{1,0:T(8,128)(2,1)S(1)}, u32[]{:S(2)}, u32[]{:S(2)}) %collective-permute-start.5) | collective-permute-done | bytes 262176 | tf_op jit(solution)/shard_map/ppermute | solution.py:494
  26.5 0.0 collective-permute-start.7
  26.5 0.3 collective-permute-start.4
  26.8 4.6 %collective-permute-start.3 = (bf16[512,256]{1,0:T(8,128)(2,1)S(1)}, bf16[512,256]{1,0:T(8,128)(2,1)S(1)}, u32[]{:S(2)}, u32[]{:S(2)}) collective-permute-start(bf16[512,256]{1,0:T(8,128)(2,1)S(1)} %get-tuple-element.53.refs_2_), channel_id=1, source_target_pairs={{4,8},{5,9},{6,10},{7,11},{8,4},{9,5},{10,6},{11,7},{20,24},{21,25... | collective-permute-start | bytes 786440 | tf_op jit(solution)/shard_map/ppermute | solution.py:494
  31.4 0.0 collective-permute-done.7.refs_3_
  31.5 2.9 %shard_map.83 = (f32[512,128]{1,0:T(8,128)S(1)}, f32[512,128]{1,0:T(8,128)S(1)}, f32[512,128]{1,0:T(8,128)S(1)}, f32[512,128]{1,0:T(8,128)S(1)}, f32[512,128]{1,0:T(8,128)S(1)}, /*index=5*/f32[512,128]{1,0:T(8,128)S(1)}) custom-call(s32[8,65]{1,0:T(8,128)S(1)} %pad_add_fusion.codes_ref, bf16[528,128]{1,0:T(8,128)(2,1)S(1)} %get-tuple-element.52.refs_0_, ...), custom_call_target="tpu_custom_call" | custom-call | flops 536870912 | bytes 4194304 | tf_op jit(solution)/shard_map/pallas_call | solution.py:440
  34.4 4.7 %collective-permute-done.4.refs_3_ = bf16[512,256]{1,0:T(8,128)(2,1)S(1)} collective-permute-done((bf16[512,256]{1,0:T(8,128)(2,1)S(1)}, bf16[512,256]{1,0:T(8,128)(2,1)S(1)}, u32[]{:S(2)}, u32[]{:S(2)}) %collective-permute-start.4) | collective-permute-done | bytes 262176 | tf_op jit(solution)/shard_map/ppermute | solution.py:494
  39.1 8.2 %collective-permute-done.3.refs_1_ = bf16[512,256]{1,0:T(8,128)(2,1)S(1)} collective-permute-done((bf16[512,256]{1,0:T(8,128)(2,1)S(1)}, bf16[512,256]{1,0:T(8,128)(2,1)S(1)}, u32[]{:S(2)}, u32[]{:S(2)}) %collective-permute-start.3) | collective-permute-done | bytes 262176 | tf_op jit(solution)/shard_map/ppermute | solution.py:494
  47.4 0.1 collective-permute-start.8
  47.4 0.4 collective-permute-start.9
  47.9 1.0 %collective-permute-done.8.refs_2_ = bf16[512,256]{1,0:T(8,128)(2,1)S(1)} collective-permute-done((bf16[512,256]{1,0:T(8,128)(2,1)S(1)}, bf16[512,256]{1,0:T(8,128)(2,1)S(1)}, u32[]{:S(2)}, u32[]{:S(2)}) %collective-permute-start.8) | collective-permute-done | bytes 262176 | tf_op jit(solution)/shard_map/ppermute | solution.py:494
  48.9 0.4 collective-permute-done.9.refs_4_
  49.3 3.6 %shard_map.85 = f32[520,128]{1,0:T(8,128)S(1)} custom-call(s32[8,65]{1,0:T(8,128)S(1)} %pad_add_fusion.codes_ref, bf16[528,128]{1,0:T(8,128)(2,1)S(1)} %collective-permute-done.2.refs_1_.refs_0_, bf16[512,256]{1,0:T(8,128)(2,1)S(1)} %collective-permute-done.3.refs_1_, bf16[512,256]{1,0:T(8,128)(2,1)S(1)} %collective-permute-done.8.refs_2_, ...), custom_call_target="tpu_custom_call" | custom-call | flops 536870912 | bytes 4194304 | tf_op jit(solution)/shard_map/pallas_call | solution.py:440
  52.8 0.1 collective-permute-start.10
  52.9 3.5 %shard_map.84 = (f32[512,128]{1,0:T(8,128)S(1)}, f32[512,128]{1,0:T(8,128)S(1)}, f32[512,128]{1,0:T(8,128)S(1)}) custom-call(s32[8,65]{1,0:T(8,128)S(1)} %pad_add_fusion.codes_ref, bf16[528,128]{1,0:T(8,128)(2,1)S(1)} %get-tuple-element.52.refs_0_, bf16[512,256]{1,0:T(8,128)(2,1)S(1)} %collective-permute-done.3.refs_1_, ...), custom_call_target="tpu_custom_call" | custom-call | flops 536870912 | bytes 4194304 | tf_op jit(solution)/shard_map/pallas_call | solution.py:440
  56.4 4.9 %collective-permute-done.10.pack_ref = f32[520,128]{1,0:T(8,128)S(1)} collective-permute-done((f32[520,128]{1,0:T(8,128)S(1)}, f32[520,128]{1,0:T(8,128)S(1)}, u32[]{:S(2)}, u32[]{:S(2)}) %collective-permute-start.10) | collective-permute-done | bytes 266272 | tf_op jit(solution)/shard_map/ppermute | solution.py:494
  61.3 1.0 %merge.1 = bf16[512,128]{1,0:T(8,128)(2,1)} custom-call(f32[512,128]{1,0:T(8,128)S(1)} %get-tuple-element.79.peak_ref, f32[512,128]{1,0:T(8,128)S(1)} %get-tuple-element.80.total_ref, f32[512,128]{1,0:T(8,128)S(1)} %get-tuple-element.81.acc_ref, f32[520,128]{1,0:T(8,128)S(1)} %collective-permute-done.10.pack_ref), custom_call_target="tpu_custom_call" | custom-call | tf_op jit(solution)/shard_map/merge/pallas_call | solution.py:529
  (2 shorter events, 0.0 us)
Async XLA Ops:
  0.8 8.2 %collective-permute-start.1 = (bf16[8,1536]{1,0:T(8,128)(2,1)S(1)}, bf16[8,1536]{1,0:T(8,128)(2,1)S(1)}, u32[]{:S(2)}, u32[]{:S(2)}) collective-permute-start(bf16[8,1536]{1,0:T(8,128)(2,1)S(1)} %get-tuple-element.85), channel_id=1, source_target_pairs={{1,2},{3,4},{5,6},{7,8},{9,10},{11,12},{13,14},{2,1},{4,3},{6,5},{... | collective-permute-start | bytes 73736 | tf_op jit(solution)/shard_map/ppermute | solution.py:31
  2.7 6.3 %copy-start.1 = (s32[4,65]{1,0:T(4,128)S(1)}, s32[4,65]{1,0:T(4,128)}, u32[]{:S(2)}) copy-start(s32[4,65]{1,0:T(4,128)} %codes_ref.1) | copy-start | bytes 3124
  2.7 6.3 %collective-permute-start = (bf16[8,1536]{1,0:T(8,128)(2,1)S(1)}, bf16[8,1536]{1,0:T(8,128)(2,1)S(1)}, u32[]{:S(2)}, u32[]{:S(2)}) collective-permute-start(bf16[8,1536]{1,0:T(8,128)(2,1)S(1)} %get-tuple-element.86), channel_id=1, source_target_pairs={{0,1},{1,0},{2,3},{3,2},{4,5},{5,4},{6,7},{7,6},{8,9},{9,8},{10,11... | collective-permute-start | bytes 73736 | tf_op jit(solution)/shard_map/ppermute | solution.py:30
  9.0 13.8 %copy-start = (s32[8192]{0:T(1024)S(1)}, s32[8192]{0:T(1024)}, u32[]{:S(2)}) copy-start(s32[8192]{0:T(1024)} %param.15) | copy-start | bytes 98308
  17.2 5.6 %collective-permute-start.2 = (bf16[528,128]{1,0:T(8,128)(2,1)S(1)}, bf16[528,128]{1,0:T(8,128)(2,1)S(1)}, u32[]{:S(2)}, u32[]{:S(2)}) collective-permute-start(bf16[528,128]{1,0:T(8,128)(2,1)S(1)} %get-tuple-element.52.refs_0_), channel_id=1, source_target_pairs={{0,2},{1,3},{2,0},{3,1},{4,6},{5,7},{6,4},{7,5},{8,10},{9,11},{10,... | collective-permute-start | bytes 405512 | tf_op jit(solution)/shard_map/ppermute | solution.py:494
  17.8 5.0 %collective-permute-start.6 = (bf16[512,256]{1,0:T(8,128)(2,1)S(1)}, bf16[512,256]{1,0:T(8,128)(2,1)S(1)}, u32[]{:S(2)}, u32[]{:S(2)}) collective-permute-start(bf16[512,256]{1,0:T(8,128)(2,1)S(1)} %get-tuple-element.53.refs_2_), channel_id=1, source_target_pairs={{0,1},{1,0},{2,3},{3,2},{4,5},{5,4},{6,7},{7,6},{8,9},{9,8},{10,11... | collective-permute-start | bytes 786440 | tf_op jit(solution)/shard_map/ppermute | solution.py:494
  17.8 8.7 %collective-permute-start.5 = (bf16[512,256]{1,0:T(8,128)(2,1)S(1)}, bf16[512,256]{1,0:T(8,128)(2,1)S(1)}, u32[]{:S(2)}, u32[]{:S(2)}) collective-permute-start(bf16[512,256]{1,0:T(8,128)(2,1)S(1)} %get-tuple-element.53.refs_2_), channel_id=1, source_target_pairs={{0,4},{1,5},{2,6},{3,7},{4,0},{5,1},{6,2},{7,3},{8,12},{9,13},{10,... | collective-permute-start | bytes 786440 | tf_op jit(solution)/shard_map/ppermute | solution.py:494
  26.5 4.9 %collective-permute-start.7 = (bf16[512,256]{1,0:T(8,128)(2,1)S(1)}, bf16[512,256]{1,0:T(8,128)(2,1)S(1)}, u32[]{:S(2)}, u32[]{:S(2)}) collective-permute-start(bf16[512,256]{1,0:T(8,128)(2,1)S(1)} %collective-permute-done.5.refs_2_), channel_id=1, source_target_pairs={{0,1},{1,0},{2,3},{3,2},{4,5},{5,4},{6,7},{7,6},{8,9},{9,8},{10,11... | collective-permute-start | bytes 786440 | tf_op jit(solution)/shard_map/ppermute | solution.py:494
  26.5 12.6 %collective-permute-start.4 = (bf16[512,256]{1,0:T(8,128)(2,1)S(1)}, bf16[512,256]{1,0:T(8,128)(2,1)S(1)}, u32[]{:S(2)}, u32[]{:S(2)}) collective-permute-start(bf16[512,256]{1,0:T(8,128)(2,1)S(1)} %get-tuple-element.53.refs_2_), channel_id=1, source_target_pairs={{0,8},{1,9},{2,10},{3,11},{4,12},{5,13},{6,14},{7,15},{8,0},{9,1},... | collective-permute-start | bytes 786440 | tf_op jit(solution)/shard_map/ppermute | solution.py:494
  26.8 20.5 %collective-permute-start.3 = (bf16[512,256]{1,0:T(8,128)(2,1)S(1)}, bf16[512,256]{1,0:T(8,128)(2,1)S(1)}, u32[]{:S(2)}, u32[]{:S(2)}) collective-permute-start(bf16[512,256]{1,0:T(8,128)(2,1)S(1)} %get-tuple-element.53.refs_2_), channel_id=1, source_target_pairs={{4,8},{5,9},{6,10},{7,11},{8,4},{9,5},{10,6},{11,7},{20,24},{21,25... | collective-permute-start | bytes 786440 | tf_op jit(solution)/shard_map/ppermute | solution.py:494
  47.4 1.5 %collective-permute-start.8 = (bf16[512,256]{1,0:T(8,128)(2,1)S(1)}, bf16[512,256]{1,0:T(8,128)(2,1)S(1)}, u32[]{:S(2)}, u32[]{:S(2)}) collective-permute-start(bf16[512,256]{1,0:T(8,128)(2,1)S(1)} %collective-permute-done.3.refs_1_), channel_id=1, source_target_pairs={{0,1},{1,0},{2,3},{3,2},{4,5},{5,4},{6,7},{7,6},{8,9},{9,8},{10,11... | collective-permute-start | bytes 786440 | tf_op jit(solution)/shard_map/ppermute | solution.py:494
  47.4 1.8 %collective-permute-start.9 = (bf16[512,256]{1,0:T(8,128)(2,1)S(1)}, bf16[512,256]{1,0:T(8,128)(2,1)S(1)}, u32[]{:S(2)}, u32[]{:S(2)}) collective-permute-start(bf16[512,256]{1,0:T(8,128)(2,1)S(1)} %collective-permute-done.4.refs_3_), channel_id=1, source_target_pairs={{0,1},{1,0},{2,3},{3,2},{4,5},{5,4},{6,7},{7,6},{8,9},{9,8},{10,11... | collective-permute-start | bytes 786440 | tf_op jit(solution)/shard_map/ppermute | solution.py:494
  52.8 8.5 %collective-permute-start.10 = (f32[520,128]{1,0:T(8,128)S(1)}, f32[520,128]{1,0:T(8,128)S(1)}, u32[]{:S(2)}, u32[]{:S(2)}) collective-permute-start(f32[520,128]{1,0:T(8,128)S(1)} %shard_map.85), channel_id=1, source_target_pairs={{0,2},{1,3},{2,0},{3,1},{4,6},{5,7},{6,4},{7,5},{8,10},{9,11},{10,... | collective-permute-start | bytes 798728 | tf_op jit(solution)/shard_map/ppermute | solution.py:494

commit v5 on v4

--- a/solution.py
+++ b/solution.py
@@ -403,7 +403,7 @@
         each(weigh)
 
         if pack:
-            out_refs[0][0:rows, :] = acc[...]
+            out_refs[0][0:rows, :] = acc[...].astype(jnp.bfloat16)
             sums = jnp.broadcast_to(jnp.sum(total[...], axis=1, keepdims=True), total.shape)
             eye = on_diagonal(tile)
             lines = []
@@ -411,7 +411,14 @@
                 for qt in range(tiles_per_block):
                     part = column[qt * tile : (qt + 1) * tile, :]
                     lines.append(jnp.sum(jnp.where(eye, part, 0.0), axis=0, keepdims=True))
-            out_refs[0][rows:, :] = jnp.concatenate(lines, axis=0)
+            exact = jnp.concatenate(lines, axis=0)
+            pieces = []
+            for _ in range(3):
+                piece = exact.astype(jnp.bfloat16).astype(jnp.float32)
+                exact = exact - piece
+                pieces.append(piece)
+            pieces.append(jnp.zeros_like(exact))
+            out_refs[0][rows:, :] = jnp.concatenate(pieces, axis=0).astype(jnp.bfloat16)
         else:
             out_refs[3 * s][...] = peak[...]
             out_refs[3 * s + 1][...] = total[...]
@@ -433,7 +440,7 @@
     smem = pl.BlockSpec(memory_space=pltpu.SMEM)
     column = jax.ShapeDtypeStruct((rows, tile), jnp.float32)
     if pack:
-        out_shape = [jax.ShapeDtypeStruct((rows + 2 * (rows // tile), head_dim), jnp.float32)]
+        out_shape = [jax.ShapeDtypeStruct((rows + 8 * (rows // tile), head_dim), jnp.bfloat16)]
     else:
         out_shape = [column, column, column] * len(flips)
     units = len(flips) * n
@@ -462,11 +469,14 @@
     tile = peak_ref.shape[1]
     eye = on_diagonal(tile)
     count = rows // tile
+    pieces = pack_ref[rows:, :].astype(jnp.float32)
+    lines = 2 * count
+    exact = pieces[:lines] + pieces[lines : 2 * lines] + pieces[2 * lines : 3 * lines]
     for qt in range(count):
         span = slice(qt * tile, (qt + 1) * tile)
 
         def column(line):
-            row = pack_ref[rows + line : rows + line + 1, :]
+            row = exact[line : line + 1, :]
             return jnp.sum(jnp.where(eye, row, 0.0), axis=1, keepdims=True)
 
         peak_a = peak_ref[span, :]
@@ -478,7 +488,7 @@
         scale_b = jnp.exp2(peak_b - top)
         whole = total_a * scale_a + total_b * scale_b
         out_ref[span, :] = (
-            (acc_ref[span, :] * scale_a + pack_ref[span, :] * scale_b) / whole
+            (acc_ref[span, :] * scale_a + pack_ref[span, :].astype(jnp.float32) * scale_b) / whole
         ).astype(out_ref.dtype)
 
 
@@ -504,24 +514,24 @@
     state = absorb(
         reach, codes, [queries, peer_queries], [keyval, twin], *common, (0, half), (0, 1), [], False
     )
-    near, state = lax.optimization_barrier((near, state))
+    near, middle, state = lax.optimization_barrier((near, middle, state))
     near_twin = trade(near, 1)
+    middle_twin = trade(middle, 1)
     state = absorb(
         reach,
         codes,
         [queries, peer_queries],
-        [near, near_twin],
+        [near, near_twin, middle, middle_twin],
         *common,
         (0, half),
-        (z, z + 1),
+        (z, z + 1, 3 * z, 3 * z + 1),
         state,
         False,
     )
-    middle, far, state = lax.optimization_barrier((middle, far, state))
-    middle_twin = trade(middle, 1)
+    far, state = lax.optimization_barrier((far, state))
     far_twin = trade(far, 1)
-    away = [middle, middle_twin, far, far_twin]
-    leaps = (3 * z, 3 * z + 1, 2 * z, 2 * z + 1)
+    away = [far, far_twin]
+    leaps = (2 * z, 2 * z + 1)
     (pack,) = absorb(reach, codes, [peer_queries], away, *common, (half,), leaps, state[3:], True)
     other = trade(pack, half)
     peak, total, acc = absorb(reach, codes, [queries], away, *common, (0,), leaps, state[:3], False)

time: 62.5 us -> 58.1 us (0.930)
  the two profiles are of different devices: /device:TPU:20 before, /device:TPU:0 now
where the time goes in v5:
time: 58.1 us; the launch traced here: 58 us
  Pallas kernels  23.3 us (40%)
  waiting for transfers between devices  19.7 us (34%)
  starting transfers between devices  14 us (24%)
  other arithmetic  0.78 us (1%)
    ppermute x9, waiting for transfers between devices, trade(): return lax.ppermute(x, 'seq', pairs)  19.7 us
    pallas_call x4, Pallas kernels, absorb(): pl.pallas_call(functools.partial(absorb_kernel, reach, flips, blocks, not...  9.58 us
    ppermute x9, starting transfers between devices, trade(): return lax.ppermute(x, 'seq', pairs)  8.91 us
    pallas_call x1, Pallas kernels, front(): pl.pallas_call(front_kernel, out_shape=[jax.ShapeDtypeStruct((rows + CODE...  8.15 us
    pallas_call x1, Pallas kernels, lift(): pl.pallas_call(lift_kernel, out_shape=[jax.ShapeDtypeStruct(a.shape, a.dt...  4.61 us
    ppermute x1, starting transfers between devices, halo_rows(): from_inner = lax.ppermute(jnp.where(odd, initial, last), 'seq', inner)  4.42 us
  transfers between devices with their start and end apart: 11, of which 4 were waited for; matrix products, arithmetic and copies ran while one was open for 0% of the time, Pallas kernels for 20%

profile of v5, /device:TPU:0, one launch (start us, length us, event | category | flops | bytes accessed | tf_op | source)
XLA Modules:
  0.0 58.0 jit_solution(11341018938623256258)
XLA Ops:
  0.0 0.8 %broadcast_select_fusion = (bf16[8,1536]{1,0:T(8,128)(2,1)S(1)}, bf16[8,1536]{1,0:T(8,128)(2,1)S(1)}) fusion(pred[]{:T(512)S(6)} %eq.5, bf16[512,1536]{1,0:T(8,128)(2,1)} %x_hbm.1), kind=kLoop, calls=%fused_computation | loop fusion | flops 24576 | bytes 98305 | tf_op jit(solution)/shard_map/jit(_where)/select_n | solution.py:31
  0.8 0.7 %collective-permute-start.1 = (bf16[8,1536]{1,0:T(8,128)(2,1)S(1)}, bf16[8,1536]{1,0:T(8,128)(2,1)S(1)}, u32[]{:S(2)}, u32[]{:S(2)}) collective-permute-start(bf16[8,1536]{1,0:T(8,128)(2,1)S(1)} %get-tuple-element.85), channel_id=1, source_target_pairs={{1,2},{3,4},{5,6},{7,8},{9,10},{11,12},{13,14},{2,1},{4,3},{6,5},{... | collective-permute-start | bytes 73736 | tf_op jit(solution)/shard_map/ppermute | solution.py:31
  1.4 0.0 copy-start.1
  1.4 4.4 %collective-permute-start = (bf16[8,1536]{1,0:T(8,128)(2,1)S(1)}, bf16[8,1536]{1,0:T(8,128)(2,1)S(1)}, u32[]{:S(2)}, u32[]{:S(2)}) collective-permute-start(bf16[8,1536]{1,0:T(8,128)(2,1)S(1)} %get-tuple-element.86), channel_id=1, source_target_pairs={{0,1},{1,0},{2,3},{3,2},{4,5},{5,4},{6,7},{7,6},{8,9},{9,8},{10,11... | collective-permute-start | bytes 73736 | tf_op jit(solution)/shard_map/ppermute | solution.py:30
  5.9 4.6 %lift.1 = (bf16[512,1536]{1,0:T(8,128)(2,1)S(1)}, bf16[3,1536,768]{2,1,0:T(8,128)(2,1)S(1)}, bf16[768,1536]{1,0:T(8,128)(2,1)S(1)}, bf16[1536,128]{1,0:T(8,128)(...) custom-call(bf16[512,1536]{1,0:T(8,128)(2,1)} %x_hbm.1, ...), custom_call_target="tpu_custom_call" | custom-call | tf_op jit(solution)/shard_map/lift/pallas_call | solution.py:87
  10.5 0.0 collective-permute-done.1.outside_ref
  10.5 0.0 collective-permute-done.twin_ref
  10.5 0.0 copy-done.1
  10.5 0.0 copy-start
  10.5 8.1 %front.1 = (bf16[528,128]{1,0:T(8,128)(2,1)S(1)}, bf16[512,256]{1,0:T(8,128)(2,1)S(1)}) custom-call(bf16[512,1536]{1,0:T(8,128)(2,1)S(1)} %get-tuple-element.45.x_ref, bf16[3,1536,768]{2,1,0:T(8,128)(2,1)S(1)} %get-tuple-element.46.taps, bf16[768,1536]{1,0:T(8,128)(2,1)S(1)} %get-tuple-element.47.mix, bf16[1536,128]{1,0:T(8,128)(2,1)S(1)} %get-tuple-element.48.wq, ...), custom_call_target="tpu_custom_call" | custom-call | tf_op jit(solution)/shard_map/front/pallas_call | solution.py:177
  18.7 1.6 %collective-permute-start.2 = (bf16[528,128]{1,0:T(8,128)(2,1)S(1)}, bf16[528,128]{1,0:T(8,128)(2,1)S(1)}, u32[]{:S(2)}, u32[]{:S(2)}) collective-permute-start(bf16[528,128]{1,0:T(8,128)(2,1)S(1)} %get-tuple-element.52.refs_0_), channel_id=1, source_target_pairs={{0,2},{1,3},{2,0},{3,1},{4,6},{5,7},{6,4},{7,5},{8,10},{9,11},{10,... | collective-permute-start | bytes 405512 | tf_op jit(solution)/shard_map/ppermute | solution.py:504
  20.3 0.0 collective-permute-start.6
  20.3 0.7 %collective-permute-start.5 = (bf16[512,256]{1,0:T(8,128)(2,1)S(1)}, bf16[512,256]{1,0:T(8,128)(2,1)S(1)}, u32[]{:S(2)}, u32[]{:S(2)}) collective-permute-start(bf16[512,256]{1,0:T(8,128)(2,1)S(1)} %get-tuple-element.53.refs_2_), channel_id=1, source_target_pairs={{4,8},{5,9},{6,10},{7,11},{8,4},{9,5},{10,6},{11,7},{20,24},{21,25... | collective-permute-start | bytes 786440 | tf_op jit(solution)/shard_map/ppermute | solution.py:504
  20.9 4.5 %collective-permute-start.4 = (bf16[512,256]{1,0:T(8,128)(2,1)S(1)}, bf16[512,256]{1,0:T(8,128)(2,1)S(1)}, u32[]{:S(2)}, u32[]{:S(2)}) collective-permute-start(bf16[512,256]{1,0:T(8,128)(2,1)S(1)} %get-tuple-element.53.refs_2_), channel_id=1, source_target_pairs={{0,4},{1,5},{2,6},{3,7},{4,0},{5,1},{6,2},{7,3},{8,12},{9,13},{10,... | collective-permute-start | bytes 786440 | tf_op jit(solution)/shard_map/ppermute | solution.py:504
  25.4 0.0 collective-permute-done.2.refs_1_.refs_0_
  25.4 0.0 collective-permute-done.6.refs_3_
  25.4 0.0 copy-done
  25.4 2.9 %shard_map.82 = (f32[512,128]{1,0:T(8,128)S(1)}, f32[512,128]{1,0:T(8,128)S(1)}, f32[512,128]{1,0:T(8,128)S(1)}, f32[512,128]{1,0:T(8,128)S(1)}, f32[512,128]{1,0:T(8,128)S(1)}, /*index=5*/f32[512,128]{1,0:T(8,128)S(1)}) custom-call(s32[8,65]{1,0:T(8,128)S(1)} %pad_add_fusion.codes_ref, bf16[528,128]{1,0:T(8,128)(2,1)S(1)} %get-tuple-element.52.refs_0_, ...), custom_call_target="tpu_custom_call" | custom-call | flops 536870912 | bytes 4194304 | tf_op jit(solution)/shard_map/pallas_call | solution.py:447
  28.3 0.0 collective-permute-done.5.refs_4_
  28.3 3.7 %collective-permute-done.4.refs_2_ = bf16[512,256]{1,0:T(8,128)(2,1)S(1)} collective-permute-done((bf16[512,256]{1,0:T(8,128)(2,1)S(1)}, bf16[512,256]{1,0:T(8,128)(2,1)S(1)}, u32[]{:S(2)}, u32[]{:S(2)}) %collective-permute-start.4) | collective-permute-done | bytes 262176 | tf_op jit(solution)/shard_map/ppermute | solution.py:504
  32.1 0.0 collective-permute-start.7
  32.1 0.5 collective-permute-start.8
  32.6 1.6 %collective-permute-start.3 = (bf16[512,256]{1,0:T(8,128)(2,1)S(1)}, bf16[512,256]{1,0:T(8,128)(2,1)S(1)}, u32[]{:S(2)}, u32[]{:S(2)}) collective-permute-start(bf16[512,256]{1,0:T(8,128)(2,1)S(1)} %get-tuple-element.53.refs_2_), channel_id=1, source_target_pairs={{0,8},{1,9},{2,10},{3,11},{4,12},{5,13},{6,14},{7,15},{8,0},{9,1},... | collective-permute-start | bytes 786440 | tf_op jit(solution)/shard_map/ppermute | solution.py:504
  34.2 0.0 collective-permute-done.7.refs_3_
  34.2 0.0 collective-permute-done.8.refs_5_
  34.2 2.7 %shard_map.83 = (f32[512,128]{1,0:T(8,128)S(1)}, f32[512,128]{1,0:T(8,128)S(1)}, f32[512,128]{1,0:T(8,128)S(1)}, f32[512,128]{1,0:T(8,128)S(1)}, f32[512,128]{1,0:T(8,128)S(1)}, /*index=5*/f32[512,128]{1,0:T(8,128)S(1)}) custom-call(s32[8,65]{1,0:T(8,128)S(1)} %pad_add_fusion.codes_ref, bf16[528,128]{1,0:T(8,128)(2,1)S(1)} %get-tuple-element.52.refs_0_, ...), custom_call_target="tpu_custom_call" | custom-call | flops 1073741824 | bytes 8388608 | tf_op jit(solution)/shard_map/pallas_call | solution.py:447
  37.0 10.4 %collective-permute-done.3.refs_1_ = bf16[512,256]{1,0:T(8,128)(2,1)S(1)} collective-permute-done((bf16[512,256]{1,0:T(8,128)(2,1)S(1)}, bf16[512,256]{1,0:T(8,128)(2,1)S(1)}, u32[]{:S(2)}, u32[]{:S(2)}) %collective-permute-start.3) | collective-permute-done | bytes 262176 | tf_op jit(solution)/shard_map/ppermute | solution.py:504
  47.3 0.0 collective-permute-start.9
  47.3 1.5 %collective-permute-done.9.refs_2_ = bf16[512,256]{1,0:T(8,128)(2,1)S(1)} collective-permute-done((bf16[512,256]{1,0:T(8,128)(2,1)S(1)}, bf16[512,256]{1,0:T(8,128)(2,1)S(1)}, u32[]{:S(2)}, u32[]{:S(2)}) %collective-permute-start.9) | collective-permute-done | bytes 262176 | tf_op jit(solution)/shard_map/ppermute | solution.py:504
  48.9 2.3 %shard_map.85 = bf16[544,128]{1,0:T(8,128)(2,1)S(1)} custom-call(s32[8,65]{1,0:T(8,128)S(1)} %pad_add_fusion.codes_ref, bf16[528,128]{1,0:T(8,128)(2,1)S(1)} %collective-permute-done.2.refs_1_.refs_0_, bf16[512,256]{1,0:T(8,128)(2,1)S(1)} %collective-permute-done.3.refs_1_, bf16[512,256]{1,0:T(8,128)(2,1)S(1)} %collective-permute-done.9.refs_2_, ...), custom_call_target="tpu_custom_call" | custom-call | flops 268435456 | bytes 2097152 | tf_op jit(solution)/shard_map/pallas_call | solution.py:447
  51.2 0.1 collective-permute-start.10
  51.3 1.6 %shard_map.84 = (f32[512,128]{1,0:T(8,128)S(1)}, f32[512,128]{1,0:T(8,128)S(1)}, f32[512,128]{1,0:T(8,128)S(1)}) custom-call(s32[8,65]{1,0:T(8,128)S(1)} %pad_add_fusion.codes_ref, bf16[528,128]{1,0:T(8,128)(2,1)S(1)} %get-tuple-element.52.refs_0_, bf16[512,256]{1,0:T(8,128)(2,1)S(1)} %collective-permute-done.3.refs_1_, ...), custom_call_target="tpu_custom_call" | custom-call | flops 268435456 | bytes 2097152 | tf_op jit(solution)/shard_map/pallas_call | solution.py:447
  52.9 4.1 %collective-permute-done.10.pack_ref = bf16[544,128]{1,0:T(8,128)(2,1)S(1)} collective-permute-done((bf16[544,128]{1,0:T(8,128)(2,1)S(1)}, bf16[544,128]{1,0:T(8,128)(2,1)S(1)}, u32[]{:S(2)}, u32[]{:S(2)}) %collective-permute-start.10) | collective-permute-done | bytes 139296 | tf_op jit(solution)/shard_map/ppermute | solution.py:504
  57.0 0.9 %merge.1 = bf16[512,128]{1,0:T(8,128)(2,1)} custom-call(f32[512,128]{1,0:T(8,128)S(1)} %get-tuple-element.79.peak_ref, f32[512,128]{1,0:T(8,128)S(1)} %get-tuple-element.80.total_ref, f32[512,128]{1,0:T(8,128)S(1)} %get-tuple-element.81.acc_ref, bf16[544,128]{1,0:T(8,128)(2,1)S(1)} %collective-permute-done.10.pack_ref), custom_call_target="tpu_custom_call" | custom-call | tf_op jit(solution)/shard_map/merge/pallas_call | solution.py:539
  (2 shorter events, 0.0 us)
Async XLA Ops:
  0.8 9.7 %collective-permute-start.1 = (bf16[8,1536]{1,0:T(8,128)(2,1)S(1)}, bf16[8,1536]{1,0:T(8,128)(2,1)S(1)}, u32[]{:S(2)}, u32[]{:S(2)}) collective-permute-start(bf16[8,1536]{1,0:T(8,128)(2,1)S(1)} %get-tuple-element.85), channel_id=1, source_target_pairs={{1,2},{3,4},{5,6},{7,8},{9,10},{11,12},{13,14},{2,1},{4,3},{6,5},{... | collective-permute-start | bytes 73736 | tf_op jit(solution)/shard_map/ppermute | solution.py:31
  1.4 9.1 %copy-start.1 = (s32[4,65]{1,0:T(4,128)S(1)}, s32[4,65]{1,0:T(4,128)}, u32[]{:S(2)}) copy-start(s32[4,65]{1,0:T(4,128)} %codes_ref.1) | copy-start | bytes 3124
  1.4 9.1 %collective-permute-start = (bf16[8,1536]{1,0:T(8,128)(2,1)S(1)}, bf16[8,1536]{1,0:T(8,128)(2,1)S(1)}, u32[]{:S(2)}, u32[]{:S(2)}) collective-permute-start(bf16[8,1536]{1,0:T(8,128)(2,1)S(1)} %get-tuple-element.86), channel_id=1, source_target_pairs={{0,1},{1,0},{2,3},{3,2},{4,5},{5,4},{6,7},{7,6},{8,9},{9,8},{10,11... | collective-permute-start | bytes 73736 | tf_op jit(solution)/shard_map/ppermute | solution.py:30
  10.5 14.9 %copy-start = (s32[8192]{0:T(1024)S(1)}, s32[8192]{0:T(1024)}, u32[]{:S(2)}) copy-start(s32[8192]{0:T(1024)} %param.15) | copy-start | bytes 98308
  18.7 6.7 %collective-permute-start.2 = (bf16[528,128]{1,0:T(8,128)(2,1)S(1)}, bf16[528,128]{1,0:T(8,128)(2,1)S(1)}, u32[]{:S(2)}, u32[]{:S(2)}) collective-permute-start(bf16[528,128]{1,0:T(8,128)(2,1)S(1)} %get-tuple-element.52.refs_0_), channel_id=1, source_target_pairs={{0,2},{1,3},{2,0},{3,1},{4,6},{5,7},{6,4},{7,5},{8,10},{9,11},{10,... | collective-permute-start | bytes 405512 | tf_op jit(solution)/shard_map/ppermute | solution.py:504
  20.3 5.2 %collective-permute-start.6 = (bf16[512,256]{1,0:T(8,128)(2,1)S(1)}, bf16[512,256]{1,0:T(8,128)(2,1)S(1)}, u32[]{:S(2)}, u32[]{:S(2)}) collective-permute-start(bf16[512,256]{1,0:T(8,128)(2,1)S(1)} %get-tuple-element.53.refs_2_), channel_id=1, source_target_pairs={{0,1},{1,0},{2,3},{3,2},{4,5},{5,4},{6,7},{7,6},{8,9},{9,8},{10,11... | collective-permute-start | bytes 786440 | tf_op jit(solution)/shard_map/ppermute | solution.py:504
  20.3 8.1 %collective-permute-start.5 = (bf16[512,256]{1,0:T(8,128)(2,1)S(1)}, bf16[512,256]{1,0:T(8,128)(2,1)S(1)}, u32[]{:S(2)}, u32[]{:S(2)}) collective-permute-start(bf16[512,256]{1,0:T(8,128)(2,1)S(1)} %get-tuple-element.53.refs_2_), channel_id=1, source_target_pairs={{4,8},{5,9},{6,10},{7,11},{8,4},{9,5},{10,6},{11,7},{20,24},{21,25... | collective-permute-start | bytes 786440 | tf_op jit(solution)/shard_map/ppermute | solution.py:504
  20.9 11.2 %collective-permute-start.4 = (bf16[512,256]{1,0:T(8,128)(2,1)S(1)}, bf16[512,256]{1,0:T(8,128)(2,1)S(1)}, u32[]{:S(2)}, u32[]{:S(2)}) collective-permute-start(bf16[512,256]{1,0:T(8,128)(2,1)S(1)} %get-tuple-element.53.refs_2_), channel_id=1, source_target_pairs={{0,4},{1,5},{2,6},{3,7},{4,0},{5,1},{6,2},{7,3},{8,12},{9,13},{10,... | collective-permute-start | bytes 786440 | tf_op jit(solution)/shard_map/ppermute | solution.py:504
  32.1 2.1 %collective-permute-start.7 = (bf16[512,256]{1,0:T(8,128)(2,1)S(1)}, bf16[512,256]{1,0:T(8,128)(2,1)S(1)}, u32[]{:S(2)}, u32[]{:S(2)}) collective-permute-start(bf16[512,256]{1,0:T(8,128)(2,1)S(1)} %collective-permute-done.4.refs_2_), channel_id=1, source_target_pairs={{0,1},{1,0},{2,3},{3,2},{4,5},{5,4},{6,7},{7,6},{8,9},{9,8},{10,11... | collective-permute-start | bytes 786440 | tf_op jit(solution)/shard_map/ppermute | solution.py:504
  32.1 2.1 %collective-permute-start.8 = (bf16[512,256]{1,0:T(8,128)(2,1)S(1)}, bf16[512,256]{1,0:T(8,128)(2,1)S(1)}, u32[]{:S(2)}, u32[]{:S(2)}) collective-permute-start(bf16[512,256]{1,0:T(8,128)(2,1)S(1)} %collective-permute-done.5.refs_4_), channel_id=1, source_target_pairs={{0,1},{1,0},{2,3},{3,2},{4,5},{5,4},{6,7},{7,6},{8,9},{9,8},{10,11... | collective-permute-start | bytes 786440 | tf_op jit(solution)/shard_map/ppermute | solution.py:504
  32.6 14.7 %collective-permute-start.3 = (bf16[512,256]{1,0:T(8,128)(2,1)S(1)}, bf16[512,256]{1,0:T(8,128)(2,1)S(1)}, u32[]{:S(2)}, u32[]{:S(2)}) collective-permute-start(bf16[512,256]{1,0:T(8,128)(2,1)S(1)} %get-tuple-element.53.refs_2_), channel_id=1, source_target_pairs={{0,8},{1,9},{2,10},{3,11},{4,12},{5,13},{6,14},{7,15},{8,0},{9,1},... | collective-permute-start | bytes 786440 | tf_op jit(solution)/shard_map/ppermute | solution.py:504
  47.3 1.5 %collective-permute-start.9 = (bf16[512,256]{1,0:T(8,128)(2,1)S(1)}, bf16[512,256]{1,0:T(8,128)(2,1)S(1)}, u32[]{:S(2)}, u32[]{:S(2)}) collective-permute-start(bf16[512,256]{1,0:T(8,128)(2,1)S(1)} %collective-permute-done.3.refs_1_), channel_id=1, source_target_pairs={{0,1},{1,0},{2,3},{3,2},{4,5},{5,4},{6,7},{7,6},{8,9},{9,8},{10,11... | collective-permute-start | bytes 786440 | tf_op jit(solution)/shard_map/ppermute | solution.py:504
  51.2 5.8 %collective-permute-start.10 = (bf16[544,128]{1,0:T(8,128)(2,1)S(1)}, bf16[544,128]{1,0:T(8,128)(2,1)S(1)}, u32[]{:S(2)}, u32[]{:S(2)}) collective-permute-start(bf16[544,128]{1,0:T(8,128)(2,1)S(1)} %shard_map.85), channel_id=1, source_target_pairs={{0,2},{1,3},{2,0},{3,1},{4,6},{5,7},{6,4},{7,5},{8,10},{9,11},{10,... | collective-permute-start | bytes 417800 | tf_op jit(solution)/shard_map/ppermute | solution.py:504

commit v6 on v5

--- a/solution.py
+++ b/solution.py
@@ -135,35 +135,51 @@
     outer[rows : rows + 2 * d, :] = jnp.concatenate([last, after], axis=0).astype(jnp.bfloat16)
 
     wide = 256
+    taps_rows, mix_rows, out_rows = rows // 2, rows // 1, rows // 1
     for n in range(hidden // wide):
         cols = slice(n * wide, (n + 1) * wide)
-        conv = jnp.dot(outer[0:rows, :], taps[0, :, cols], preferred_element_type=jnp.float32)
-        conv += jnp.dot(inner[...], taps[1, :, cols], preferred_element_type=jnp.float32)
-        conv += jnp.dot(
-            outer[2 * d : rows + 2 * d, :], taps[2, :, cols], preferred_element_type=jnp.float32
-        )
-        squeezed[:, cols] = gelu(conv).astype(jnp.bfloat16)
-
-    square = jnp.zeros((rows, 128), jnp.float32)
+        for r in range(0, rows, taps_rows):
+            conv = jnp.dot(
+                outer[r : r + taps_rows, :], taps[0, :, cols], preferred_element_type=jnp.float32
+            )
+            conv += jnp.dot(
+                inner[r : r + taps_rows, :], taps[1, :, cols], preferred_element_type=jnp.float32
+            )
+            conv += jnp.dot(
+                outer[r + 2 * d : r + 2 * d + taps_rows, :],
+                taps[2, :, cols],
+                preferred_element_type=jnp.float32,
+            )
+            squeezed[r : r + taps_rows, cols] = gelu(conv).astype(jnp.bfloat16)
+
+    squares = [jnp.zeros((mix_rows, 128), jnp.float32) for _ in range(rows // mix_rows)]
     for n in range(channels // wide):
         cols = slice(n * wide, (n + 1) * wide)
-        part = x_ref[:, cols].astype(jnp.float32) + jnp.dot(
-            squeezed[...], mix[:, cols], preferred_element_type=jnp.float32
-        )
-        mixed[:, cols] = part
-        for k in range(wide // 128):
-            piece = part[:, k * 128 : (k + 1) * 128]
-            square += piece * piece
-    gain = lax.rsqrt(jnp.sum(square, axis=1, keepdims=True) / channels + norm_eps)
-    normed = (mixed[...] * gain).astype(jnp.bfloat16)
-    q_ref[0:rows, :] = jnp.dot(normed, wq[...], preferred_element_type=jnp.float32).astype(
-        jnp.bfloat16
+        for i in range(rows // mix_rows):
+            span = slice(i * mix_rows, (i + 1) * mix_rows)
+            part = x_ref[span, cols].astype(jnp.float32) + jnp.dot(
+                squeezed[span, :], mix[:, cols], preferred_element_type=jnp.float32
+            )
+            mixed[span, cols] = part
+            for k in range(wide // 128):
+                piece = part[:, k * 128 : (k + 1) * 128]
+                squares[i] += piece * piece
+    gain = lax.rsqrt(
+        jnp.sum(jnp.concatenate(squares, axis=0), axis=1, keepdims=True) / channels + norm_eps
     )
+    for r in range(0, rows, out_rows):
+        span = slice(r, r + out_rows)
+        normed = (mixed[span, :] * gain[span]).astype(jnp.bfloat16)
+        q_ref[span, :] = jnp.dot(normed, wq[...], preferred_element_type=jnp.float32).astype(
+            jnp.bfloat16
+        )
+        kv_ref[span, :] = jnp.dot(normed, wkv[...], preferred_element_type=jnp.float32).astype(
+            jnp.bfloat16
+        )
     q_ref[rows:, :] = jnp.zeros((q_ref.shape[0] - rows, q_ref.shape[1]), jnp.bfloat16)
     q_ref[rows : rows + codes_ref.shape[0], 0 : codes_ref.shape[1]] = (
         codes_ref[...].astype(jnp.float32).astype(jnp.bfloat16)
     )
-    kv_ref[...] = jnp.dot(normed, wkv[...], preferred_element_type=jnp.float32).astype(jnp.bfloat16)
 
 
 CODE_ROWS = 16

time: 58.1 us -> 55.8 us (0.960)
  Pallas kernels: 23.3 us -> 21 us
    pallas_call x1, Pallas kernels: 8.15 us -> 6.02 us  [front(): pl.pallas_call(front_kernel, out_shape=[jax.ShapeDtypeStruct((rows + CODE...]
  transfers between devices with their start and end apart: 11 -> 11, of which waited for: 4 -> 4; matrix products, arithmetic and copies ran while one was open for 0% -> 0% of each run, Pallas kernels for 20% -> 21%
where the time goes in v6:
time: 55.8 us; the launch traced here: 55.6 us
  Pallas kernels  21 us (38%)
  waiting for transfers between devices  19.8 us (35%)
  starting transfers between devices  14 us (25%)
  other arithmetic  0.78 us (1%)
    ppermute x9, waiting for transfers between devices, trade(): return lax.ppermute(x, 'seq', pairs)  19.8 us
    pallas_call x4, Pallas kernels, absorb(): pl.pallas_call(functools.partial(absorb_kernel, reach, flips, blocks, not...  9.39 us
    ppermute x9, starting transfers between devices, trade(): return lax.ppermute(x, 'seq', pairs)  8.91 us
    pallas_call x1, Pallas kernels, front(): pl.pallas_call(front_kernel, out_shape=[jax.ShapeDtypeStruct((rows + CODE...  6.02 us
    pallas_call x1, Pallas kernels, lift(): pl.pallas_call(lift_kernel, out_shape=[jax.ShapeDtypeStruct(a.shape, a.dt...  4.61 us
    ppermute x1, starting transfers between devices, halo_rows(): from_inner = lax.ppermute(jnp.where(odd, initial, last), 'seq', inner)  4.42 us
  transfers between devices with their start and end apart: 11, of which 4 were waited for; matrix products, arithmetic and copies ran while one was open for 0% of the time, Pallas kernels for 21%

profile of v6, /device:TPU:0, one launch (start us, length us, event | category | flops | bytes accessed | tf_op | source)
XLA Modules:
  0.0 55.6 jit_solution(1654455415638147152)
XLA Ops:
  0.0 0.8 %broadcast_select_fusion = (bf16[8,1536]{1,0:T(8,128)(2,1)S(1)}, bf16[8,1536]{1,0:T(8,128)(2,1)S(1)}) fusion(pred[]{:T(512)S(6)} %eq.5, bf16[512,1536]{1,0:T(8,128)(2,1)} %x_hbm.1), kind=kLoop, calls=%fused_computation | loop fusion | flops 24576 | bytes 98305 | tf_op jit(solution)/shard_map/jit(_where)/select_n | solution.py:31
  0.8 0.7 %collective-permute-start.1 = (bf16[8,1536]{1,0:T(8,128)(2,1)S(1)}, bf16[8,1536]{1,0:T(8,128)(2,1)S(1)}, u32[]{:S(2)}, u32[]{:S(2)}) collective-permute-start(bf16[8,1536]{1,0:T(8,128)(2,1)S(1)} %get-tuple-element.85), channel_id=1, source_target_pairs={{1,2},{3,4},{5,6},{7,8},{9,10},{11,12},{13,14},{2,1},{4,3},{6,5},{... | collective-permute-start | bytes 73736 | tf_op jit(solution)/shard_map/ppermute | solution.py:31
  1.4 0.0 copy-start.1
  1.4 4.4 %collective-permute-start = (bf16[8,1536]{1,0:T(8,128)(2,1)S(1)}, bf16[8,1536]{1,0:T(8,128)(2,1)S(1)}, u32[]{:S(2)}, u32[]{:S(2)}) collective-permute-start(bf16[8,1536]{1,0:T(8,128)(2,1)S(1)} %get-tuple-element.86), channel_id=1, source_target_pairs={{0,1},{1,0},{2,3},{3,2},{4,5},{5,4},{6,7},{7,6},{8,9},{9,8},{10,11... | collective-permute-start | bytes 73736 | tf_op jit(solution)/shard_map/ppermute | solution.py:30
  5.9 4.6 %lift.1 = (bf16[512,1536]{1,0:T(8,128)(2,1)S(1)}, bf16[3,1536,768]{2,1,0:T(8,128)(2,1)S(1)}, bf16[768,1536]{1,0:T(8,128)(2,1)S(1)}, bf16[1536,128]{1,0:T(8,128)(...) custom-call(bf16[512,1536]{1,0:T(8,128)(2,1)} %x_hbm.1, ...), custom_call_target="tpu_custom_call" | custom-call | tf_op jit(solution)/shard_map/lift/pallas_call | solution.py:87
  10.5 0.0 collective-permute-done.1.outside_ref
  10.5 0.0 collective-permute-done.twin_ref
  10.5 0.0 copy-done.1
  10.5 0.0 copy-start
  10.5 6.0 %front.1 = (bf16[528,128]{1,0:T(8,128)(2,1)S(1)}, bf16[512,256]{1,0:T(8,128)(2,1)S(1)}) custom-call(bf16[512,1536]{1,0:T(8,128)(2,1)S(1)} %get-tuple-element.45.x_ref, bf16[3,1536,768]{2,1,0:T(8,128)(2,1)S(1)} %get-tuple-element.46.taps, bf16[768,1536]{1,0:T(8,128)(2,1)S(1)} %get-tuple-element.47.mix, bf16[1536,128]{1,0:T(8,128)(2,1)S(1)} %get-tuple-element.48.wq, ...), custom_call_target="tpu_custom_call" | custom-call | tf_op jit(solution)/shard_map/front/pallas_call | solution.py:193
  16.5 1.6 %collective-permute-start.2 = (bf16[528,128]{1,0:T(8,128)(2,1)S(1)}, bf16[528,128]{1,0:T(8,128)(2,1)S(1)}, u32[]{:S(2)}, u32[]{:S(2)}) collective-permute-start(bf16[528,128]{1,0:T(8,128)(2,1)S(1)} %get-tuple-element.52.refs_0_), channel_id=1, source_target_pairs={{0,2},{1,3},{2,0},{3,1},{4,6},{5,7},{6,4},{7,5},{8,10},{9,11},{10,... | collective-permute-start | bytes 405512 | tf_op jit(solution)/shard_map/ppermute | solution.py:520
  18.1 0.0 collective-permute-start.6
  18.1 0.7 %collective-permute-start.5 = (bf16[512,256]{1,0:T(8,128)(2,1)S(1)}, bf16[512,256]{1,0:T(8,128)(2,1)S(1)}, u32[]{:S(2)}, u32[]{:S(2)}) collective-permute-start(bf16[512,256]{1,0:T(8,128)(2,1)S(1)} %get-tuple-element.53.refs_2_), channel_id=1, source_target_pairs={{4,8},{5,9},{6,10},{7,11},{8,4},{9,5},{10,6},{11,7},{20,24},{21,25... | collective-permute-start | bytes 786440 | tf_op jit(solution)/shard_map/ppermute | solution.py:520
  18.8 4.5 %collective-permute-start.4 = (bf16[512,256]{1,0:T(8,128)(2,1)S(1)}, bf16[512,256]{1,0:T(8,128)(2,1)S(1)}, u32[]{:S(2)}, u32[]{:S(2)}) collective-permute-start(bf16[512,256]{1,0:T(8,128)(2,1)S(1)} %get-tuple-element.53.refs_2_), channel_id=1, source_target_pairs={{0,4},{1,5},{2,6},{3,7},{4,0},{5,1},{6,2},{7,3},{8,12},{9,13},{10,... | collective-permute-start | bytes 786440 | tf_op jit(solution)/shard_map/ppermute | solution.py:520
  23.3 0.0 collective-permute-done.2.refs_1_.refs_0_
  23.3 0.0 collective-permute-done.6.refs_3_
  23.3 0.0 copy-done
  23.3 2.9 %shard_map.82 = (f32[512,128]{1,0:T(8,128)S(1)}, f32[512,128]{1,0:T(8,128)S(1)}, f32[512,128]{1,0:T(8,128)S(1)}, f32[512,128]{1,0:T(8,128)S(1)}, f32[512,128]{1,0:T(8,128)S(1)}, /*index=5*/f32[512,128]{1,0:T(8,128)S(1)}) custom-call(s32[8,65]{1,0:T(8,128)S(1)} %pad_add_fusion.codes_ref, bf16[528,128]{1,0:T(8,128)(2,1)S(1)} %get-tuple-element.52.refs_0_, ...), custom_call_target="tpu_custom_call" | custom-call | flops 536870912 | bytes 4194304 | tf_op jit(solution)/shard_map/pallas_call | solution.py:463
  26.2 0.0 collective-permute-done.5.refs_4_
  26.2 3.7 %collective-permute-done.4.refs_2_ = bf16[512,256]{1,0:T(8,128)(2,1)S(1)} collective-permute-done((bf16[512,256]{1,0:T(8,128)(2,1)S(1)}, bf16[512,256]{1,0:T(8,128)(2,1)S(1)}, u32[]{:S(2)}, u32[]{:S(2)}) %collective-permute-start.4) | collective-permute-done | bytes 262176 | tf_op jit(solution)/shard_map/ppermute | solution.py:520
  30.0 0.0 collective-permute-start.7
  30.0 0.5 collective-permute-start.8
  30.5 1.6 %collective-permute-start.3 = (bf16[512,256]{1,0:T(8,128)(2,1)S(1)}, bf16[512,256]{1,0:T(8,128)(2,1)S(1)}, u32[]{:S(2)}, u32[]{:S(2)}) collective-permute-start(bf16[512,256]{1,0:T(8,128)(2,1)S(1)} %get-tuple-element.53.refs_2_), channel_id=1, source_target_pairs={{0,8},{1,9},{2,10},{3,11},{4,12},{5,13},{6,14},{7,15},{8,0},{9,1},... | collective-permute-start | bytes 786440 | tf_op jit(solution)/shard_map/ppermute | solution.py:520
  32.1 0.0 collective-permute-done.7.refs_3_
  32.1 0.0 collective-permute-done.8.refs_5_
  32.1 2.7 %shard_map.83 = (f32[512,128]{1,0:T(8,128)S(1)}, f32[512,128]{1,0:T(8,128)S(1)}, f32[512,128]{1,0:T(8,128)S(1)}, f32[512,128]{1,0:T(8,128)S(1)}, f32[512,128]{1,0:T(8,128)S(1)}, /*index=5*/f32[512,128]{1,0:T(8,128)S(1)}) custom-call(s32[8,65]{1,0:T(8,128)S(1)} %pad_add_fusion.codes_ref, bf16[528,128]{1,0:T(8,128)(2,1)S(1)} %get-tuple-element.52.refs_0_, ...), custom_call_target="tpu_custom_call" | custom-call | flops 1073741824 | bytes 8388608 | tf_op jit(solution)/shard_map/pallas_call | solution.py:463
  34.8 10.4 %collective-permute-done.3.refs_1_ = bf16[512,256]{1,0:T(8,128)(2,1)S(1)} collective-permute-done((bf16[512,256]{1,0:T(8,128)(2,1)S(1)}, bf16[512,256]{1,0:T(8,128)(2,1)S(1)}, u32[]{:S(2)}, u32[]{:S(2)}) %collective-permute-start.3) | collective-permute-done | bytes 262176 | tf_op jit(solution)/shard_map/ppermute | solution.py:520
  45.2 0.0 collective-permute-start.9
  45.2 1.5 %collective-permute-done.9.refs_2_ = bf16[512,256]{1,0:T(8,128)(2,1)S(1)} collective-permute-done((bf16[512,256]{1,0:T(8,128)(2,1)S(1)}, bf16[512,256]{1,0:T(8,128)(2,1)S(1)}, u32[]{:S(2)}, u32[]{:S(2)}) %collective-permute-start.9) | collective-permute-done | bytes 262176 | tf_op jit(solution)/shard_map/ppermute | solution.py:520
  46.7 2.2 %shard_map.85 = bf16[544,128]{1,0:T(8,128)(2,1)S(1)} custom-call(s32[8,65]{1,0:T(8,128)S(1)} %pad_add_fusion.codes_ref, bf16[528,128]{1,0:T(8,128)(2,1)S(1)} %collective-permute-done.2.refs_1_.refs_0_, bf16[512,256]{1,0:T(8,128)(2,1)S(1)} %collective-permute-done.3.refs_1_, bf16[512,256]{1,0:T(8,128)(2,1)S(1)} %collective-permute-done.9.refs_2_, ...), custom_call_target="tpu_custom_call" | custom-call | flops 268435456 | bytes 2097152 | tf_op jit(solution)/shard_map/pallas_call | solution.py:463
  48.9 0.1 collective-permute-start.10
  49.0 1.6 %shard_map.84 = (f32[512,128]{1,0:T(8,128)S(1)}, f32[512,128]{1,0:T(8,128)S(1)}, f32[512,128]{1,0:T(8,128)S(1)}) custom-call(s32[8,65]{1,0:T(8,128)S(1)} %pad_add_fusion.codes_ref, bf16[528,128]{1,0:T(8,128)(2,1)S(1)} %get-tuple-element.52.refs_0_, bf16[512,256]{1,0:T(8,128)(2,1)S(1)} %collective-permute-done.3.refs_1_, ...), custom_call_target="tpu_custom_call" | custom-call | flops 268435456 | bytes 2097152 | tf_op jit(solution)/shard_map/pallas_call | solution.py:463
  50.6 4.1 %collective-permute-done.10.pack_ref = bf16[544,128]{1,0:T(8,128)(2,1)S(1)} collective-permute-done((bf16[544,128]{1,0:T(8,128)(2,1)S(1)}, bf16[544,128]{1,0:T(8,128)(2,1)S(1)}, u32[]{:S(2)}, u32[]{:S(2)}) %collective-permute-start.10) | collective-permute-done | bytes 139296 | tf_op jit(solution)/shard_map/ppermute | solution.py:520
  54.7 0.9 %merge.1 = bf16[512,128]{1,0:T(8,128)(2,1)} custom-call(f32[512,128]{1,0:T(8,128)S(1)} %get-tuple-element.79.peak_ref, f32[512,128]{1,0:T(8,128)S(1)} %get-tuple-element.80.total_ref, f32[512,128]{1,0:T(8,128)S(1)} %get-tuple-element.81.acc_ref, bf16[544,128]{1,0:T(8,128)(2,1)S(1)} %collective-permute-done.10.pack_ref), custom_call_target="tpu_custom_call" | custom-call | tf_op jit(solution)/shard_map/merge/pallas_call | solution.py:555
  (2 shorter events, 0.0 us)
Async XLA Ops:
  0.8 9.7 %collective-permute-start.1 = (bf16[8,1536]{1,0:T(8,128)(2,1)S(1)}, bf16[8,1536]{1,0:T(8,128)(2,1)S(1)}, u32[]{:S(2)}, u32[]{:S(2)}) collective-permute-start(bf16[8,1536]{1,0:T(8,128)(2,1)S(1)} %get-tuple-element.85), channel_id=1, source_target_pairs={{1,2},{3,4},{5,6},{7,8},{9,10},{11,12},{13,14},{2,1},{4,3},{6,5},{... | collective-permute-start | bytes 73736 | tf_op jit(solution)/shard_map/ppermute | solution.py:31
  1.4 9.1 %copy-start.1 = (s32[4,65]{1,0:T(4,128)S(1)}, s32[4,65]{1,0:T(4,128)}, u32[]{:S(2)}) copy-start(s32[4,65]{1,0:T(4,128)} %codes_ref.1) | copy-start | bytes 3124
  1.4 9.1 %collective-permute-start = (bf16[8,1536]{1,0:T(8,128)(2,1)S(1)}, bf16[8,1536]{1,0:T(8,128)(2,1)S(1)}, u32[]{:S(2)}, u32[]{:S(2)}) collective-permute-start(bf16[8,1536]{1,0:T(8,128)(2,1)S(1)} %get-tuple-element.86), channel_id=1, source_target_pairs={{0,1},{1,0},{2,3},{3,2},{4,5},{5,4},{6,7},{7,6},{8,9},{9,8},{10,11... | collective-permute-start | bytes 73736 | tf_op jit(solution)/shard_map/ppermute | solution.py:30
  10.5 12.8 %copy-start = (s32[8192]{0:T(1024)S(1)}, s32[8192]{0:T(1024)}, u32[]{:S(2)}) copy-start(s32[8192]{0:T(1024)} %param.15) | copy-start | bytes 98308
  16.5 6.7 %collective-permute-start.2 = (bf16[528,128]{1,0:T(8,128)(2,1)S(1)}, bf16[528,128]{1,0:T(8,128)(2,1)S(1)}, u32[]{:S(2)}, u32[]{:S(2)}) collective-permute-start(bf16[528,128]{1,0:T(8,128)(2,1)S(1)} %get-tuple-element.52.refs_0_), channel_id=1, source_target_pairs={{0,2},{1,3},{2,0},{3,1},{4,6},{5,7},{6,4},{7,5},{8,10},{9,11},{10,... | collective-permute-start | bytes 405512 | tf_op jit(solution)/shard_map/ppermute | solution.py:520
  18.1 5.2 %collective-permute-start.6 = (bf16[512,256]{1,0:T(8,128)(2,1)S(1)}, bf16[512,256]{1,0:T(8,128)(2,1)S(1)}, u32[]{:S(2)}, u32[]{:S(2)}) collective-permute-start(bf16[512,256]{1,0:T(8,128)(2,1)S(1)} %get-tuple-element.53.refs_2_), channel_id=1, source_target_pairs={{0,1},{1,0},{2,3},{3,2},{4,5},{5,4},{6,7},{7,6},{8,9},{9,8},{10,11... | collective-permute-start | bytes 786440 | tf_op jit(solution)/shard_map/ppermute | solution.py:520
  18.1 8.1 %collective-permute-start.5 = (bf16[512,256]{1,0:T(8,128)(2,1)S(1)}, bf16[512,256]{1,0:T(8,128)(2,1)S(1)}, u32[]{:S(2)}, u32[]{:S(2)}) collective-permute-start(bf16[512,256]{1,0:T(8,128)(2,1)S(1)} %get-tuple-element.53.refs_2_), channel_id=1, source_target_pairs={{4,8},{5,9},{6,10},{7,11},{8,4},{9,5},{10,6},{11,7},{20,24},{21,25... | collective-permute-start | bytes 786440 | tf_op jit(solution)/shard_map/ppermute | solution.py:520
  18.8 11.2 %collective-permute-start.4 = (bf16[512,256]{1,0:T(8,128)(2,1)S(1)}, bf16[512,256]{1,0:T(8,128)(2,1)S(1)}, u32[]{:S(2)}, u32[]{:S(2)}) collective-permute-start(bf16[512,256]{1,0:T(8,128)(2,1)S(1)} %get-tuple-element.53.refs_2_), channel_id=1, source_target_pairs={{0,4},{1,5},{2,6},{3,7},{4,0},{5,1},{6,2},{7,3},{8,12},{9,13},{10,... | collective-permute-start | bytes 786440 | tf_op jit(solution)/shard_map/ppermute | solution.py:520
  30.0 2.1 %collective-permute-start.7 = (bf16[512,256]{1,0:T(8,128)(2,1)S(1)}, bf16[512,256]{1,0:T(8,128)(2,1)S(1)}, u32[]{:S(2)}, u32[]{:S(2)}) collective-permute-start(bf16[512,256]{1,0:T(8,128)(2,1)S(1)} %collective-permute-done.4.refs_2_), channel_id=1, source_target_pairs={{0,1},{1,0},{2,3},{3,2},{4,5},{5,4},{6,7},{7,6},{8,9},{9,8},{10,11... | collective-permute-start | bytes 786440 | tf_op jit(solution)/shard_map/ppermute | solution.py:520
  30.0 2.1 %collective-permute-start.8 = (bf16[512,256]{1,0:T(8,128)(2,1)S(1)}, bf16[512,256]{1,0:T(8,128)(2,1)S(1)}, u32[]{:S(2)}, u32[]{:S(2)}) collective-permute-start(bf16[512,256]{1,0:T(8,128)(2,1)S(1)} %collective-permute-done.5.refs_4_), channel_id=1, source_target_pairs={{0,1},{1,0},{2,3},{3,2},{4,5},{5,4},{6,7},{7,6},{8,9},{9,8},{10,11... | collective-permute-start | bytes 786440 | tf_op jit(solution)/shard_map/ppermute | solution.py:520
  30.5 14.7 %collective-permute-start.3 = (bf16[512,256]{1,0:T(8,128)(2,1)S(1)}, bf16[512,256]{1,0:T(8,128)(2,1)S(1)}, u32[]{:S(2)}, u32[]{:S(2)}) collective-permute-start(bf16[512,256]{1,0:T(8,128)(2,1)S(1)} %get-tuple-element.53.refs_2_), channel_id=1, source_target_pairs={{0,8},{1,9},{2,10},{3,11},{4,12},{5,13},{6,14},{7,15},{8,0},{9,1},... | collective-permute-start | bytes 786440 | tf_op jit(solution)/shard_map/ppermute | solution.py:520
  45.2 1.5 %collective-permute-start.9 = (bf16[512,256]{1,0:T(8,128)(2,1)S(1)}, bf16[512,256]{1,0:T(8,128)(2,1)S(1)}, u32[]{:S(2)}, u32[]{:S(2)}) collective-permute-start(bf16[512,256]{1,0:T(8,128)(2,1)S(1)} %collective-permute-done.3.refs_1_), channel_id=1, source_target_pairs={{0,1},{1,0},{2,3},{3,2},{4,5},{5,4},{6,7},{7,6},{8,9},{9,8},{10,11... | collective-permute-start | bytes 786440 | tf_op jit(solution)/shard_map/ppermute | solution.py:520
  48.9 5.8 %collective-permute-start.10 = (bf16[544,128]{1,0:T(8,128)(2,1)S(1)}, bf16[544,128]{1,0:T(8,128)(2,1)S(1)}, u32[]{:S(2)}, u32[]{:S(2)}) collective-permute-start(bf16[544,128]{1,0:T(8,128)(2,1)S(1)} %shard_map.85), channel_id=1, source_target_pairs={{0,2},{1,3},{2,0},{3,1},{4,6},{5,7},{6,4},{7,5},{8,10},{9,11},{10,... | collective-permute-start | bytes 417800 | tf_op jit(solution)/shard_map/ppermute | solution.py:520

commit v7 on v6

--- a/solution.py
+++ b/solution.py
@@ -548,7 +548,12 @@
     far_twin = trade(far, 1)
     away = [far, far_twin]
     leaps = (2 * z, 2 * z + 1)
-    (pack,) = absorb(reach, codes, [peer_queries], away, *common, (half,), leaps, state[3:], True)
+    theirs = absorb(
+        reach, codes, [peer_queries], away[:1], *common, (half,), leaps[:1], state[3:], False
+    )
+    (pack,) = absorb(
+        reach, codes, [peer_queries], away[1:], *common, (half,), leaps[1:], theirs, True
+    )
     other = trade(pack, half)
     peak, total, acc = absorb(reach, codes, [queries], away, *common, (0,), leaps, state[:3], False)
     vmem = pl.BlockSpec(memory_space=pltpu.VMEM)

time: 55.8 us -> 55.5 us (level)
  waiting for transfers between devices: 19.8 us -> 18.6 us
  Pallas kernels: 21 us -> 21.8 us
    ppermute x9, waiting for transfers between devices: 19.8 us -> 18.6 us  [trade(): return lax.ppermute(x, 'seq', pairs)]
    pallas_call x4 -> x5, Pallas kernels: 9.39 us -> 10.2 us  [absorb(): pl.pallas_call(functools.partial(absorb_kernel, reach, flips, blocks, not...]
  transfers between devices with their start and end apart: 11 -> 11, of which waited for: 4 -> 4; matrix products, arithmetic and copies ran while one was open for 0% -> 0% of each run, Pallas kernels for 21% -> 24%
where the time goes in v7:
time: 55.5 us; the launch traced here: 55.3 us
  Pallas kernels  21.8 us (39%)
  waiting for transfers between devices  18.6 us (34%)
  starting transfers between devices  14 us (25%)
  other arithmetic  0.78 us (1%)
    ppermute x9, waiting for transfers between devices, trade(): return lax.ppermute(x, 'seq', pairs)  18.6 us
    pallas_call x5, Pallas kernels, absorb(): pl.pallas_call(functools.partial(absorb_kernel, reach, flips, blocks, not...  10.2 us
    ppermute x9, starting transfers between devices, trade(): return lax.ppermute(x, 'seq', pairs)  8.91 us
    pallas_call x1, Pallas kernels, front(): pl.pallas_call(front_kernel, out_shape=[jax.ShapeDtypeStruct((rows + CODE...  6.02 us
    pallas_call x1, Pallas kernels, lift(): pl.pallas_call(lift_kernel, out_shape=[jax.ShapeDtypeStruct(a.shape, a.dt...  4.61 us
    ppermute x1, starting transfers between devices, halo_rows(): from_inner = lax.ppermute(jnp.where(odd, initial, last), 'seq', inner)  4.42 us
  transfers between devices with their start and end apart: 11, of which 4 were waited for; matrix products, arithmetic and copies ran while one was open for 0% of the time, Pallas kernels for 24%

profile of v7, /device:TPU:0, one launch (start us, length us, event | category | flops | bytes accessed | tf_op | source)
XLA Modules:
  0.0 55.3 jit_solution(10897803429197001093)
XLA Ops:
  0.0 0.8 %broadcast_select_fusion = (bf16[8,1536]{1,0:T(8,128)(2,1)S(1)}, bf16[8,1536]{1,0:T(8,128)(2,1)S(1)}) fusion(pred[]{:T(512)S(6)} %eq.5, bf16[512,1536]{1,0:T(8,128)(2,1)} %x_hbm.1), kind=kLoop, calls=%fused_computation | loop fusion | flops 24576 | bytes 98305 | tf_op jit(solution)/shard_map/jit(_where)/select_n | solution.py:31
  0.8 0.7 %collective-permute-start.1 = (bf16[8,1536]{1,0:T(8,128)(2,1)S(1)}, bf16[8,1536]{1,0:T(8,128)(2,1)S(1)}, u32[]{:S(2)}, u32[]{:S(2)}) collective-permute-start(bf16[8,1536]{1,0:T(8,128)(2,1)S(1)} %get-tuple-element.91), channel_id=1, source_target_pairs={{1,2},{3,4},{5,6},{7,8},{9,10},{11,12},{13,14},{2,1},{4,3},{6,5},{... | collective-permute-start | bytes 73736 | tf_op jit(solution)/shard_map/ppermute | solution.py:31
  1.4 0.0 copy-start.1
  1.4 4.4 %collective-permute-start = (bf16[8,1536]{1,0:T(8,128)(2,1)S(1)}, bf16[8,1536]{1,0:T(8,128)(2,1)S(1)}, u32[]{:S(2)}, u32[]{:S(2)}) collective-permute-start(bf16[8,1536]{1,0:T(8,128)(2,1)S(1)} %get-tuple-element.92), channel_id=1, source_target_pairs={{0,1},{1,0},{2,3},{3,2},{4,5},{5,4},{6,7},{7,6},{8,9},{9,8},{10,11... | collective-permute-start | bytes 73736 | tf_op jit(solution)/shard_map/ppermute | solution.py:30
  5.9 4.6 %lift.1 = (bf16[512,1536]{1,0:T(8,128)(2,1)S(1)}, bf16[3,1536,768]{2,1,0:T(8,128)(2,1)S(1)}, bf16[768,1536]{1,0:T(8,128)(2,1)S(1)}, bf16[1536,128]{1,0:T(8,128)(...) custom-call(bf16[512,1536]{1,0:T(8,128)(2,1)} %x_hbm.1, ...), custom_call_target="tpu_custom_call" | custom-call | tf_op jit(solution)/shard_map/lift/pallas_call | solution.py:87
  10.5 0.0 collective-permute-done.1.outside_ref
  10.5 0.0 collective-permute-done.twin_ref
  10.5 0.0 copy-done.1
  10.5 0.0 copy-start
  10.5 6.0 %front.1 = (bf16[528,128]{1,0:T(8,128)(2,1)S(1)}, bf16[512,256]{1,0:T(8,128)(2,1)S(1)}) custom-call(bf16[512,1536]{1,0:T(8,128)(2,1)S(1)} %get-tuple-element.48.x_ref, bf16[3,1536,768]{2,1,0:T(8,128)(2,1)S(1)} %get-tuple-element.49.taps, bf16[768,1536]{1,0:T(8,128)(2,1)S(1)} %get-tuple-element.50.mix, bf16[1536,128]{1,0:T(8,128)(2,1)S(1)} %get-tuple-element.51.wq, ...), custom_call_target="tpu_custom_call" | custom-call | tf_op jit(solution)/shard_map/front/pallas_call | solution.py:193
  16.5 1.6 %collective-permute-start.2 = (bf16[528,128]{1,0:T(8,128)(2,1)S(1)}, bf16[528,128]{1,0:T(8,128)(2,1)S(1)}, u32[]{:S(2)}, u32[]{:S(2)}) collective-permute-start(bf16[528,128]{1,0:T(8,128)(2,1)S(1)} %get-tuple-element.55.refs_0_), channel_id=1, source_target_pairs={{0,2},{1,3},{2,0},{3,1},{4,6},{5,7},{6,4},{7,5},{8,10},{9,11},{10,... | collective-permute-start | bytes 405512 | tf_op jit(solution)/shard_map/ppermute | solution.py:520
  18.1 0.0 collective-permute-start.6
  18.1 0.7 %collective-permute-start.5 = (bf16[512,256]{1,0:T(8,128)(2,1)S(1)}, bf16[512,256]{1,0:T(8,128)(2,1)S(1)}, u32[]{:S(2)}, u32[]{:S(2)}) collective-permute-start(bf16[512,256]{1,0:T(8,128)(2,1)S(1)} %get-tuple-element.56.refs_2_), channel_id=1, source_target_pairs={{4,8},{5,9},{6,10},{7,11},{8,4},{9,5},{10,6},{11,7},{20,24},{21,25... | collective-permute-start | bytes 786440 | tf_op jit(solution)/shard_map/ppermute | solution.py:520
  18.8 4.5 %collective-permute-start.4 = (bf16[512,256]{1,0:T(8,128)(2,1)S(1)}, bf16[512,256]{1,0:T(8,128)(2,1)S(1)}, u32[]{:S(2)}, u32[]{:S(2)}) collective-permute-start(bf16[512,256]{1,0:T(8,128)(2,1)S(1)} %get-tuple-element.56.refs_2_), channel_id=1, source_target_pairs={{0,4},{1,5},{2,6},{3,7},{4,0},{5,1},{6,2},{7,3},{8,12},{9,13},{10,... | collective-permute-start | bytes 786440 | tf_op jit(solution)/shard_map/ppermute | solution.py:520
  23.3 0.0 collective-permute-done.2.refs_1_.refs_0_
  23.3 0.0 collective-permute-done.6.refs_3_
  23.3 0.0 copy-done
  23.3 2.9 %shard_map.82 = (f32[512,128]{1,0:T(8,128)S(1)}, f32[512,128]{1,0:T(8,128)S(1)}, f32[512,128]{1,0:T(8,128)S(1)}, f32[512,128]{1,0:T(8,128)S(1)}, f32[512,128]{1,0:T(8,128)S(1)}, /*index=5*/f32[512,128]{1,0:T(8,128)S(1)}) custom-call(s32[8,65]{1,0:T(8,128)S(1)} %pad_add_fusion.codes_ref, bf16[528,128]{1,0:T(8,128)(2,1)S(1)} %get-tuple-element.55.refs_0_, ...), custom_call_target="tpu_custom_call" | custom-call | flops 536870912 | bytes 4194304 | tf_op jit(solution)/shard_map/pallas_call | solution.py:463
  26.2 0.0 collective-permute-done.5.refs_4_
  26.2 3.7 %collective-permute-done.4.refs_2_ = bf16[512,256]{1,0:T(8,128)(2,1)S(1)} collective-permute-done((bf16[512,256]{1,0:T(8,128)(2,1)S(1)}, bf16[512,256]{1,0:T(8,128)(2,1)S(1)}, u32[]{:S(2)}, u32[]{:S(2)}) %collective-permute-start.4) | collective-permute-done | bytes 262176 | tf_op jit(solution)/shard_map/ppermute | solution.py:520
  30.0 0.0 collective-permute-start.7
  30.0 0.5 collective-permute-start.8
  30.5 1.6 %collective-permute-start.3 = (bf16[512,256]{1,0:T(8,128)(2,1)S(1)}, bf16[512,256]{1,0:T(8,128)(2,1)S(1)}, u32[]{:S(2)}, u32[]{:S(2)}) collective-permute-start(bf16[512,256]{1,0:T(8,128)(2,1)S(1)} %get-tuple-element.56.refs_2_), channel_id=1, source_target_pairs={{0,8},{1,9},{2,10},{3,11},{4,12},{5,13},{6,14},{7,15},{8,0},{9,1},... | collective-permute-start | bytes 786440 | tf_op jit(solution)/shard_map/ppermute | solution.py:520
  32.1 0.0 collective-permute-done.7.refs_3_
  32.1 0.0 collective-permute-done.8.refs_5_
  32.1 2.7 %shard_map.83 = (f32[512,128]{1,0:T(8,128)S(1)}, f32[512,128]{1,0:T(8,128)S(1)}, f32[512,128]{1,0:T(8,128)S(1)}, f32[512,128]{1,0:T(8,128)S(1)}, f32[512,128]{1,0:T(8,128)S(1)}, /*index=5*/f32[512,128]{1,0:T(8,128)S(1)}) custom-call(s32[8,65]{1,0:T(8,128)S(1)} %pad_add_fusion.codes_ref, bf16[528,128]{1,0:T(8,128)(2,1)S(1)} %get-tuple-element.55.refs_0_, ...), custom_call_target="tpu_custom_call" | custom-call | flops 1073741824 | bytes 8388608 | tf_op jit(solution)/shard_map/pallas_call | solution.py:463
  34.8 10.4 %collective-permute-done.3.refs_1_ = bf16[512,256]{1,0:T(8,128)(2,1)S(1)} collective-permute-done((bf16[512,256]{1,0:T(8,128)(2,1)S(1)}, bf16[512,256]{1,0:T(8,128)(2,1)S(1)}, u32[]{:S(2)}, u32[]{:S(2)}) %collective-permute-start.3) | collective-permute-done | bytes 262176 | tf_op jit(solution)/shard_map/ppermute | solution.py:520
  45.2 0.0 collective-permute-start.9
  45.2 1.4 %shard_map.85 = (f32[512,128]{1,0:T(8,128)S(1)}, f32[512,128]{1,0:T(8,128)S(1)}, f32[512,128]{1,0:T(8,128)S(1)}) custom-call(s32[8,65]{1,0:T(8,128)S(1)} %pad_add_fusion.codes_ref, bf16[528,128]{1,0:T(8,128)(2,1)S(1)} %collective-permute-done.2.refs_1_.refs_0_, bf16[512,256]{1,0:T(8,128)(2,1)S(1)} %collective-permute-done.3.refs_1_, ...), custom_call_target="tpu_custom_call" | custom-call | flops 134217728 | bytes 1048576 | tf_op jit(solution)/shard_map/pallas_call | solution.py:463
  46.7 0.1 collective-permute-done.9.refs_2_.refs_1_
  46.7 1.5 %shard_map.86 = bf16[544,128]{1,0:T(8,128)(2,1)S(1)} custom-call(s32[8,65]{1,0:T(8,128)S(1)} %pad_add_fusion.codes_ref, bf16[528,128]{1,0:T(8,128)(2,1)S(1)} %collective-permute-done.2.refs_1_.refs_0_, bf16[512,256]{1,0:T(8,128)(2,1)S(1)} %collective-permute-done.9.refs_2_.refs_1_, f32[16,128,128]{2,1,0:T(8,128)S(1)} %get-tuple-element.57.refs_4_.refs_6_.refs_3_.refs_2_, ...), custom_call_target="tpu_custom_call" | custom-call | flops 134217728 | bytes 1048576 | tf_op jit(solution)/shard_map/pallas_call | solution.py:463
  48.3 0.1 collective-permute-start.10
  48.4 1.6 %shard_map.84 = (f32[512,128]{1,0:T(8,128)S(1)}, f32[512,128]{1,0:T(8,128)S(1)}, f32[512,128]{1,0:T(8,128)S(1)}) custom-call(s32[8,65]{1,0:T(8,128)S(1)} %pad_add_fusion.codes_ref, bf16[528,128]{1,0:T(8,128)(2,1)S(1)} %get-tuple-element.55.refs_0_, bf16[512,256]{1,0:T(8,128)(2,1)S(1)} %collective-permute-done.3.refs_1_, ...), custom_call_target="tpu_custom_call" | custom-call | flops 268435456 | bytes 2097152 | tf_op jit(solution)/shard_map/pallas_call | solution.py:463
  50.0 4.4 %collective-permute-done.10.pack_ref = bf16[544,128]{1,0:T(8,128)(2,1)S(1)} collective-permute-done((bf16[544,128]{1,0:T(8,128)(2,1)S(1)}, bf16[544,128]{1,0:T(8,128)(2,1)S(1)}, u32[]{:S(2)}, u32[]{:S(2)}) %collective-permute-start.10) | collective-permute-done | bytes 139296 | tf_op jit(solution)/shard_map/ppermute | solution.py:520
  54.4 1.0 %merge.1 = bf16[512,128]{1,0:T(8,128)(2,1)} custom-call(f32[512,128]{1,0:T(8,128)S(1)} %get-tuple-element.82.peak_ref, f32[512,128]{1,0:T(8,128)S(1)} %get-tuple-element.83.total_ref, f32[512,128]{1,0:T(8,128)S(1)} %get-tuple-element.84.acc_ref, bf16[544,128]{1,0:T(8,128)(2,1)S(1)} %collective-permute-done.10.pack_ref), custom_call_target="tpu_custom_call" | custom-call | tf_op jit(solution)/shard_map/merge/pallas_call | solution.py:560
  (2 shorter events, 0.0 us)
Async XLA Ops:
  0.8 9.7 %collective-permute-start.1 = (bf16[8,1536]{1,0:T(8,128)(2,1)S(1)}, bf16[8,1536]{1,0:T(8,128)(2,1)S(1)}, u32[]{:S(2)}, u32[]{:S(2)}) collective-permute-start(bf16[8,1536]{1,0:T(8,128)(2,1)S(1)} %get-tuple-element.91), channel_id=1, source_target_pairs={{1,2},{3,4},{5,6},{7,8},{9,10},{11,12},{13,14},{2,1},{4,3},{6,5},{... | collective-permute-start | bytes 73736 | tf_op jit(solution)/shard_map/ppermute | solution.py:31
  1.4 9.1 %copy-start.1 = (s32[4,65]{1,0:T(4,128)S(1)}, s32[4,65]{1,0:T(4,128)}, u32[]{:S(2)}) copy-start(s32[4,65]{1,0:T(4,128)} %codes_ref.1) | copy-start | bytes 3124
  1.4 9.1 %collective-permute-start = (bf16[8,1536]{1,0:T(8,128)(2,1)S(1)}, bf16[8,1536]{1,0:T(8,128)(2,1)S(1)}, u32[]{:S(2)}, u32[]{:S(2)}) collective-permute-start(bf16[8,1536]{1,0:T(8,128)(2,1)S(1)} %get-tuple-element.92), channel_id=1, source_target_pairs={{0,1},{1,0},{2,3},{3,2},{4,5},{5,4},{6,7},{7,6},{8,9},{9,8},{10,11... | collective-permute-start | bytes 73736 | tf_op jit(solution)/shard_map/ppermute | solution.py:30
  10.5 12.8 %copy-start = (s32[8192]{0:T(1024)S(1)}, s32[8192]{0:T(1024)}, u32[]{:S(2)}) copy-start(s32[8192]{0:T(1024)} %param.15) | copy-start | bytes 98308
  16.5 6.7 %collective-permute-start.2 = (bf16[528,128]{1,0:T(8,128)(2,1)S(1)}, bf16[528,128]{1,0:T(8,128)(2,1)S(1)}, u32[]{:S(2)}, u32[]{:S(2)}) collective-permute-start(bf16[528,128]{1,0:T(8,128)(2,1)S(1)} %get-tuple-element.55.refs_0_), channel_id=1, source_target_pairs={{0,2},{1,3},{2,0},{3,1},{4,6},{5,7},{6,4},{7,5},{8,10},{9,11},{10,... | collective-permute-start | bytes 405512 | tf_op jit(solution)/shard_map/ppermute | solution.py:520
  18.1 5.2 %collective-permute-start.6 = (bf16[512,256]{1,0:T(8,128)(2,1)S(1)}, bf16[512,256]{1,0:T(8,128)(2,1)S(1)}, u32[]{:S(2)}, u32[]{:S(2)}) collective-permute-start(bf16[512,256]{1,0:T(8,128)(2,1)S(1)} %get-tuple-element.56.refs_2_), channel_id=1, source_target_pairs={{0,1},{1,0},{2,3},{3,2},{4,5},{5,4},{6,7},{7,6},{8,9},{9,8},{10,11... | collective-permute-start | bytes 786440 | tf_op jit(solution)/shard_map/ppermute | solution.py:520
  18.1 8.1 %collective-permute-start.5 = (bf16[512,256]{1,0:T(8,128)(2,1)S(1)}, bf16[512,256]{1,0:T(8,128)(2,1)S(1)}, u32[]{:S(2)}, u32[]{:S(2)}) collective-permute-start(bf16[512,256]{1,0:T(8,128)(2,1)S(1)} %get-tuple-element.56.refs_2_), channel_id=1, source_target_pairs={{4,8},{5,9},{6,10},{7,11},{8,4},{9,5},{10,6},{11,7},{20,24},{21,25... | collective-permute-start | bytes 786440 | tf_op jit(solution)/shard_map/ppermute | solution.py:520
  18.8 11.2 %collective-permute-start.4 = (bf16[512,256]{1,0:T(8,128)(2,1)S(1)}, bf16[512,256]{1,0:T(8,128)(2,1)S(1)}, u32[]{:S(2)}, u32[]{:S(2)}) collective-permute-start(bf16[512,256]{1,0:T(8,128)(2,1)S(1)} %get-tuple-element.56.refs_2_), channel_id=1, source_target_pairs={{0,4},{1,5},{2,6},{3,7},{4,0},{5,1},{6,2},{7,3},{8,12},{9,13},{10,... | collective-permute-start | bytes 786440 | tf_op jit(solution)/shard_map/ppermute | solution.py:520
  30.0 2.1 %collective-permute-start.7 = (bf16[512,256]{1,0:T(8,128)(2,1)S(1)}, bf16[512,256]{1,0:T(8,128)(2,1)S(1)}, u32[]{:S(2)}, u32[]{:S(2)}) collective-permute-start(bf16[512,256]{1,0:T(8,128)(2,1)S(1)} %collective-permute-done.4.refs_2_), channel_id=1, source_target_pairs={{0,1},{1,0},{2,3},{3,2},{4,5},{5,4},{6,7},{7,6},{8,9},{9,8},{10,11... | collective-permute-start | bytes 786440 | tf_op jit(solution)/shard_map/ppermute | solution.py:520
  30.0 2.1 %collective-permute-start.8 = (bf16[512,256]{1,0:T(8,128)(2,1)S(1)}, bf16[512,256]{1,0:T(8,128)(2,1)S(1)}, u32[]{:S(2)}, u32[]{:S(2)}) collective-permute-start(bf16[512,256]{1,0:T(8,128)(2,1)S(1)} %collective-permute-done.5.refs_4_), channel_id=1, source_target_pairs={{0,1},{1,0},{2,3},{3,2},{4,5},{5,4},{6,7},{7,6},{8,9},{9,8},{10,11... | collective-permute-start | bytes 786440 | tf_op jit(solution)/shard_map/ppermute | solution.py:520
  30.5 14.7 %collective-permute-start.3 = (bf16[512,256]{1,0:T(8,128)(2,1)S(1)}, bf16[512,256]{1,0:T(8,128)(2,1)S(1)}, u32[]{:S(2)}, u32[]{:S(2)}) collective-permute-start(bf16[512,256]{1,0:T(8,128)(2,1)S(1)} %get-tuple-element.56.refs_2_), channel_id=1, source_target_pairs={{0,8},{1,9},{2,10},{3,11},{4,12},{5,13},{6,14},{7,15},{8,0},{9,1},... | collective-permute-start | bytes 786440 | tf_op jit(solution)/shard_map/ppermute | solution.py:520
  45.2 1.5 %collective-permute-start.9 = (bf16[512,256]{1,0:T(8,128)(2,1)S(1)}, bf16[512,256]{1,0:T(8,128)(2,1)S(1)}, u32[]{:S(2)}, u32[]{:S(2)}) collective-permute-start(bf16[512,256]{1,0:T(8,128)(2,1)S(1)} %collective-permute-done.3.refs_1_), channel_id=1, source_target_pairs={{0,1},{1,0},{2,3},{3,2},{4,5},{5,4},{6,7},{7,6},{8,9},{9,8},{10,11... | collective-permute-start | bytes 786440 | tf_op jit(solution)/shard_map/ppermute | solution.py:520
  48.3 6.1 %collective-permute-start.10 = (bf16[544,128]{1,0:T(8,128)(2,1)S(1)}, bf16[544,128]{1,0:T(8,128)(2,1)S(1)}, u32[]{:S(2)}, u32[]{:S(2)}) collective-permute-start(bf16[544,128]{1,0:T(8,128)(2,1)S(1)} %shard_map.86), channel_id=1, source_target_pairs={{0,2},{1,3},{2,0},{3,1},{4,6},{5,7},{6,4},{7,5},{8,10},{9,11},{10,... | collective-permute-start | bytes 417800 | tf_op jit(solution)/shard_map/ppermute | solution.py:520

commit v8 on v7

--- a/solution.py
+++ b/solution.py
@@ -350,8 +350,8 @@
         state_refs, refs = refs[: 3 * sets], refs[3 * sets :]
     outs = 1 if pack else 3 * sets
     out_refs, refs = refs[:outs], refs[outs:]
-    scores, peak, total, acc = refs
-    rows, head_dim = acc.shape
+    scores, *carried = refs
+    rows, head_dim = q_refs[0].shape[0] - CODE_ROWS, q_refs[0].shape[1]
     tile = table.shape[1]
     tiles_per_block = rows // tile
     position = lax.axis_index("seq")
@@ -360,6 +360,7 @@
         owner = position ^ flip
         q_ref = q_refs[s]
         half = 0 if flip == 0 else tiles_per_block
+        peak, total, acc = carried if pack else out_refs[3 * s : 3 * s + 3]
         if begin:
             peak[...] = jnp.full_like(peak, masked_score)
         else:
@@ -374,7 +375,7 @@
                 else:
                     pl.when(jnp.abs(shift) <= reach)(run)
 
-        def score(j, shift, edge):
+        def score(j, shift, edge, peak=peak):
             raw = lax.dot_general(
                 q_ref[0:rows, :],
                 kv_refs[j][:, :head_dim],
@@ -393,7 +394,7 @@
                     peak_now = jnp.maximum(peak_now, column)
                 peak[span, :] = peak_now
 
-        def weigh(j, shift, edge):
+        def weigh(j, shift, edge, peak=peak, total=total, acc=acc):
             parts = []
             sums = total[...]
             for kt in range(tiles_per_block):
@@ -435,10 +436,6 @@
                 pieces.append(piece)
             pieces.append(jnp.zeros_like(exact))
             out_refs[0][rows:, :] = jnp.concatenate(pieces, axis=0).astype(jnp.bfloat16)
-        else:
-            out_refs[3 * s][...] = peak[...]
-            out_refs[3 * s + 1][...] = total[...]
-            out_refs[3 * s + 2][...] = acc[...]
 
 
 def on_diagonal(tile):
@@ -467,10 +464,8 @@
         out_specs=[vmem] * len(out_shape),
         scratch_shapes=[
             pltpu.VMEM((n, rows, rows), jnp.float32),
-            pltpu.VMEM((rows, tile), jnp.float32),
-            pltpu.VMEM((rows, tile), jnp.float32),
-            pltpu.VMEM((rows, head_dim), jnp.float32),
-        ],
+        ]
+        + pack * [pltpu.VMEM((rows, tile), jnp.float32)] * 3,
         compiler_params=pltpu.CompilerParams(vmem_limit_bytes=24 << 20),
         cost_estimate=pl.CostEstimate(
             flops=units * 4 * rows * rows * head_dim,
@@ -520,7 +515,6 @@
         return lax.ppermute(x, "seq", pairs)
 
     peer_queries = trade(queries, half)
-    far = trade(keyval, 2 * z)
     middle = trade(keyval, 3 * z, lambda level: level in (1, 2))
     near = trade(keyval, z)
     twin = trade(keyval, 1)
@@ -531,17 +525,33 @@
         reach, codes, [queries, peer_queries], [keyval, twin], *common, (0, half), (0, 1), [], False
     )
     near, middle, state = lax.optimization_barrier((near, middle, state))
+    level = lax.axis_index("seq") // z
+    onward = jnp.where((level == 1) | (level == 2), middle, keyval)
+    leap = (2 * z, -z, z, -2 * z)
+    far = lax.ppermute(onward, "seq", [(i, i + leap[i // z]) for i in range(seq_size)])
     near_twin = trade(near, 1)
     middle_twin = trade(middle, 1)
     state = absorb(
         reach,
         codes,
         [queries, peer_queries],
-        [near, near_twin, middle, middle_twin],
+        [near, middle],
         *common,
         (0, half),
-        (z, z + 1, 3 * z, 3 * z + 1),
+        (z, 3 * z),
         state,
+        False,
+    )
+    mine = state[:3]
+    state = absorb(
+        reach,
+        codes,
+        [peer_queries],
+        [near_twin, middle_twin],
+        *common,
+        (half,),
+        (z + 1, 3 * z + 1),
+        state[3:],
         False,
     )
     far, state = lax.optimization_barrier((far, state))
@@ -549,13 +559,23 @@
     away = [far, far_twin]
     leaps = (2 * z, 2 * z + 1)
     theirs = absorb(
-        reach, codes, [peer_queries], away[:1], *common, (half,), leaps[:1], state[3:], False
+        reach, codes, [peer_queries], away[:1], *common, (half,), leaps[:1], state, False
     )
     (pack,) = absorb(
         reach, codes, [peer_queries], away[1:], *common, (half,), leaps[1:], theirs, True
     )
     other = trade(pack, half)
-    peak, total, acc = absorb(reach, codes, [queries], away, *common, (0,), leaps, state[:3], False)
+    peak, total, acc = absorb(
+        reach,
+        codes,
+        [queries],
+        [near_twin, middle_twin, *away],
+        *common,
+        (0,),
+        (z + 1, 3 * z + 1, *leaps),
+        mine,
+        False,
+    )
     vmem = pl.BlockSpec(memory_space=pltpu.VMEM)
     return pl.pallas_call(
         merge_kernel,

time: 55.5 us -> 49 us (0.88)
  waiting for transfers between devices: 18.6 us -> 11.2 us
  Pallas kernels: 21.8 us -> 22.6 us
    ppermute x9 -> x8, waiting for transfers between devices: 18.6 us -> 7.98 us  [trade(): return lax.ppermute(x, 'seq', pairs)]
    ppermute x0 -> x1, waiting for transfers between devices: none -> 3.23 us  [attend_split(): lax.ppermute(onward, 'seq', [(i, i + leap[i // z]) for i in range(seq_siz...]
    ppermute x0 -> x1, starting transfers between devices: none -> 1.67 us  [attend_split(): lax.ppermute(onward, 'seq', [(i, i + leap[i // z]) for i in range(seq_siz...]
    ppermute x9 -> x8, starting transfers between devices: 8.91 us -> 7.29 us  [trade(): return lax.ppermute(x, 'seq', pairs)]
    pallas_call x5 -> x6, Pallas kernels: 10.2 us -> 11 us  [absorb(): pl.pallas_call(functools.partial(absorb_kernel, reach, flips, blocks, not...]
  transfers between devices with their start and end apart: 11 -> 11, of which waited for: 4 -> 4; matrix products, arithmetic and copies ran while one was open for 0% -> 0% of each run, Pallas kernels for 24% -> 29%
where the time goes in v8:
time: 49 us; the launch traced here: 48.8 us
  Pallas kernels  22.6 us (46%)
  starting transfers between devices  14 us (29%)
  waiting for transfers between devices  11.2 us (23%)
  other arithmetic  0.81 us (2%)
    pallas_call x6, Pallas kernels, absorb(): pl.pallas_call(functools.partial(absorb_kernel, reach, flips, blocks, not...  11 us
    ppermute x8, waiting for transfers between devices, trade(): return lax.ppermute(x, 'seq', pairs)  7.98 us
    ppermute x8, starting transfers between devices, trade(): return lax.ppermute(x, 'seq', pairs)  7.29 us
    pallas_call x1, Pallas kernels, front(): pl.pallas_call(front_kernel, out_shape=[jax.ShapeDtypeStruct((rows + CODE...  6.02 us
    pallas_call x1, Pallas kernels, lift(): pl.pallas_call(lift_kernel, out_shape=[jax.ShapeDtypeStruct(a.shape, a.dt...  4.61 us
    ppermute x1, starting transfers between devices, halo_rows(): from_inner = lax.ppermute(jnp.where(odd, initial, last), 'seq', inner)  4.42 us
    ppermute x1, waiting for transfers between devices, attend_split(): lax.ppermute(onward, 'seq', [(i, i + leap[i // z]) for i in range(seq_siz...  3.23 us
    ppermute x1, starting transfers between devices, attend_split(): lax.ppermute(onward, 'seq', [(i, i + leap[i // z]) for i in range(seq_siz...  1.67 us
  transfers between devices with their start and end apart: 11, of which 4 were waited for; matrix products, arithmetic and copies ran while one was open for 0% of the time, Pallas kernels for 29%

profile of v8, /device:TPU:0, one launch (start us, length us, event | category | flops | bytes accessed | tf_op | source)
XLA Modules:
  0.0 48.8 jit_solution(14485794052218969158)
XLA Ops:
  0.0 0.8 %broadcast_select_fusion.1 = (bf16[8,1536]{1,0:T(8,128)(2,1)S(1)}, bf16[8,1536]{1,0:T(8,128)(2,1)S(1)}) fusion(pred[]{:T(512)S(6)} %eq.11, bf16[512,1536]{1,0:T(8,128)(2,1)} %x_hbm.1), kind=kLoop, calls=%fused_computation.1 | loop fusion | flops 24576 | bytes 98305 | tf_op jit(solution)/shard_map/jit(_where)/select_n | solution.py:31
  0.8 0.7 %collective-permute-start.1 = (bf16[8,1536]{1,0:T(8,128)(2,1)S(1)}, bf16[8,1536]{1,0:T(8,128)(2,1)S(1)}, u32[]{:S(2)}, u32[]{:S(2)}) collective-permute-start(bf16[8,1536]{1,0:T(8,128)(2,1)S(1)} %get-tuple-element.91), channel_id=1, source_target_pairs={{1,2},{3,4},{5,6},{7,8},{9,10},{11,12},{13,14},{2,1},{4,3},{6,5},{... | collective-permute-start | bytes 73736 | tf_op jit(solution)/shard_map/ppermute | solution.py:31
  1.4 0.0 copy-start.1
  1.4 4.4 %collective-permute-start = (bf16[8,1536]{1,0:T(8,128)(2,1)S(1)}, bf16[8,1536]{1,0:T(8,128)(2,1)S(1)}, u32[]{:S(2)}, u32[]{:S(2)}) collective-permute-start(bf16[8,1536]{1,0:T(8,128)(2,1)S(1)} %get-tuple-element.92), channel_id=1, source_target_pairs={{0,1},{1,0},{2,3},{3,2},{4,5},{5,4},{6,7},{7,6},{8,9},{9,8},{10,11... | collective-permute-start | bytes 73736 | tf_op jit(solution)/shard_map/ppermute | solution.py:30
  5.9 4.6 %lift.1 = (bf16[512,1536]{1,0:T(8,128)(2,1)S(1)}, bf16[3,1536,768]{2,1,0:T(8,128)(2,1)S(1)}, bf16[768,1536]{1,0:T(8,128)(2,1)S(1)}, bf16[1536,128]{1,0:T(8,128)(...) custom-call(bf16[512,1536]{1,0:T(8,128)(2,1)} %x_hbm.1, ...), custom_call_target="tpu_custom_call" | custom-call | tf_op jit(solution)/shard_map/lift/pallas_call | solution.py:87
  10.5 0.0 collective-permute-done.1.outside_ref
  10.5 0.0 collective-permute-done.twin_ref
  10.5 0.0 copy-done.1
  10.5 0.0 copy-start
  10.5 6.0 %front.1 = (bf16[528,128]{1,0:T(8,128)(2,1)S(1)}, bf16[512,256]{1,0:T(8,128)(2,1)S(1)}) custom-call(bf16[512,1536]{1,0:T(8,128)(2,1)S(1)} %get-tuple-element.48.x_ref, bf16[3,1536,768]{2,1,0:T(8,128)(2,1)S(1)} %get-tuple-element.49.taps, bf16[768,1536]{1,0:T(8,128)(2,1)S(1)} %get-tuple-element.50.mix, bf16[1536,128]{1,0:T(8,128)(2,1)S(1)} %get-tuple-element.51.wq, ...), custom_call_target="tpu_custom_call" | custom-call | tf_op jit(solution)/shard_map/front/pallas_call | solution.py:193
  16.5 1.6 %collective-permute-start.2 = (bf16[528,128]{1,0:T(8,128)(2,1)S(1)}, bf16[528,128]{1,0:T(8,128)(2,1)S(1)}, u32[]{:S(2)}, u32[]{:S(2)}) collective-permute-start(bf16[528,128]{1,0:T(8,128)(2,1)S(1)} %get-tuple-element.55.refs_0_), channel_id=1, source_target_pairs={{0,2},{1,3},{2,0},{3,1},{4,6},{5,7},{6,4},{7,5},{8,10},{9,11},{10,... | collective-permute-start | bytes 405512 | tf_op jit(solution)/shard_map/ppermute | solution.py:515
  18.1 0.0 collective-permute-start.5
  18.1 0.7 %collective-permute-start.4 = (bf16[512,256]{1,0:T(8,128)(2,1)S(1)}, bf16[512,256]{1,0:T(8,128)(2,1)S(1)}, u32[]{:S(2)}, u32[]{:S(2)}) collective-permute-start(bf16[512,256]{1,0:T(8,128)(2,1)S(1)} %get-tuple-element.56.refs_2_), channel_id=1, source_target_pairs={{4,8},{5,9},{6,10},{7,11},{8,4},{9,5},{10,6},{11,7},{20,24},{21,25... | collective-permute-start | bytes 786440 | tf_op jit(solution)/shard_map/ppermute | solution.py:515
  18.8 4.5 %collective-permute-start.3 = (bf16[512,256]{1,0:T(8,128)(2,1)S(1)}, bf16[512,256]{1,0:T(8,128)(2,1)S(1)}, u32[]{:S(2)}, u32[]{:S(2)}) collective-permute-start(bf16[512,256]{1,0:T(8,128)(2,1)S(1)} %get-tuple-element.56.refs_2_), channel_id=1, source_target_pairs={{0,4},{1,5},{2,6},{3,7},{4,0},{5,1},{6,2},{7,3},{8,12},{9,13},{10,... | collective-permute-start | bytes 786440 | tf_op jit(solution)/shard_map/ppermute | solution.py:515
  23.3 0.0 collective-permute-done.2.refs_1_.refs_0_
  23.3 0.0 collective-permute-done.5.refs_3_
  23.3 0.0 copy-done
  23.3 2.6 %shard_map.82 = (f32[512,128]{1,0:T(8,128)S(1)}, f32[512,128]{1,0:T(8,128)S(1)}, f32[512,128]{1,0:T(8,128)S(1)}, f32[512,128]{1,0:T(8,128)S(1)}, f32[512,128]{1,0:T(8,128)S(1)}, /*index=5*/f32[512,128]{1,0:T(8,128)S(1)}) custom-call(s32[8,65]{1,0:T(8,128)S(1)} %pad_add_fusion.codes_ref, bf16[528,128]{1,0:T(8,128)(2,1)S(1)} %get-tuple-element.55.refs_0_, ...), custom_call_target="tpu_custom_call" | custom-call | flops 536870912 | bytes 4194304 | tf_op jit(solution)/shard_map/pallas_call | solution.py:460
  26.0 0.0 collective-permute-done.4.refs_3_
  26.0 4.0 %collective-permute-done.3.refs_2_ = bf16[512,256]{1,0:T(8,128)(2,1)S(1)} collective-permute-done((bf16[512,256]{1,0:T(8,128)(2,1)S(1)}, bf16[512,256]{1,0:T(8,128)(2,1)S(1)}, u32[]{:S(2)}, u32[]{:S(2)}) %collective-permute-start.3) | collective-permute-done | bytes 262176 | tf_op jit(solution)/shard_map/ppermute | solution.py:515
  30.0 0.0 collective-permute-start.6
  30.0 0.5 %collective-permute-start.7 = (bf16[512,256]{1,0:T(8,128)(2,1)S(1)}, bf16[512,256]{1,0:T(8,128)(2,1)S(1)}, u32[]{:S(2)}, u32[]{:S(2)}) collective-permute-start(bf16[512,256]{1,0:T(8,128)(2,1)S(1)} %collective-permute-done.4.refs_3_), channel_id=1, source_target_pairs={{0,1},{1,0},{2,3},{3,2},{4,5},{5,4},{6,7},{7,6},{8,9},{9,8},{10,11... | collective-permute-start | bytes 786440 | tf_op jit(solution)/shard_map/ppermute | solution.py:515
  30.5 1.7 %collective-permute-start.8 = (bf16[512,256]{1,0:T(8,128)(2,1)S(1)}, bf16[512,256]{1,0:T(8,128)(2,1)S(1)}, u32[]{:S(2)}, u32[]{:S(2)}) collective-permute-start(bf16[512,256]{1,0:T(8,128)(2,1)S(1)} %broadcast_select_fusion), channel_id=1, source_target_pairs={{0,8},{1,9},{2,10},{3,11},{4,0},{5,1},{6,2},{7,3},{8,12},{9,13},{1... | collective-permute-start | bytes 786440 | tf_op jit(solution)/shard_map/ppermute | solution.py:531
  32.2 2.0 %shard_map.83 = (f32[512,128]{1,0:T(8,128)S(1)}, f32[512,128]{1,0:T(8,128)S(1)}, f32[512,128]{1,0:T(8,128)S(1)}, f32[512,128]{1,0:T(8,128)S(1)}, f32[512,128]{1,0:T(8,128)S(1)}, /*index=5*/f32[512,128]{1,0:T(8,128)S(1)}) custom-call(s32[8,65]{1,0:T(8,128)S(1)} %pad_add_fusion.codes_ref, bf16[528,128]{1,0:T(8,128)(2,1)S(1)} %get-tuple-element.55.refs_0_, ...), custom_call_target="tpu_custom_call" | custom-call | flops 536870912 | bytes 4194304 | tf_op jit(solution)/shard_map/pallas_call | solution.py:460
  34.2 0.0 collective-permute-done.6.refs_1_
  34.2 0.0 collective-permute-done.7.refs_2_
  34.2 1.3 %shard_map.84 = (f32[512,128]{1,0:T(8,128)S(1)}, f32[512,128]{1,0:T(8,128)S(1)}, f32[512,128]{1,0:T(8,128)S(1)}) custom-call(s32[8,65]{1,0:T(8,128)S(1)} %pad_add_fusion.codes_ref, bf16[528,128]{1,0:T(8,128)(2,1)S(1)} %collective-permute-done.2.refs_1_.refs_0_, bf16[512,256]{1,0:T(8,128)(2,1)S(1)} %collective-permute-done.6.refs_1_, ...), custom_call_target="tpu_custom_call" | custom-call | flops 268435456 | bytes 2097152 | tf_op jit(solution)/shard_map/pallas_call | solution.py:460
  35.5 3.2 %collective-permute-done.8.refs_3_.refs_1_ = bf16[512,256]{1,0:T(8,128)(2,1)S(1)} collective-permute-done((bf16[512,256]{1,0:T(8,128)(2,1)S(1)}, bf16[512,256]{1,0:T(8,128)(2,1)S(1)}, u32[]{:S(2)}, u32[]{:S(2)}) %collective-permute-start.8) | collective-permute-done | bytes 262176 | tf_op jit(solution)/shard_map/ppermute | solution.py:531
  38.8 0.0 collective-permute-start.9
  38.8 1.4 %shard_map.86 = (f32[512,128]{1,0:T(8,128)S(1)}, f32[512,128]{1,0:T(8,128)S(1)}, f32[512,128]{1,0:T(8,128)S(1)}) custom-call(s32[8,65]{1,0:T(8,128)S(1)} %pad_add_fusion.codes_ref, bf16[528,128]{1,0:T(8,128)(2,1)S(1)} %collective-permute-done.2.refs_1_.refs_0_, bf16[512,256]{1,0:T(8,128)(2,1)S(1)} %collective-permute-done.8.refs_3_.refs_1_, ...), custom_call_target="tpu_custom_call" | custom-call | flops 134217728 | bytes 1048576 | tf_op jit(solution)/shard_map/pallas_call | solution.py:460
  40.2 0.1 collective-permute-done.9.refs_4_.refs_1_
  40.3 1.5 %shard_map.87 = bf16[544,128]{1,0:T(8,128)(2,1)S(1)} custom-call(s32[8,65]{1,0:T(8,128)S(1)} %pad_add_fusion.codes_ref, bf16[528,128]{1,0:T(8,128)(2,1)S(1)} %collective-permute-done.2.refs_1_.refs_0_, bf16[512,256]{1,0:T(8,128)(2,1)S(1)} %collective-permute-done.9.refs_4_.refs_1_, f32[16,128,128]{2,1,0:T(8,128)S(1)} %get-tuple-element.57.refs_4_.refs_3_.refs_5_.refs_2_, ...), custom_call_target="tpu_custom_call" | custom-call | flops 134217728 | bytes 1048576 | tf_op jit(solution)/shard_map/pallas_call | solution.py:460
  41.8 0.1 collective-permute-start.10
  41.9 2.1 %shard_map.85 = (f32[512,128]{1,0:T(8,128)S(1)}, f32[512,128]{1,0:T(8,128)S(1)}, f32[512,128]{1,0:T(8,128)S(1)}) custom-call(s32[8,65]{1,0:T(8,128)S(1)} %pad_add_fusion.codes_ref, bf16[528,128]{1,0:T(8,128)(2,1)S(1)} %get-tuple-element.55.refs_0_, bf16[512,256]{1,0:T(8,128)(2,1)S(1)} %collective-permute-done.6.refs_1_, ...), custom_call_target="tpu_custom_call" | custom-call | flops 536870912 | bytes 4194304 | tf_op jit(solution)/shard_map/pallas_call | solution.py:460
  44.0 3.8 %collective-permute-done.10.pack_ref = bf16[544,128]{1,0:T(8,128)(2,1)S(1)} collective-permute-done((bf16[544,128]{1,0:T(8,128)(2,1)S(1)}, bf16[544,128]{1,0:T(8,128)(2,1)S(1)}, u32[]{:S(2)}, u32[]{:S(2)}) %collective-permute-start.10) | collective-permute-done | bytes 139296 | tf_op jit(solution)/shard_map/ppermute | solution.py:515
  47.9 0.9 %merge.1 = bf16[512,128]{1,0:T(8,128)(2,1)} custom-call(f32[512,128]{1,0:T(8,128)S(1)} %get-tuple-element.82.peak_ref, f32[512,128]{1,0:T(8,128)S(1)} %get-tuple-element.83.total_ref, f32[512,128]{1,0:T(8,128)S(1)} %get-tuple-element.84.acc_ref, bf16[544,128]{1,0:T(8,128)(2,1)S(1)} %collective-permute-done.10.pack_ref), custom_call_target="tpu_custom_call" | custom-call | tf_op jit(solution)/shard_map/merge/pallas_call | solution.py:580
  (3 shorter events, 0.1 us)
Async XLA Ops:
  0.8 9.7 %collective-permute-start.1 = (bf16[8,1536]{1,0:T(8,128)(2,1)S(1)}, bf16[8,1536]{1,0:T(8,128)(2,1)S(1)}, u32[]{:S(2)}, u32[]{:S(2)}) collective-permute-start(bf16[8,1536]{1,0:T(8,128)(2,1)S(1)} %get-tuple-element.91), channel_id=1, source_target_pairs={{1,2},{3,4},{5,6},{7,8},{9,10},{11,12},{13,14},{2,1},{4,3},{6,5},{... | collective-permute-start | bytes 73736 | tf_op jit(solution)/shard_map/ppermute | solution.py:31
  1.4 9.1 %copy-start.1 = (s32[4,65]{1,0:T(4,128)S(1)}, s32[4,65]{1,0:T(4,128)}, u32[]{:S(2)}) copy-start(s32[4,65]{1,0:T(4,128)} %codes_ref.1) | copy-start | bytes 3124
  1.4 9.1 %collective-permute-start = (bf16[8,1536]{1,0:T(8,128)(2,1)S(1)}, bf16[8,1536]{1,0:T(8,128)(2,1)S(1)}, u32[]{:S(2)}, u32[]{:S(2)}) collective-permute-start(bf16[8,1536]{1,0:T(8,128)(2,1)S(1)} %get-tuple-element.92), channel_id=1, source_target_pairs={{0,1},{1,0},{2,3},{3,2},{4,5},{5,4},{6,7},{7,6},{8,9},{9,8},{10,11... | collective-permute-start | bytes 73736 | tf_op jit(solution)/shard_map/ppermute | solution.py:30
  10.5 12.8 %copy-start = (s32[8192]{0:T(1024)S(1)}, s32[8192]{0:T(1024)}, u32[]{:S(2)}) copy-start(s32[8192]{0:T(1024)} %param.15) | copy-start | bytes 98308
  16.5 6.7 %collective-permute-start.2 = (bf16[528,128]{1,0:T(8,128)(2,1)S(1)}, bf16[528,128]{1,0:T(8,128)(2,1)S(1)}, u32[]{:S(2)}, u32[]{:S(2)}) collective-permute-start(bf16[528,128]{1,0:T(8,128)(2,1)S(1)} %get-tuple-element.55.refs_0_), channel_id=1, source_target_pairs={{0,2},{1,3},{2,0},{3,1},{4,6},{5,7},{6,4},{7,5},{8,10},{9,11},{10,... | collective-permute-start | bytes 405512 | tf_op jit(solution)/shard_map/ppermute | solution.py:515
  18.1 5.2 %collective-permute-start.5 = (bf16[512,256]{1,0:T(8,128)(2,1)S(1)}, bf16[512,256]{1,0:T(8,128)(2,1)S(1)}, u32[]{:S(2)}, u32[]{:S(2)}) collective-permute-start(bf16[512,256]{1,0:T(8,128)(2,1)S(1)} %get-tuple-element.56.refs_2_), channel_id=1, source_target_pairs={{0,1},{1,0},{2,3},{3,2},{4,5},{5,4},{6,7},{7,6},{8,9},{9,8},{10,11... | collective-permute-start | bytes 786440 | tf_op jit(solution)/shard_map/ppermute | solution.py:515
  18.1 7.8 %collective-permute-start.4 = (bf16[512,256]{1,0:T(8,128)(2,1)S(1)}, bf16[512,256]{1,0:T(8,128)(2,1)S(1)}, u32[]{:S(2)}, u32[]{:S(2)}) collective-permute-start(bf16[512,256]{1,0:T(8,128)(2,1)S(1)} %get-tuple-element.56.refs_2_), channel_id=1, source_target_pairs={{4,8},{5,9},{6,10},{7,11},{8,4},{9,5},{10,6},{11,7},{20,24},{21,25... | collective-permute-start | bytes 786440 | tf_op jit(solution)/shard_map/ppermute | solution.py:515
  18.8 11.2 %collective-permute-start.3 = (bf16[512,256]{1,0:T(8,128)(2,1)S(1)}, bf16[512,256]{1,0:T(8,128)(2,1)S(1)}, u32[]{:S(2)}, u32[]{:S(2)}) collective-permute-start(bf16[512,256]{1,0:T(8,128)(2,1)S(1)} %get-tuple-element.56.refs_2_), channel_id=1, source_target_pairs={{0,4},{1,5},{2,6},{3,7},{4,0},{5,1},{6,2},{7,3},{8,12},{9,13},{10,... | collective-permute-start | bytes 786440 | tf_op jit(solution)/shard_map/ppermute | solution.py:515
  30.0 4.2 %collective-permute-start.6 = (bf16[512,256]{1,0:T(8,128)(2,1)S(1)}, bf16[512,256]{1,0:T(8,128)(2,1)S(1)}, u32[]{:S(2)}, u32[]{:S(2)}) collective-permute-start(bf16[512,256]{1,0:T(8,128)(2,1)S(1)} %collective-permute-done.3.refs_2_), channel_id=1, source_target_pairs={{0,1},{1,0},{2,3},{3,2},{4,5},{5,4},{6,7},{7,6},{8,9},{9,8},{10,11... | collective-permute-start | bytes 786440 | tf_op jit(solution)/shard_map/ppermute | solution.py:515
  30.0 4.3 %collective-permute-start.7 = (bf16[512,256]{1,0:T(8,128)(2,1)S(1)}, bf16[512,256]{1,0:T(8,128)(2,1)S(1)}, u32[]{:S(2)}, u32[]{:S(2)}) collective-permute-start(bf16[512,256]{1,0:T(8,128)(2,1)S(1)} %collective-permute-done.4.refs_3_), channel_id=1, source_target_pairs={{0,1},{1,0},{2,3},{3,2},{4,5},{5,4},{6,7},{7,6},{8,9},{9,8},{10,11... | collective-permute-start | bytes 786440 | tf_op jit(solution)/shard_map/ppermute | solution.py:515
  30.5 8.3 %collective-permute-start.8 = (bf16[512,256]{1,0:T(8,128)(2,1)S(1)}, bf16[512,256]{1,0:T(8,128)(2,1)S(1)}, u32[]{:S(2)}, u32[]{:S(2)}) collective-permute-start(bf16[512,256]{1,0:T(8,128)(2,1)S(1)} %broadcast_select_fusion), channel_id=1, source_target_pairs={{0,8},{1,9},{2,10},{3,11},{4,0},{5,1},{6,2},{7,3},{8,12},{9,13},{1... | collective-permute-start | bytes 786440 | tf_op jit(solution)/shard_map/ppermute | solution.py:531
  38.8 1.5 %collective-permute-start.9 = (bf16[512,256]{1,0:T(8,128)(2,1)S(1)}, bf16[512,256]{1,0:T(8,128)(2,1)S(1)}, u32[]{:S(2)}, u32[]{:S(2)}) collective-permute-start(bf16[512,256]{1,0:T(8,128)(2,1)S(1)} %collective-permute-done.8.refs_3_.refs_1_), channel_id=1, source_target_pairs={{0,1},{1,0},{2,3},{3,2},{4,5},{5,4},{6,7},{7,6},{8,9},{9,8},{10,11... | collective-permute-start | bytes 786440 | tf_op jit(solution)/shard_map/ppermute | solution.py:515
  41.8 6.0 %collective-permute-start.10 = (bf16[544,128]{1,0:T(8,128)(2,1)S(1)}, bf16[544,128]{1,0:T(8,128)(2,1)S(1)}, u32[]{:S(2)}, u32[]{:S(2)}) collective-permute-start(bf16[544,128]{1,0:T(8,128)(2,1)S(1)} %shard_map.87), channel_id=1, source_target_pairs={{0,2},{1,3},{2,0},{3,1},{4,6},{5,7},{6,4},{7,5},{8,10},{9,11},{10,... | collective-permute-start | bytes 417800 | tf_op jit(solution)/shard_map/ppermute | solution.py:515

commit v9 on v8

--- a/solution.py
+++ b/solution.py
@@ -518,31 +518,28 @@
     middle = trade(keyval, 3 * z, lambda level: level in (1, 2))
     near = trade(keyval, z)
     twin = trade(keyval, 1)
-    peer_codes = peer_queries[rows : rows + tile_codes.shape[0], : tile_codes.shape[1]]
-    codes = jnp.concatenate([tile_codes, peer_codes.astype(jnp.int32)], axis=0)
     common = (table, valid_rows)
-    state = absorb(
-        reach, codes, [queries, peer_queries], [keyval, twin], *common, (0, half), (0, 1), [], False
-    )
-    near, middle, state = lax.optimization_barrier((near, middle, state))
+    mine = absorb(reach, tile_codes, [queries], [keyval, twin], *common, (0,), (0, 1), [], False)
+    middle, mine = lax.optimization_barrier((middle, mine))
     level = lax.axis_index("seq") // z
     onward = jnp.where((level == 1) | (level == 2), middle, keyval)
     leap = (2 * z, -z, z, -2 * z)
     far = lax.ppermute(onward, "seq", [(i, i + leap[i // z]) for i in range(seq_size)])
     near_twin = trade(near, 1)
     middle_twin = trade(middle, 1)
+    peer_codes = peer_queries[rows : rows + tile_codes.shape[0], : tile_codes.shape[1]]
+    codes = jnp.concatenate([tile_codes, peer_codes.astype(jnp.int32)], axis=0)
     state = absorb(
         reach,
         codes,
-        [queries, peer_queries],
-        [near, middle],
+        [peer_queries],
+        [keyval, twin, near, middle],
         *common,
-        (0, half),
-        (z, 3 * z),
-        state,
+        (half,),
+        (0, 1, z, 3 * z),
+        [],
         False,
     )
-    mine = state[:3]
     state = absorb(
         reach,
         codes,
@@ -551,7 +548,7 @@
         *common,
         (half,),
         (z + 1, 3 * z + 1),
-        state[3:],
+        state,
         False,
     )
     far, state = lax.optimization_barrier((far, state))
@@ -569,10 +566,10 @@
         reach,
         codes,
         [queries],
-        [near_twin, middle_twin, *away],
+        [near, middle, near_twin, middle_twin, *away],
         *common,
         (0,),
-        (z + 1, 3 * z + 1, *leaps),
+        (z, 3 * z, z + 1, 3 * z + 1, *leaps),
         mine,
         False,
     )

time: 49 us -> 46.4 us (0.947)
  waiting for transfers between devices: 11.2 us -> 5.15 us
  starting transfers between devices: 14 us -> 17.6 us
    ppermute x8, waiting for transfers between devices: 7.98 us -> 2.48 us  [trade(): return lax.ppermute(x, 'seq', pairs)]
    ppermute x1, starting transfers between devices: 1.67 us -> 4.48 us  [attend_split(): lax.ppermute(onward, 'seq', [(i, i + leap[i // z]) for i in range(seq_siz...]
    ppermute x8, starting transfers between devices: 7.29 us -> 8 us  [trade(): return lax.ppermute(x, 'seq', pairs)]
    ppermute x1, waiting for transfers between devices: 3.23 us -> 2.67 us  [attend_split(): lax.ppermute(onward, 'seq', [(i, i + leap[i // z]) for i in range(seq_siz...]
  transfers between devices with their start and end apart: 11 -> 11, of which waited for: 4 -> 3; matrix products, arithmetic and copies ran while one was open for 0% -> 0% of each run, Pallas kernels for 29% -> 30%
where the time goes in v9:
time: 46.4 us; the launch traced here: 46.2 us
  Pallas kernels  22.5 us (48%)
  starting transfers between devices  17.6 us (38%)
  waiting for transfers between devices  5.15 us (11%)
  other arithmetic  0.81 us (2%)
    pallas_call x6, Pallas kernels, absorb(): pl.pallas_call(functools.partial(absorb_kernel, reach, flips, blocks, not...  10.9 us
    ppermute x8, starting transfers between devices, trade(): return lax.ppermute(x, 'seq', pairs)  8 us
    pallas_call x1, Pallas kernels, front(): pl.pallas_call(front_kernel, out_shape=[jax.ShapeDtypeStruct((rows + CODE...  6.02 us
    pallas_call x1, Pallas kernels, lift(): pl.pallas_call(lift_kernel, out_shape=[jax.ShapeDtypeStruct(a.shape, a.dt...  4.61 us
    ppermute x1, starting transfers between devices, attend_split(): lax.ppermute(onward, 'seq', [(i, i + leap[i // z]) for i in range(seq_siz...  4.48 us
    ppermute x1, starting transfers between devices, halo_rows(): from_inner = lax.ppermute(jnp.where(odd, initial, last), 'seq', inner)  4.42 us
    ppermute x1, waiting for transfers between devices, attend_split(): lax.ppermute(onward, 'seq', [(i, i + leap[i // z]) for i in range(seq_siz...  2.67 us
    ppermute x8, waiting for transfers between devices, trade(): return lax.ppermute(x, 'seq', pairs)  2.48 us
  transfers between devices with their start and end apart: 11, of which 3 were waited for; matrix products, arithmetic and copies ran while one was open for 0% of the time, Pallas kernels for 30%

profile of v9, /device:TPU:0, one launch (start us, length us, event | category | flops | bytes accessed | tf_op | source)
XLA Modules:
  0.0 46.2 jit_solution(17443396141147809815)
XLA Ops:
  0.0 0.8 %broadcast_select_fusion.1 = (bf16[8,1536]{1,0:T(8,128)(2,1)S(1)}, bf16[8,1536]{1,0:T(8,128)(2,1)S(1)}) fusion(pred[]{:T(512)S(6)} %eq.11, bf16[512,1536]{1,0:T(8,128)(2,1)} %x_hbm.1), kind=kLoop, calls=%fused_computation.1 | loop fusion | flops 24576 | bytes 98305 | tf_op jit(solution)/shard_map/jit(_where)/select_n | solution.py:31
  0.8 0.7 %collective-permute-start.1 = (bf16[8,1536]{1,0:T(8,128)(2,1)S(1)}, bf16[8,1536]{1,0:T(8,128)(2,1)S(1)}, u32[]{:S(2)}, u32[]{:S(2)}) collective-permute-start(bf16[8,1536]{1,0:T(8,128)(2,1)S(1)} %get-tuple-element.71), channel_id=1, source_target_pairs={{1,2},{3,4},{5,6},{7,8},{9,10},{11,12},{13,14},{2,1},{4,3},{6,5},{... | collective-permute-start | bytes 73736 | tf_op jit(solution)/shard_map/ppermute | solution.py:31
  1.4 0.0 copy-start.1
  1.4 4.4 %collective-permute-start = (bf16[8,1536]{1,0:T(8,128)(2,1)S(1)}, bf16[8,1536]{1,0:T(8,128)(2,1)S(1)}, u32[]{:S(2)}, u32[]{:S(2)}) collective-permute-start(bf16[8,1536]{1,0:T(8,128)(2,1)S(1)} %get-tuple-element.72), channel_id=1, source_target_pairs={{0,1},{1,0},{2,3},{3,2},{4,5},{5,4},{6,7},{7,6},{8,9},{9,8},{10,11... | collective-permute-start | bytes 73736 | tf_op jit(solution)/shard_map/ppermute | solution.py:30
  5.9 4.6 %lift.1 = (bf16[512,1536]{1,0:T(8,128)(2,1)S(1)}, bf16[3,1536,768]{2,1,0:T(8,128)(2,1)S(1)}, bf16[768,1536]{1,0:T(8,128)(2,1)S(1)}, bf16[1536,128]{1,0:T(8,128)(...) custom-call(bf16[512,1536]{1,0:T(8,128)(2,1)} %x_hbm.1, ...), custom_call_target="tpu_custom_call" | custom-call | tf_op jit(solution)/shard_map/lift/pallas_call | solution.py:87
  10.5 0.0 collective-permute-done.1.outside_ref
  10.5 0.0 collective-permute-done.twin_ref
  10.5 0.0 copy-done.1
  10.5 0.0 copy-start
  10.5 6.0 %front.1 = (bf16[528,128]{1,0:T(8,128)(2,1)S(1)}, bf16[512,256]{1,0:T(8,128)(2,1)S(1)}) custom-call(bf16[512,1536]{1,0:T(8,128)(2,1)S(1)} %get-tuple-element.38.x_ref, bf16[3,1536,768]{2,1,0:T(8,128)(2,1)S(1)} %get-tuple-element.39.taps, bf16[768,1536]{1,0:T(8,128)(2,1)S(1)} %get-tuple-element.40.mix, bf16[1536,128]{1,0:T(8,128)(2,1)S(1)} %get-tuple-element.41.wq, ...), custom_call_target="tpu_custom_call" | custom-call | tf_op jit(solution)/shard_map/front/pallas_call | solution.py:193
  16.5 0.1 collective-permute-start.5
  16.6 0.7 %collective-permute-start.4 = (bf16[512,256]{1,0:T(8,128)(2,1)S(1)}, bf16[512,256]{1,0:T(8,128)(2,1)S(1)}, u32[]{:S(2)}, u32[]{:S(2)}) collective-permute-start(bf16[512,256]{1,0:T(8,128)(2,1)S(1)} %get-tuple-element.46.refs_1_), channel_id=1, source_target_pairs={{4,8},{5,9},{6,10},{7,11},{8,4},{9,5},{10,6},{11,7},{20,24},{21,25... | collective-permute-start | bytes 786440 | tf_op jit(solution)/shard_map/ppermute | solution.py:515
  17.3 4.4 %collective-permute-start.3 = (bf16[512,256]{1,0:T(8,128)(2,1)S(1)}, bf16[512,256]{1,0:T(8,128)(2,1)S(1)}, u32[]{:S(2)}, u32[]{:S(2)}) collective-permute-start(bf16[512,256]{1,0:T(8,128)(2,1)S(1)} %get-tuple-element.46.refs_1_), channel_id=1, source_target_pairs={{0,4},{1,5},{2,6},{3,7},{4,0},{5,1},{6,2},{7,3},{8,12},{9,13},{10,... | collective-permute-start | bytes 786440 | tf_op jit(solution)/shard_map/ppermute | solution.py:515
  21.8 1.5 %collective-permute-start.2 = (bf16[528,128]{1,0:T(8,128)(2,1)S(1)}, bf16[528,128]{1,0:T(8,128)(2,1)S(1)}, u32[]{:S(2)}, u32[]{:S(2)}) collective-permute-start(bf16[528,128]{1,0:T(8,128)(2,1)S(1)} %get-tuple-element.45.refs_0_), channel_id=1, source_target_pairs={{0,2},{1,3},{2,0},{3,1},{4,6},{5,7},{6,4},{7,5},{8,10},{9,11},{10,... | collective-permute-start | bytes 405512 | tf_op jit(solution)/shard_map/ppermute | solution.py:515
  23.3 0.0 collective-permute-done.5.refs_2_
  23.3 0.0 copy-done
  23.3 2.0 %shard_map.82 = (f32[512,128]{1,0:T(8,128)S(1)}, f32[512,128]{1,0:T(8,128)S(1)}, f32[512,128]{1,0:T(8,128)S(1)}) custom-call(s32[4,65]{1,0:T(4,128)S(1)} %copy-done.1, bf16[528,128]{1,0:T(8,128)(2,1)S(1)} %get-tuple-element.45.refs_0_, bf16[512,256]{1,0:T(8,128)(2,1)S(1)} %get-tuple-element.46.refs_1_, bf16[512,256]{1,0:T(8,128)(2,1)S(1)} %collective-permute-done.5.refs_2_, ...), custom_call_target="tpu_custom_call" | custom-call | flops 268435456 | bytes 2097152 | tf_op jit(solution)/shard_map/pallas_call | solution.py:460
  25.3 0.0 collective-permute-done.4.refs_4_.refs_2_
  25.3 0.1 collective-permute-start.7
  25.4 4.5 %collective-permute-start.8 = (bf16[512,256]{1,0:T(8,128)(2,1)S(1)}, bf16[512,256]{1,0:T(8,128)(2,1)S(1)}, u32[]{:S(2)}, u32[]{:S(2)}) collective-permute-start(bf16[512,256]{1,0:T(8,128)(2,1)S(1)} %broadcast_select_fusion), channel_id=1, source_target_pairs={{0,8},{1,9},{2,10},{3,11},{4,0},{5,1},{6,2},{7,3},{8,12},{9,13},{1... | collective-permute-start | bytes 786440 | tf_op jit(solution)/shard_map/ppermute | solution.py:527
  29.9 0.0 collective-permute-done.3.refs_3_.refs_1_
  29.9 0.2 collective-permute-start.6
  30.1 0.0 collective-permute-done.2.refs_0_
  30.1 2.0 %shard_map.83 = (f32[512,128]{1,0:T(8,128)S(1)}, f32[512,128]{1,0:T(8,128)S(1)}, f32[512,128]{1,0:T(8,128)S(1)}) custom-call(s32[8,65]{1,0:T(8,128)S(1)} %pad_add_fusion.codes_ref, bf16[528,128]{1,0:T(8,128)(2,1)S(1)} %collective-permute-done.2.refs_0_, bf16[512,256]{1,0:T(8,128)(2,1)S(1)} %get-tuple-element.46.refs_1_, ...), custom_call_target="tpu_custom_call" | custom-call | flops 536870912 | bytes 4194304 | tf_op jit(solution)/shard_map/pallas_call | solution.py:460
  32.1 0.0 collective-permute-done.6.refs_1_.refs_3_
  32.1 0.0 collective-permute-done.7.refs_2_.refs_4_
  32.1 1.3 %shard_map.84 = (f32[512,128]{1,0:T(8,128)S(1)}, f32[512,128]{1,0:T(8,128)S(1)}, f32[512,128]{1,0:T(8,128)S(1)}) custom-call(s32[8,65]{1,0:T(8,128)S(1)} %pad_add_fusion.codes_ref, bf16[528,128]{1,0:T(8,128)(2,1)S(1)} %collective-permute-done.2.refs_0_, bf16[512,256]{1,0:T(8,128)(2,1)S(1)} %collective-permute-done.6.refs_1_.refs_3_, ...), custom_call_target="tpu_custom_call" | custom-call | flops 268435456 | bytes 2097152 | tf_op jit(solution)/shard_map/pallas_call | solution.py:460
  33.5 2.7 %collective-permute-done.8.refs_5_.refs_1_ = bf16[512,256]{1,0:T(8,128)(2,1)S(1)} collective-permute-done((bf16[512,256]{1,0:T(8,128)(2,1)S(1)}, bf16[512,256]{1,0:T(8,128)(2,1)S(1)}, u32[]{:S(2)}, u32[]{:S(2)}) %collective-permute-start.8) | collective-permute-done | bytes 262176 | tf_op jit(solution)/shard_map/ppermute | solution.py:527
  36.1 0.0 collective-permute-start.9
  36.1 1.4 %shard_map.86 = (f32[512,128]{1,0:T(8,128)S(1)}, f32[512,128]{1,0:T(8,128)S(1)}, f32[512,128]{1,0:T(8,128)S(1)}) custom-call(s32[8,65]{1,0:T(8,128)S(1)} %pad_add_fusion.codes_ref, bf16[528,128]{1,0:T(8,128)(2,1)S(1)} %collective-permute-done.2.refs_0_, bf16[512,256]{1,0:T(8,128)(2,1)S(1)} %collective-permute-done.8.refs_5_.refs_1_, ...), custom_call_target="tpu_custom_call" | custom-call | flops 134217728 | bytes 1048576 | tf_op jit(solution)/shard_map/pallas_call | solution.py:460
  37.5 0.1 collective-permute-done.9.refs_6_.refs_1_
  37.7 1.5 %shard_map.87 = bf16[544,128]{1,0:T(8,128)(2,1)S(1)} custom-call(s32[8,65]{1,0:T(8,128)S(1)} %pad_add_fusion.codes_ref, bf16[528,128]{1,0:T(8,128)(2,1)S(1)} %collective-permute-done.2.refs_0_, bf16[512,256]{1,0:T(8,128)(2,1)S(1)} %collective-permute-done.9.refs_6_.refs_1_, f32[16,128,128]{2,1,0:T(8,128)S(1)} %get-tuple-element.47.refs_3_.refs_5_.refs_7_.refs_2_, ...), custom_call_target="tpu_custom_call" | custom-call | flops 134217728 | bytes 1048576 | tf_op jit(solution)/shard_map/pallas_call | solution.py:460
  39.2 1.0 %collective-permute-start.10 = (bf16[544,128]{1,0:T(8,128)(2,1)S(1)}, bf16[544,128]{1,0:T(8,128)(2,1)S(1)}, u32[]{:S(2)}, u32[]{:S(2)}) collective-permute-start(bf16[544,128]{1,0:T(8,128)(2,1)S(1)} %shard_map.87), channel_id=1, source_target_pairs={{0,2},{1,3},{2,0},{3,1},{4,6},{5,7},{6,4},{7,5},{8,10},{9,11},{10,... | collective-permute-start | bytes 417800 | tf_op jit(solution)/shard_map/ppermute | solution.py:515
  40.2 2.7 %shard_map.85 = (f32[512,128]{1,0:T(8,128)S(1)}, f32[512,128]{1,0:T(8,128)S(1)}, f32[512,128]{1,0:T(8,128)S(1)}) custom-call(s32[8,65]{1,0:T(8,128)S(1)} %pad_add_fusion.codes_ref, bf16[528,128]{1,0:T(8,128)(2,1)S(1)} %get-tuple-element.45.refs_0_, bf16[512,256]{1,0:T(8,128)(2,1)S(1)} %collective-permute-done.3.refs_3_.refs_1_, ...), custom_call_target="tpu_custom_call" | custom-call | flops 805306368 | bytes 6291456 | tf_op jit(solution)/shard_map/pallas_call | solution.py:460
  42.9 2.3 %collective-permute-done.10.pack_ref = bf16[544,128]{1,0:T(8,128)(2,1)S(1)} collective-permute-done((bf16[544,128]{1,0:T(8,128)(2,1)S(1)}, bf16[544,128]{1,0:T(8,128)(2,1)S(1)}, u32[]{:S(2)}, u32[]{:S(2)}) %collective-permute-start.10) | collective-permute-done | bytes 139296 | tf_op jit(solution)/shard_map/ppermute | solution.py:515
  45.2 1.0 %merge.1 = bf16[512,128]{1,0:T(8,128)(2,1)} custom-call(f32[512,128]{1,0:T(8,128)S(1)} %get-tuple-element.62.peak_ref, f32[512,128]{1,0:T(8,128)S(1)} %get-tuple-element.63.total_ref, f32[512,128]{1,0:T(8,128)S(1)} %get-tuple-element.64.acc_ref, bf16[544,128]{1,0:T(8,128)(2,1)S(1)} %collective-permute-done.10.pack_ref), custom_call_target="tpu_custom_call" | custom-call | tf_op jit(solution)/shard_map/merge/pallas_call | solution.py:577
  (3 shorter events, 0.1 us)
Async XLA Ops:
  0.8 9.7 %collective-permute-start.1 = (bf16[8,1536]{1,0:T(8,128)(2,1)S(1)}, bf16[8,1536]{1,0:T(8,128)(2,1)S(1)}, u32[]{:S(2)}, u32[]{:S(2)}) collective-permute-start(bf16[8,1536]{1,0:T(8,128)(2,1)S(1)} %get-tuple-element.71), channel_id=1, source_target_pairs={{1,2},{3,4},{5,6},{7,8},{9,10},{11,12},{13,14},{2,1},{4,3},{6,5},{... | collective-permute-start | bytes 73736 | tf_op jit(solution)/shard_map/ppermute | solution.py:31
  1.4 9.1 %copy-start.1 = (s32[4,65]{1,0:T(4,128)S(1)}, s32[4,65]{1,0:T(4,128)}, u32[]{:S(2)}) copy-start(s32[4,65]{1,0:T(4,128)} %codes_ref.3) | copy-start | bytes 3124
  1.4 9.1 %collective-permute-start = (bf16[8,1536]{1,0:T(8,128)(2,1)S(1)}, bf16[8,1536]{1,0:T(8,128)(2,1)S(1)}, u32[]{:S(2)}, u32[]{:S(2)}) collective-permute-start(bf16[8,1536]{1,0:T(8,128)(2,1)S(1)} %get-tuple-element.72), channel_id=1, source_target_pairs={{0,1},{1,0},{2,3},{3,2},{4,5},{5,4},{6,7},{7,6},{8,9},{9,8},{10,11... | collective-permute-start | bytes 73736 | tf_op jit(solution)/shard_map/ppermute | solution.py:30
  10.5 12.8 %copy-start = (s32[8192]{0:T(1024)S(1)}, s32[8192]{0:T(1024)}, u32[]{:S(2)}) copy-start(s32[8192]{0:T(1024)} %param.15) | copy-start | bytes 98308
  16.5 6.8 %collective-permute-start.5 = (bf16[512,256]{1,0:T(8,128)(2,1)S(1)}, bf16[512,256]{1,0:T(8,128)(2,1)S(1)}, u32[]{:S(2)}, u32[]{:S(2)}) collective-permute-start(bf16[512,256]{1,0:T(8,128)(2,1)S(1)} %get-tuple-element.46.refs_1_), channel_id=1, source_target_pairs={{0,1},{1,0},{2,3},{3,2},{4,5},{5,4},{6,7},{7,6},{8,9},{9,8},{10,11... | collective-permute-start | bytes 786440 | tf_op jit(solution)/shard_map/ppermute | solution.py:515
  16.6 8.7 %collective-permute-start.4 = (bf16[512,256]{1,0:T(8,128)(2,1)S(1)}, bf16[512,256]{1,0:T(8,128)(2,1)S(1)}, u32[]{:S(2)}, u32[]{:S(2)}) collective-permute-start(bf16[512,256]{1,0:T(8,128)(2,1)S(1)} %get-tuple-element.46.refs_1_), channel_id=1, source_target_pairs={{4,8},{5,9},{6,10},{7,11},{8,4},{9,5},{10,6},{11,7},{20,24},{21,25... | collective-permute-start | bytes 786440 | tf_op jit(solution)/shard_map/ppermute | solution.py:515
  17.3 12.6 %collective-permute-start.3 = (bf16[512,256]{1,0:T(8,128)(2,1)S(1)}, bf16[512,256]{1,0:T(8,128)(2,1)S(1)}, u32[]{:S(2)}, u32[]{:S(2)}) collective-permute-start(bf16[512,256]{1,0:T(8,128)(2,1)S(1)} %get-tuple-element.46.refs_1_), channel_id=1, source_target_pairs={{0,4},{1,5},{2,6},{3,7},{4,0},{5,1},{6,2},{7,3},{8,12},{9,13},{10,... | collective-permute-start | bytes 786440 | tf_op jit(solution)/shard_map/ppermute | solution.py:515
  21.8 8.3 %collective-permute-start.2 = (bf16[528,128]{1,0:T(8,128)(2,1)S(1)}, bf16[528,128]{1,0:T(8,128)(2,1)S(1)}, u32[]{:S(2)}, u32[]{:S(2)}) collective-permute-start(bf16[528,128]{1,0:T(8,128)(2,1)S(1)} %get-tuple-element.45.refs_0_), channel_id=1, source_target_pairs={{0,2},{1,3},{2,0},{3,1},{4,6},{5,7},{6,4},{7,5},{8,10},{9,11},{10,... | collective-permute-start | bytes 405512 | tf_op jit(solution)/shard_map/ppermute | solution.py:515
  25.3 6.8 %collective-permute-start.7 = (bf16[512,256]{1,0:T(8,128)(2,1)S(1)}, bf16[512,256]{1,0:T(8,128)(2,1)S(1)}, u32[]{:S(2)}, u32[]{:S(2)}) collective-permute-start(bf16[512,256]{1,0:T(8,128)(2,1)S(1)} %collective-permute-done.4.refs_4_.refs_2_), channel_id=1, source_target_pairs={{0,1},{1,0},{2,3},{3,2},{4,5},{5,4},{6,7},{7,6},{8,9},{9,8},{10,11... | collective-permute-start | bytes 786440 | tf_op jit(solution)/shard_map/ppermute | solution.py:515
  25.4 10.7 %collective-permute-start.8 = (bf16[512,256]{1,0:T(8,128)(2,1)S(1)}, bf16[512,256]{1,0:T(8,128)(2,1)S(1)}, u32[]{:S(2)}, u32[]{:S(2)}) collective-permute-start(bf16[512,256]{1,0:T(8,128)(2,1)S(1)} %broadcast_select_fusion), channel_id=1, source_target_pairs={{0,8},{1,9},{2,10},{3,11},{4,0},{5,1},{6,2},{7,3},{8,12},{9,13},{1... | collective-permute-start | bytes 786440 | tf_op jit(solution)/shard_map/ppermute | solution.py:527
  29.9 2.2 %collective-permute-start.6 = (bf16[512,256]{1,0:T(8,128)(2,1)S(1)}, bf16[512,256]{1,0:T(8,128)(2,1)S(1)}, u32[]{:S(2)}, u32[]{:S(2)}) collective-permute-start(bf16[512,256]{1,0:T(8,128)(2,1)S(1)} %collective-permute-done.3.refs_3_.refs_1_), channel_id=1, source_target_pairs={{0,1},{1,0},{2,3},{3,2},{4,5},{5,4},{6,7},{7,6},{8,9},{9,8},{10,11... | collective-permute-start | bytes 786440 | tf_op jit(solution)/shard_map/ppermute | solution.py:515
  36.1 1.5 %collective-permute-start.9 = (bf16[512,256]{1,0:T(8,128)(2,1)S(1)}, bf16[512,256]{1,0:T(8,128)(2,1)S(1)}, u32[]{:S(2)}, u32[]{:S(2)}) collective-permute-start(bf16[512,256]{1,0:T(8,128)(2,1)S(1)} %collective-permute-done.8.refs_5_.refs_1_), channel_id=1, source_target_pairs={{0,1},{1,0},{2,3},{3,2},{4,5},{5,4},{6,7},{7,6},{8,9},{9,8},{10,11... | collective-permute-start | bytes 786440 | tf_op jit(solution)/shard_map/ppermute | solution.py:515
  39.2 6.0 %collective-permute-start.10 = (bf16[544,128]{1,0:T(8,128)(2,1)S(1)}, bf16[544,128]{1,0:T(8,128)(2,1)S(1)}, u32[]{:S(2)}, u32[]{:S(2)}) collective-permute-start(bf16[544,128]{1,0:T(8,128)(2,1)S(1)} %shard_map.87), channel_id=1, source_target_pairs={{0,2},{1,3},{2,0},{3,1},{4,6},{5,7},{6,4},{7,5},{8,10},{9,11},{10,... | collective-permute-start | bytes 417800 | tf_op jit(solution)/shard_map/ppermute | solution.py:515
